TPU v7x, 512 devices: a whole 4x4x16 slice. The times are simulated.
512 devices in a mesh: slab: 32 (over x, y, z_hi), tile: 16 (over z_lo, core).
Axes of the slice: x: 4, y: 4, z: 16 (z_hi: 2, z_lo: 8; z = z_hi * 8 + z_lo), core: 2. Of those that a mesh axis runs over, the one named last changes fastest.
Arguments:
- field: float32 [256, 256, 1024], P('slab', 'tile'), may hold values from -1 to 1
- dual: float32 [3, 256, 256, 1024], P(None, 'slab', 'tile'), may hold values from -0.5 to 0.5
- depth: float32 [32, 2, 4, 256, 1024], P('slab', None, None, 'tile'), may hold values from 0 to 256
- owner: int32 [2], replicated, may hold values from 0 to 31
- visible: int32 [2, 4, 16], P(None, None, 'tile'), may hold values 0 or 1
Outputs:
- field_out: float32 [256, 256, 1024], P('slab', 'tile')
- dual_out: float32 [3, 256, 256, 1024], P(None, 'slab', 'tile')
All inputs are finite; a program needn't handle non-finite values. No bound on the sum of `visible` on one device may be relied on, other than what follows from the above.
Results may differ from a plain program's by a relative error of at most 0.00002.
Values sent between devices are 32-bit elements; how exact they have to be, the bound alone decides.
No kernel may reach another device: no remote copies, remote signals or barrier semaphores. Data moves between devices by JAX's collectives and lax.ppermute only.
A program may use at most 64 MiB of HBM per device.

v0:
```python
import jax
import jax.numpy as jnp
from jax import lax
from jax.sharding import PartitionSpec as P

VIEWS = 4
BINS = 8
BAND = 6
ITERS = 2


def from_root(value, axis, root):
    mine = lax.axis_index(axis) == root
    return lax.psum(jnp.where(mine, value, jnp.zeros_like(value)), axis)


def passed_along(value, axis, steps):
    count = lax.axis_size(axis)
    first, last = (max(0, -steps), min(count, count - steps))
    return lax.ppermute(value, axis, [(source, source + steps) for source in range(first, last)])


def add_votes(histogram, depth_map, seen, zfloat):
    ratio = (depth_map[None, :, :] - zfloat) / float(BAND)
    weight = jnp.clip(ratio + 2.0, 0.0, 1.0) * seen
    place = (jnp.clip(ratio, -1.0, 1.0) + 1.0) * ((BINS - 1) / 2.0)
    return [
        histogram[bin_index] + weight * jnp.maximum(0.0, 1.0 - jnp.abs(place - float(bin_index)))
        for bin_index in range(BINS)
    ]


def proximal(values, histogram):
    total = histogram[0]
    for bin_index in range(1, BINS):
        total = total + histogram[bin_index]
    weights = -total
    best = jnp.minimum(values - 0.05 * weights, -1.0)
    weights = weights + 2.0 * histogram[0]
    for bin_index in range(1, BINS):
        centre = -1.0 + 2.0 * bin_index / (BINS - 1)
        best = jnp.maximum(best, jnp.minimum(values - 0.05 * weights, centre))
        weights = weights + 2.0 * histogram[bin_index]
    return jnp.maximum(best, values - 0.05 * weights)


def dual_step(
    dual_z, dual_x, dual_y, here, ahead_z, ahead_x, zpos, xpos, ypos, total_z, total_x, total_y
):
    zero_y = jnp.zeros(here.shape[:2] + (1,), jnp.float32)
    ahead_y = jnp.concatenate([here[:, :, 1:], zero_y], 2)
    grad_z = jnp.where(zpos < total_z - 1, ahead_z - here, 0.0)
    grad_x = jnp.where(xpos < total_x - 1, ahead_x - here, 0.0)
    grad_y = jnp.where(ypos < total_y - 1, ahead_y - here, 0.0)
    moved_z = dual_z + 0.25 * grad_z
    moved_x = dual_x + 0.25 * grad_x
    moved_y = dual_y + 0.25 * grad_y
    scale = jnp.maximum(1.0, jnp.sqrt(moved_z * moved_z + moved_x * moved_x + moved_y * moved_y))
    inside_z = (zpos >= 0) & (zpos < total_z - 1)
    inside_x = (xpos >= 0) & (xpos < total_x - 1)
    new_z = jnp.where(inside_z, moved_z / scale, 0.0)
    new_x = jnp.where(inside_x, moved_x / scale, 0.0)
    new_y = jnp.where(ypos < total_y - 1, moved_y / scale, 0.0)
    return (new_z, new_x, new_y)


def per_device(field, dual, depth, owner, visible):
    slab_cells, strip_cells, depth_cells = field.shape
    total_z = slab_cells * lax.axis_size("slab")
    total_x = strip_cells * lax.axis_size("tile")
    slab_start = lax.axis_index("slab") * slab_cells
    strip_start = lax.axis_index("tile") * strip_cells
    zpos = slab_start + jnp.arange(slab_cells, dtype=jnp.int32)[:, None, None]
    xpos = strip_start + jnp.arange(strip_cells, dtype=jnp.int32)[None, :, None]
    ypos = jnp.arange(depth_cells, dtype=jnp.int32)[None, None, :]
    zfloat = zpos.astype(jnp.float32)
    histogram = [jnp.zeros(field.shape, jnp.float32) for bin_index in range(BINS)]
    current = field
    dual_z, dual_x, dual_y = (dual[0], dual[1], dual[2])
    extra = field
    zero_y = jnp.zeros((slab_cells, strip_cells, 1), jnp.float32)
    for step_index in range(ITERS):
        batch = from_root(depth[0, step_index], "slab", owner[step_index])
        for view_index in range(VIEWS):
            seen = visible[step_index, view_index, 0].astype(jnp.float32)
            histogram = add_votes(histogram, batch[view_index], seen, zfloat)
        below = passed_along(extra[0:1], "slab", -1)
        beside = passed_along(extra[:, 0:1], "tile", -1)
        ahead_z = jnp.concatenate([extra[1:], below], 0)
        ahead_x = jnp.concatenate([extra[:, 1:], beside], 1)
        dual_z, dual_x, dual_y = dual_step(
            dual_z,
            dual_x,
            dual_y,
            extra,
            ahead_z,
            ahead_x,
            zpos,
            xpos,
            ypos,
            total_z,
            total_x,
            depth_cells,
        )
        above = passed_along(dual_z[-1:], "slab", 1)
        before = passed_along(dual_x[:, -1:], "tile", 1)
        prev_z = jnp.concatenate([above, dual_z[:-1]], 0)
        prev_x = jnp.concatenate([before, dual_x[:, :-1]], 1)
        prev_y = jnp.concatenate([zero_y, dual_y[:, :, :-1]], 2)
        divergence = dual_z - prev_z + (dual_x - prev_x) + (dual_y - prev_y)
        updated = proximal(current + 0.25 * divergence, histogram)
        extra = 2.0 * updated - current
        current = updated
    return (current, jnp.stack([dual_z, dual_x, dual_y]))


def solution(mesh):
    placed = (
        P("slab", "tile", None),
        P(None, "slab", "tile", None),
        P("slab", None, None, "tile", None),
        P(),
        P(None, None, "tile"),
    )
    return jax.shard_map(
        per_device,
        mesh=mesh,
        in_specs=placed,
        out_specs=(P("slab", "tile", None), P(None, "slab", "tile", None)),
        check_vma=False,
    )
```

profile of v0, /device:TPU:31, one launch (start us, length us, event | category | flops | bytes accessed | tf_op | source)
XLA Modules:
  0.0 672.1 jit_solution(14026309236746614929)
XLA Ops:
  7.2 0.0 copy-start
  7.2 0.0 copy-start.2
  7.2 0.0 all-reduce.7.cloned.1.call-start
  7.2 1.0 slice.134
  8.3 2.6 collective-permute-start.1
  10.8 0.8 slice.131
  11.7 15.6 %collective-permute-start = (f32[1,16,1024]{2,1,0:T(8,128)S(1)}, f32[1,16,1024]{2,1,0:T(8,128)S(1)}, u32[]{:S(2)}, u32[]{:S(2)}) collective-permute-start(f32[1,16,1024]{2,1,0:T(8,128)S(1)} %slice.131), channel_id=1, source_target_pairs={{16,0},{32,16},{48,32},{64,48},{80,64},{96,80},{112,96},{128,112},... | collective-permute-start | bytes 196616 | tf_op jit(solution)/shard_map/ppermute | solution.py:20
  27.3 1.3 fusion.28
  29.9 1.9 select_bitcast_fusion
  31.8 0.0 all-reduce.7.cloned.1.call-update
  31.8 0.0 slice-start
  31.9 0.0 copy-done.2
  31.9 0.7 fusion.27
  32.6 0.0 copy-done
  32.6 0.1 slice.133
  32.6 0.2 slice.136
  37.7 0.0 collective-permute-done.1
  37.7 0.0 collective-permute-done
  37.8 0.0 slice-done
  37.8 2.0 divide_select_fusion.3
  39.7 0.3 divide_select_fusion.5
  40.1 3.3 collective-permute-start.3
  43.4 1.9 collective-permute-start.2
  45.3 541.3 %all-reduce.7.cloned.1.call-done = (f32[4,16,1024]{2,1,0:T(8,128)}, f32[4,16,1024]{2,1,0:T(8,128)}) async-done(((f32[4,16,1024]{2,1,0:T(8,128)}, f32[4,16,1024]{2,1,0:T(8,128)}), (f32[4,16,1024]{2,1,0:T(8,128)}, f32[4,16,1024]{2,1,0:T(8,128)})) %all-reduce.7.cloned.1.call-update) | async-done | bytes 524304 | tf_op jit(solution)/shard_map/psum | solution.py:14
  586.6 1.0 slice_bitcast_fusion.7
  587.6 0.0 collective-permute-done.3
  587.6 0.0 collective-permute-done.2
  587.6 0.0 copy-start.1
  587.6 5.0 multiply_subtract_fusion
  592.7 25.0 %collective-permute-start.5 = (f32[8,1,1024]{2,1,0:T(1,128)S(1)}, f32[8,1,1024]{2,1,0:T(1,128)S(1)}, u32[]{:S(2)}, u32[]{:S(2)}) collective-permute-start(f32[8,1,1024]{2,1,0:T(1,128)S(1)} %slice.184), channel_id=1, source_target_pairs={{1,0},{2,1},{3,2},{4,3},{5,4},{6,5},{7,6},{8,7},{9,8},{10,9},{11,1... | collective-permute-start | bytes 98312 | tf_op jit(solution)/shard_map/ppermute | solution.py:20
  617.7 6.0 collective-permute-start.4
  623.7 0.0 copy-done.1
  623.8 0.2 slice.185
  624.0 0.1 slice.183
  624.0 0.0 collective-permute-done.5
  624.0 12.1 %collective-permute-done.4 = f32[1,16,1024]{2,1,0:T(8,128)S(1)} collective-permute-done((f32[1,16,1024]{2,1,0:T(8,128)S(1)}, f32[1,16,1024]{2,1,0:T(8,128)S(1)}, u32[]{:S(2)}, u32[]{:S(2)}) %collective-permute-start.4) | collective-permute-done | bytes 65568 | tf_op jit(solution)/shard_map/ppermute | solution.py:20
  636.1 0.6 divide_select_fusion
  636.7 0.2 divide_select_fusion.2
  637.0 3.0 collective-permute-start.7
  640.0 1.9 collective-permute-start.6
  641.9 1.2 pad_maximum_fusion
  643.2 0.0 collective-permute-done.7
  643.2 12.4 %collective-permute-done.6 = f32[1,16,1024]{2,1,0:T(8,128)S(1)} collective-permute-done((f32[1,16,1024]{2,1,0:T(8,128)S(1)}, f32[1,16,1024]{2,1,0:T(8,128)S(1)}, u32[]{:S(2)}, u32[]{:S(2)}) %collective-permute-start.6) | collective-permute-done | bytes 65568 | tf_op jit(solution)/shard_map/ppermute | solution.py:20
  655.7 9.6 %subtract_maximum_fusion = f32[8,16,1024]{2,1,0:T(8,128)} fusion(f32[8,16,1024]{2,1,0:T(8,128)S(1)} %get-tuple-element.9, f32[8,16,1024]{2,1,0:T(8,128)S(1)} %get-tuple-element.17, f32[8,15,1024]{2,1,0:T(8,128)S(1)} %bitcast.48, f32[8,1,1024]{2,1,0:T(1,128)S(1)} %collective-permute-done.7, f32[8,16,1024]{2,1,0:T(8,128)S(1)} %get-tuple-element.16, ...), kind=kLoop, calls=%fused_computation.30 | loop fusion | flops 65404928 | bytes 4718144 | tf_op jit(solution)/shard_map/max | solution.py:44
  (14 shorter events, 0.2 us)
Async XLA Ops:
  7.2 25.4 %copy-start = (f32[8,16,1024]{2,1,0:T(8,128)S(1)}, f32[8,16,1024]{2,1,0:T(8,128)}, u32[]{:S(2)}) copy-start(f32[8,16,1024]{2,1,0:T(8,128)} %param.5) | copy-start | bytes 1572868
  7.2 24.7 %copy-start.2 = (s32[2,4,1]{1,2,0:T(1,128)S(1)}, s32[2,4,1]{1,2,0:T(1,128)}, u32[]{:S(2)}) copy-start(s32[2,4,1]{1,2,0:T(1,128)} %param.9) | copy-start | bytes 100
  7.2 579.5 %all-reduce.7.cloned.1.call-start = ((), (), s32[]{:S(2)}) async-start(), calls=%async_computation | async-start | bytes 1048576 | tf_op jit(solution)/shard_map/psum | solution.py:14
  8.3 29.5 %collective-permute-start.1 = (f32[8,1,1024]{2,1,0:T(1,128)S(1)}, f32[8,1,1024]{2,1,0:T(1,128)S(1)}, u32[]{:S(2)}, u32[]{:S(2)}) collective-permute-start(f32[8,1,1024]{2,1,0:T(1,128)S(1)} %slice.134), channel_id=1, source_target_pairs={{1,0},{2,1},{3,2},{4,3},{5,4},{6,5},{7,6},{8,7},{9,8},{10,9},{11,1... | collective-permute-start | bytes 98312 | tf_op jit(solution)/shard_map/ppermute | solution.py:20
  11.7 26.1 %collective-permute-start = (f32[1,16,1024]{2,1,0:T(8,128)S(1)}, f32[1,16,1024]{2,1,0:T(8,128)S(1)}, u32[]{:S(2)}, u32[]{:S(2)}) collective-permute-start(f32[1,16,1024]{2,1,0:T(8,128)S(1)} %slice.131), channel_id=1, source_target_pairs={{16,0},{32,16},{48,32},{64,48},{80,64},{96,80},{112,96},{128,112},... | collective-permute-start | bytes 196616 | tf_op jit(solution)/shard_map/ppermute | solution.py:20
  31.8 5.9 slice-start
  40.1 547.5 %collective-permute-start.3 = (f32[8,1,1024]{2,1,0:T(1,128)S(1)}, f32[8,1,1024]{2,1,0:T(1,128)S(1)}, u32[]{:S(2)}, u32[]{:S(2)}) collective-permute-start(f32[8,1,1024]{2,1,0:T(1,128)S(1)} %slice.174), channel_id=1, source_target_pairs={{0,1},{1,2},{2,3},{3,4},{4,5},{5,6},{6,7},{7,8},{8,9},{9,10},{10,1... | collective-permute-start | bytes 98312 | tf_op jit(solution)/shard_map/ppermute | solution.py:20
  43.4 544.2 %collective-permute-start.2 = (f32[1,16,1024]{2,1,0:T(8,128)S(1)}, f32[1,16,1024]{2,1,0:T(8,128)S(1)}, u32[]{:S(2)}, u32[]{:S(2)}) collective-permute-start(f32[1,16,1024]{2,1,0:T(8,128)S(1)} %slice.172), channel_id=1, source_target_pairs={{0,16},{16,32},{32,48},{48,64},{64,80},{80,96},{96,112},{112,128},... | collective-permute-start | bytes 196616 | tf_op jit(solution)/shard_map/ppermute | solution.py:20
  587.6 36.1 %copy-start.1 = (f32[4,16,1024]{2,1,0:T(8,128)S(1)}, f32[4,16,1024]{2,1,0:T(8,128)}, u32[]{:S(2)}) copy-start(f32[4,16,1024]{2,1,0:T(8,128)} %get-tuple-element.3) | copy-start | bytes 786436
  592.7 31.3 %collective-permute-start.5 = (f32[8,1,1024]{2,1,0:T(1,128)S(1)}, f32[8,1,1024]{2,1,0:T(1,128)S(1)}, u32[]{:S(2)}, u32[]{:S(2)}) collective-permute-start(f32[8,1,1024]{2,1,0:T(1,128)S(1)} %slice.184), channel_id=1, source_target_pairs={{1,0},{2,1},{3,2},{4,3},{5,4},{6,5},{7,6},{8,7},{9,8},{10,9},{11,1... | collective-permute-start | bytes 98312 | tf_op jit(solution)/shard_map/ppermute | solution.py:20
  617.7 18.4 %collective-permute-start.4 = (f32[1,16,1024]{2,1,0:T(8,128)S(1)}, f32[1,16,1024]{2,1,0:T(8,128)S(1)}, u32[]{:S(2)}, u32[]{:S(2)}) collective-permute-start(f32[1,16,1024]{2,1,0:T(8,128)S(1)} %slice.182), channel_id=1, source_target_pairs={{16,0},{32,16},{48,32},{64,48},{80,64},{96,80},{112,96},{128,112},... | collective-permute-start | bytes 196616 | tf_op jit(solution)/shard_map/ppermute | solution.py:20
  637.0 6.2 collective-permute-start.7
  640.0 15.7 %collective-permute-start.6 = (f32[1,16,1024]{2,1,0:T(8,128)S(1)}, f32[1,16,1024]{2,1,0:T(8,128)S(1)}, u32[]{:S(2)}, u32[]{:S(2)}) collective-permute-start(f32[1,16,1024]{2,1,0:T(8,128)S(1)} %slice.186), channel_id=1, source_target_pairs={{0,16},{16,32},{32,48},{48,64},{64,80},{80,96},{96,112},{112,128},... | collective-permute-start | bytes 196616 | tf_op jit(solution)/shard_map/ppermute | solution.py:20
Sparse Core Ops, SparseCore 0:
  31.9 554.6 all-reduce.6
where the time goes:
time: 673 us; the launch traced here: 672 us
  waiting for transfers between devices  566 us (84%)
  starting transfers between devices  59.3 us (9%)
  other arithmetic  20.8 us (3%)
  between operations  20.5 us (3%)
    psum x1, waiting for transfers between devices, from_root(): return lax.psum(jnp.where(mine, value, jnp.zeros_like(value)), axis)  541 us
    ppermute x8, starting transfers between devices, passed_along(): lax.ppermute(value, axis, [(source, source + steps) for source in range(f...  59.2 us
    ppermute x8, waiting for transfers between devices, passed_along(): lax.ppermute(value, axis, [(source, source + steps) for source in range(f...  24.5 us
  transfers between devices with their start and end apart: 9, of which 3 were waited for; matrix products, arithmetic and copies ran while one was open for 1% of the time, Pallas kernels for 0%

commit v1 on v0

--- a/solution.py
+++ b/solution.py
@@ -9,9 +9,24 @@
 ITERS = 2
 
 
-def from_root(value, axis, root):
-    mine = lax.axis_index(axis) == root
-    return lax.psum(jnp.where(mine, value, jnp.zeros_like(value)), axis)
+def from_roots(batches, roots):
+    groups = [[2 * place + half for place in range(16)] for half in range(2)]
+    flip = [(index, index ^ 1) for index in range(32)]
+    my_half = lax.axis_index("slab") % 2
+    pieces = batches.reshape(ITERS, VIEWS, 2, 8, 2, 4, 128).transpose(1, 2, 4, 0, 5, 3, 6)
+    pieces = pieces.reshape(16, ITERS, 4, 8, 128)
+    spread = lax.all_to_all(pieces, "slab", 0, 0, axis_index_groups=groups)
+    kept = jnp.stack([
+        lax.dynamic_index_in_dim(spread[:, step], roots[step] // 2, 0, keepdims=False) for step in range(ITERS)
+    ])
+    across = lax.ppermute(kept, "slab", flip)
+    right_half = (roots % 2 == my_half)[:, None, None, None]
+    kept = jnp.where(right_half, kept, across)
+    whole = lax.all_to_all(
+        jnp.broadcast_to(kept[None], (16,) + kept.shape), "slab", 0, 0, axis_index_groups=groups
+    )
+    whole = whole.reshape(VIEWS, 2, 2, ITERS, 4, 8, 128).transpose(3, 0, 1, 5, 2, 4, 6)
+    return whole.reshape(ITERS, VIEWS, 16, 1024)
 
 
 def passed_along(value, axis, steps):
@@ -79,8 +94,9 @@
     dual_z, dual_x, dual_y = (dual[0], dual[1], dual[2])
     extra = field
     zero_y = jnp.zeros((slab_cells, strip_cells, 1), jnp.float32)
+    batches = from_roots(depth[0], owner)
     for step_index in range(ITERS):
-        batch = from_root(depth[0, step_index], "slab", owner[step_index])
+        batch = batches[step_index]
         for view_index in range(VIEWS):
             seen = visible[step_index, view_index, 0].astype(jnp.float32)
             histogram = add_votes(histogram, batch[view_index], seen, zfloat)

time: 673 us -> 141 us (0.21)
  the two profiles are of different devices: /device:TPU:31 before, /device:TPU:38 now
where the time goes in v1:
time: 141 us; the launch traced here: 140 us
  waiting for transfers between devices  52 us (37%)
  starting transfers between devices  50.8 us (36%)
  other arithmetic  19 us (13%)
  between operations  11.1 us (8%)
  local copies, waits for them, and re-layouts  6.64 us (5%)
    ppermute x8, waiting for transfers between devices, passed_along(): lax.ppermute(value, axis, [(source, source + steps) for source in range(f...  38.4 us
    ppermute x8, starting transfers between devices, passed_along(): lax.ppermute(value, axis, [(source, source + steps) for source in range(f...  38.2 us
    ppermute x1, waiting for transfers between devices, from_roots(): across = lax.ppermute(kept, 'slab', flip)  9.8 us
    max x1, other arithmetic, proximal(): return jnp.maximum(best, values - 0.05 * weights)  9.57 us
    all_to_all x1, starting transfers between devices, from_roots(): lax.all_to_all(jnp.broadcast_to(kept[None], (16,) + kept.shape), 'slab',...  5.57 us
    sub x1, other arithmetic, per_device(): extra = 2.0 * updated - current  5 us
    all_to_all x1, starting transfers between devices, from_roots(): spread = lax.all_to_all(pieces, 'slab', 0, 0, axis_index_groups=groups)  4.84 us
    all_to_all x1, waiting for transfers between devices, from_roots(): spread = lax.all_to_all(pieces, 'slab', 0, 0, axis_index_groups=groups)  2.9 us
  transfers between devices with their start and end apart: 11, of which 7 were waited for; matrix products, arithmetic and copies ran while one was open for 7% of the time, Pallas kernels for 0%

profile of v1, /device:TPU:38, one launch (start us, length us, event | category | flops | bytes accessed | tf_op | source)
XLA Modules:
  0.0 139.6 jit_solution(14066418844510020268)
XLA Ops:
  0.6 0.0 copy-start.2
  0.6 0.0 copy-start.1
  0.6 1.0 slice.154
  1.6 1.9 %collective-permute-start.1 = (f32[8,1,1024]{2,1,0:T(1,128)S(1)}, f32[8,1,1024]{2,1,0:T(1,128)S(1)}, u32[]{:S(2)}, u32[]{:S(2)}) collective-permute-start(f32[8,1,1024]{2,1,0:T(1,128)S(1)} %slice.154), channel_id=1, source_target_pairs={{1,0},{2,1},{3,2},{4,3},{5,4},{6,5},{7,6},{8,7},{9,8},{10,9},{11,1... | collective-permute-start | bytes 98312 | tf_op jit(solution)/shard_map/ppermute | solution.py:35
  3.6 0.8 slice.151
  4.4 18.0 %collective-permute-start = (f32[1,16,1024]{2,1,0:T(8,128)S(1)}, f32[1,16,1024]{2,1,0:T(8,128)S(1)}, u32[]{:S(2)}, u32[]{:S(2)}) collective-permute-start(f32[1,16,1024]{2,1,0:T(8,128)S(1)} %slice.151), channel_id=1, source_target_pairs={{16,0},{32,16},{48,32},{64,48},{80,64},{96,80},{112,96},{128,112},... | collective-permute-start | bytes 196616 | tf_op jit(solution)/shard_map/ppermute | solution.py:35
  22.4 1.9 %copy.7 = f32[2,4,2,8,2,4,128]{6,3,5,0,4,2,1:T(8,128)} copy(f32[2,4,2,8,2,4,128]{6,3,5,4,2,1,0:T(8,128)} %bitcast.61) | data formatting | bytes 1048576 | tf_op jit(solution)/shard_map/reshape;squeeze | solution.py:16
  24.3 0.0 copy-start
  24.3 4.8 %all-to-all-start = ((f32[16,2,4,8,128]{4,3,2,1,0:T(8,128)}), f32[16,2,4,8,128]{4,3,2,1,0:T(8,128)S(1)}, u32[]{:S(2)}, u32[]{:S(2)}) async-start(f32[16,2,4,8,128]{4,3,2,1,0:T(8,128)} %bitcast.5), calls=%async_computation | async-start | bytes 1048576 | tf_op jit(solution)/shard_map/all_to_all | solution.py:18
  29.1 0.0 copy-done.2
  29.1 0.6 fusion.32
  34.9 0.0 copy-done.1
  34.9 0.7 fusion.31
  35.6 2.9 %all-to-all-done = f32[16,2,4,8,128]{4,3,2,1,0:T(8,128)S(1)} async-done(((f32[16,2,4,8,128]{4,3,2,1,0:T(8,128)}), f32[16,2,4,8,128]{4,3,2,1,0:T(8,128)S(1)}, u32[]{:S(2)}, u32[]{:S(2)}) %all-to-all-start) | async-done | bytes 524320 | tf_op jit(solution)/shard_map/all_to_all | solution.py:18
  38.6 2.2 %collective-permute-start.4 = (f32[2,4,8,128]{3,2,1,0:T(8,128)S(1)}, f32[2,4,8,128]{3,2,1,0:T(8,128)S(1)}, u32[]{:S(2)}, u32[]{:S(2)}) collective-permute-start(f32[2,4,8,128]{3,2,1,0:T(8,128)S(1)} %pad_maximum_fusion.1), channel_id=1, source_target_pairs={{0,16},{16,0},{32,48},{48,32},{64,80},{80,64},{96,112},{112,96},{1... | collective-permute-start | bytes 98312 | tf_op jit(solution)/shard_map/ppermute | solution.py:22
  40.8 0.0 copy-done
  40.8 0.1 slice.153
  40.9 0.0 slice-start
  40.9 0.2 slice.156
  43.7 9.8 %collective-permute-done.4 = f32[2,4,8,128]{3,2,1,0:T(8,128)S(1)} collective-permute-done((f32[2,4,8,128]{3,2,1,0:T(8,128)S(1)}, f32[2,4,8,128]{3,2,1,0:T(8,128)S(1)}, u32[]{:S(2)}, u32[]{:S(2)}) %collective-permute-start.4) | collective-permute-done | bytes 32800 | tf_op jit(solution)/shard_map/ppermute | solution.py:22
  53.5 0.1 broadcast_select_fusion
  53.5 0.9 broadcast_in_dim.103
  54.4 5.6 %all-to-all-start.1 = ((f32[16,2,4,8,128]{4,3,2,1,0:T(8,128)}), f32[16,2,4,8,128]{4,3,2,1,0:T(8,128)S(1)}, u32[]{:S(2)}, u32[]{:S(2)}) async-start(f32[16,2,4,8,128]{4,3,2,1,0:T(8,128)} %broadcast_in_dim.103), calls=%async_computation.1 | async-start | bytes 1048576 | tf_op jit(solution)/shard_map/all_to_all | solution.py:25
  60.0 0.0 collective-permute-done.1
  60.0 0.0 collective-permute-done
  60.0 0.0 slice-done
  60.0 2.0 %divide_select_fusion.3 = (f32[8,16,1024]{2,1,0:T(8,128)S(1)}, f32[8,16,1024]{2,1,0:T(8,128)S(1)}, f32[8,16,1024]{2,1,0:T(8,128)S(1)}, f32[8,16,1024]{2,1,0:T(8,128)S(1)}) fusion(pred[1024]{0:T(1024)(128)(4,1)S(1)} %iota_compare_fusion, f32[8,16,1024]{2,1,0:T(8,128)S(1)} %copy-done, f32[1,16,1024]{2,1,0:T(8,128)S(1)} %collective-permute-done, ...), kind=kLoop, calls=%fused_computation.58 | loop fusion | flops 2883584 | bytes 5767704 | tf_op jit(solution)/shard_map/jit(_where)/select_n | solution.py:78
  61.9 0.3 divide_select_fusion.5
  62.4 1.9 %collective-permute-start.3 = (f32[8,1,1024]{2,1,0:T(1,128)S(1)}, f32[8,1,1024]{2,1,0:T(1,128)S(1)}, u32[]{:S(2)}, u32[]{:S(2)}) collective-permute-start(f32[8,1,1024]{2,1,0:T(1,128)S(1)} %slice.194), channel_id=1, source_target_pairs={{0,1},{1,2},{2,3},{3,4},{4,5},{5,6},{6,7},{7,8},{8,9},{9,10},{10,1... | collective-permute-start | bytes 98312 | tf_op jit(solution)/shard_map/ppermute | solution.py:35
  64.3 2.7 %collective-permute-start.2 = (f32[1,16,1024]{2,1,0:T(8,128)S(1)}, f32[1,16,1024]{2,1,0:T(8,128)S(1)}, u32[]{:S(2)}, u32[]{:S(2)}) collective-permute-start(f32[1,16,1024]{2,1,0:T(8,128)S(1)} %slice.192), channel_id=1, source_target_pairs={{0,16},{16,32},{32,48},{48,64},{64,80},{80,96},{96,112},{112,128},... | collective-permute-start | bytes 196616 | tf_op jit(solution)/shard_map/ppermute | solution.py:35
  67.0 0.9 all-to-all-done.1
  68.0 0.0 collective-permute-done.3
  68.0 15.3 %collective-permute-done.2 = f32[1,16,1024]{2,1,0:T(8,128)S(1)} collective-permute-done((f32[1,16,1024]{2,1,0:T(8,128)S(1)}, f32[1,16,1024]{2,1,0:T(8,128)S(1)}, u32[]{:S(2)}, u32[]{:S(2)}) %collective-permute-start.2) | collective-permute-done | bytes 65568 | tf_op jit(solution)/shard_map/ppermute | solution.py:35
  83.3 5.0 %multiply_subtract_fusion = (f32[8,16,1024]{2,1,0:T(8,128)S(1)}, f32[8,16,1024]{2,1,0:T(8,128)S(1)}) fusion(f32[8,16,1024]{2,1,0:T(8,128)S(1)} %copy-done, f32[]{:T(128)} %bitcast.20, f32[16,1024]{1,0:T(8,128)S(1)} %bitcast.53, f32[]{:T(128)} %bitcast.18, f32[16,1024]{1,0:T(8,128)S(1)} %bitcast.55, f32[]{:T(128)} %bitcast.16, f32[16,1024]{1,0:T(8,128)S(1)} %bitcast.57, ...), kind=kLoop, calls=%fused_computation.36 | loop fusion | flops 36831232 | bytes 4980272 | tf_op jit(solution)/shard_map/sub | solution.py:128
  88.3 1.9 %collective-permute-start.5 = (f32[1,16,1024]{2,1,0:T(8,128)S(1)}, f32[1,16,1024]{2,1,0:T(8,128)S(1)}, u32[]{:S(2)}, u32[]{:S(2)}) collective-permute-start(f32[1,16,1024]{2,1,0:T(8,128)S(1)} %slice.204), channel_id=1, source_target_pairs={{16,0},{32,16},{48,32},{64,48},{80,64},{96,80},{112,96},{128,112},... | collective-permute-start | bytes 196616 | tf_op jit(solution)/shard_map/ppermute | solution.py:35
  90.3 2.3 %collective-permute-start.6 = (f32[8,1,1024]{2,1,0:T(1,128)S(1)}, f32[8,1,1024]{2,1,0:T(1,128)S(1)}, u32[]{:S(2)}, u32[]{:S(2)}) collective-permute-start(f32[8,1,1024]{2,1,0:T(1,128)S(1)} %slice.206), channel_id=1, source_target_pairs={{1,0},{2,1},{3,2},{4,3},{5,4},{6,5},{7,6},{8,7},{9,8},{10,9},{11,1... | collective-permute-start | bytes 98312 | tf_op jit(solution)/shard_map/ppermute | solution.py:35
  95.0 0.2 slice.207
  95.2 0.1 slice.205
  95.3 0.8 collective-permute-done.6
  96.1 7.1 %collective-permute-done.5 = f32[1,16,1024]{2,1,0:T(8,128)S(1)} collective-permute-done((f32[1,16,1024]{2,1,0:T(8,128)S(1)}, f32[1,16,1024]{2,1,0:T(8,128)S(1)}, u32[]{:S(2)}, u32[]{:S(2)}) %collective-permute-start.5) | collective-permute-done | bytes 65568 | tf_op jit(solution)/shard_map/ppermute | solution.py:35
  103.2 0.6 divide_select_fusion
  103.8 0.2 divide_select_fusion.2
  104.1 6.5 %collective-permute-start.8 = (f32[8,1,1024]{2,1,0:T(1,128)S(1)}, f32[8,1,1024]{2,1,0:T(1,128)S(1)}, u32[]{:S(2)}, u32[]{:S(2)}) collective-permute-start(f32[8,1,1024]{2,1,0:T(1,128)S(1)} %slice.210), channel_id=1, source_target_pairs={{0,1},{1,2},{2,3},{3,4},{4,5},{5,6},{6,7},{7,8},{8,9},{9,10},{10,1... | collective-permute-start | bytes 98312 | tf_op jit(solution)/shard_map/ppermute | solution.py:35
  110.6 2.9 %collective-permute-start.7 = (f32[1,16,1024]{2,1,0:T(8,128)S(1)}, f32[1,16,1024]{2,1,0:T(8,128)S(1)}, u32[]{:S(2)}, u32[]{:S(2)}) collective-permute-start(f32[1,16,1024]{2,1,0:T(8,128)S(1)} %slice.208), channel_id=1, source_target_pairs={{0,16},{16,32},{32,48},{48,64},{64,80},{80,96},{96,112},{112,128},... | collective-permute-start | bytes 196616 | tf_op jit(solution)/shard_map/ppermute | solution.py:35
  113.6 1.2 pad_maximum_fusion
  114.9 0.0 collective-permute-done.8
  114.9 15.2 %collective-permute-done.7 = f32[1,16,1024]{2,1,0:T(8,128)S(1)} collective-permute-done((f32[1,16,1024]{2,1,0:T(8,128)S(1)}, f32[1,16,1024]{2,1,0:T(8,128)S(1)}, u32[]{:S(2)}, u32[]{:S(2)}) %collective-permute-start.7) | collective-permute-done | bytes 65568 | tf_op jit(solution)/shard_map/ppermute | solution.py:35
  130.1 9.6 %subtract_maximum_fusion = f32[8,16,1024]{2,1,0:T(8,128)} fusion(f32[8,16,1024]{2,1,0:T(8,128)S(1)} %get-tuple-element.7, f32[8,16,1024]{2,1,0:T(8,128)S(1)} %get-tuple-element.23, f32[8,15,1024]{2,1,0:T(8,128)S(1)} %bitcast.47, f32[8,1,1024]{2,1,0:T(1,128)S(1)} %collective-permute-done.8, f32[8,16,1024]{2,1,0:T(8,128)S(1)} %get-tuple-element.22, ...), kind=kLoop, calls=%fused_computation.30 | loop fusion | flops 65404928 | bytes 4718144 | tf_op jit(solution)/shard_map/max | solution.py:59
  (18 shorter events, 0.3 us)
Async XLA Ops:
  0.6 28.5 %copy-start.2 = (s32[2]{0:T(128)S(1)}, s32[2]{0:T(128)}, u32[]{:S(2)}) copy-start(s32[2]{0:T(128)} %param.8) | copy-start | bytes 28
  0.6 34.3 %copy-start.1 = (s32[2,4,1]{1,2,0:T(1,128)S(1)}, s32[2,4,1]{1,2,0:T(1,128)}, u32[]{:S(2)}) copy-start(s32[2,4,1]{1,2,0:T(1,128)} %param.9) | copy-start | bytes 100
  1.6 58.3 %collective-permute-start.1 = (f32[8,1,1024]{2,1,0:T(1,128)S(1)}, f32[8,1,1024]{2,1,0:T(1,128)S(1)}, u32[]{:S(2)}, u32[]{:S(2)}) collective-permute-start(f32[8,1,1024]{2,1,0:T(1,128)S(1)} %slice.154), channel_id=1, source_target_pairs={{1,0},{2,1},{3,2},{4,3},{5,4},{6,5},{7,6},{8,7},{9,8},{10,9},{11,1... | collective-permute-start | bytes 98312 | tf_op jit(solution)/shard_map/ppermute | solution.py:35
  4.4 55.6 %collective-permute-start = (f32[1,16,1024]{2,1,0:T(8,128)S(1)}, f32[1,16,1024]{2,1,0:T(8,128)S(1)}, u32[]{:S(2)}, u32[]{:S(2)}) collective-permute-start(f32[1,16,1024]{2,1,0:T(8,128)S(1)} %slice.151), channel_id=1, source_target_pairs={{16,0},{32,16},{48,32},{64,48},{80,64},{96,80},{112,96},{128,112},... | collective-permute-start | bytes 196616 | tf_op jit(solution)/shard_map/ppermute | solution.py:35
  24.3 16.5 %copy-start = (f32[8,16,1024]{2,1,0:T(8,128)S(1)}, f32[8,16,1024]{2,1,0:T(8,128)}, u32[]{:S(2)}) copy-start(f32[8,16,1024]{2,1,0:T(8,128)} %param.5) | copy-start | bytes 1572868
  24.3 14.2 %all-to-all-start = ((f32[16,2,4,8,128]{4,3,2,1,0:T(8,128)}), f32[16,2,4,8,128]{4,3,2,1,0:T(8,128)S(1)}, u32[]{:S(2)}, u32[]{:S(2)}) async-start(f32[16,2,4,8,128]{4,3,2,1,0:T(8,128)} %bitcast.5), calls=%async_computation | async-start | bytes 1048576 | tf_op jit(solution)/shard_map/all_to_all | solution.py:18
  38.6 14.9 %collective-permute-start.4 = (f32[2,4,8,128]{3,2,1,0:T(8,128)S(1)}, f32[2,4,8,128]{3,2,1,0:T(8,128)S(1)}, u32[]{:S(2)}, u32[]{:S(2)}) collective-permute-start(f32[2,4,8,128]{3,2,1,0:T(8,128)S(1)} %pad_maximum_fusion.1), channel_id=1, source_target_pairs={{0,16},{16,0},{32,48},{48,32},{64,80},{80,64},{96,112},{112,96},{1... | collective-permute-start | bytes 98312 | tf_op jit(solution)/shard_map/ppermute | solution.py:22
  40.9 19.1 %slice-start = ((f32[8,16,1024]{2,1,0:T(8,128)}), f32[7,16,1024]{2,1,0:T(8,128)S(1)}, s32[]{:S(2)}) async-start(f32[8,16,1024]{2,1,0:T(8,128)} %param.5), calls=%async_computation.2 | async-start | bytes 917504 | tf_op jit(solution)/shard_map/slice | solution.py:105
  54.4 13.6 %all-to-all-start.1 = ((f32[16,2,4,8,128]{4,3,2,1,0:T(8,128)}), f32[16,2,4,8,128]{4,3,2,1,0:T(8,128)S(1)}, u32[]{:S(2)}, u32[]{:S(2)}) async-start(f32[16,2,4,8,128]{4,3,2,1,0:T(8,128)} %broadcast_in_dim.103), calls=%async_computation.1 | async-start | bytes 1048576 | tf_op jit(solution)/shard_map/all_to_all | solution.py:25
  62.4 5.7 %collective-permute-start.3 = (f32[8,1,1024]{2,1,0:T(1,128)S(1)}, f32[8,1,1024]{2,1,0:T(1,128)S(1)}, u32[]{:S(2)}, u32[]{:S(2)}) collective-permute-start(f32[8,1,1024]{2,1,0:T(1,128)S(1)} %slice.194), channel_id=1, source_target_pairs={{0,1},{1,2},{2,3},{3,4},{4,5},{5,6},{6,7},{7,8},{8,9},{9,10},{10,1... | collective-permute-start | bytes 98312 | tf_op jit(solution)/shard_map/ppermute | solution.py:35
  64.3 19.0 %collective-permute-start.2 = (f32[1,16,1024]{2,1,0:T(8,128)S(1)}, f32[1,16,1024]{2,1,0:T(8,128)S(1)}, u32[]{:S(2)}, u32[]{:S(2)}) collective-permute-start(f32[1,16,1024]{2,1,0:T(8,128)S(1)} %slice.192), channel_id=1, source_target_pairs={{0,16},{16,32},{32,48},{48,64},{64,80},{80,96},{96,112},{112,128},... | collective-permute-start | bytes 196616 | tf_op jit(solution)/shard_map/ppermute | solution.py:35
  88.3 14.9 %collective-permute-start.5 = (f32[1,16,1024]{2,1,0:T(8,128)S(1)}, f32[1,16,1024]{2,1,0:T(8,128)S(1)}, u32[]{:S(2)}, u32[]{:S(2)}) collective-permute-start(f32[1,16,1024]{2,1,0:T(8,128)S(1)} %slice.204), channel_id=1, source_target_pairs={{16,0},{32,16},{48,32},{64,48},{80,64},{96,80},{112,96},{128,112},... | collective-permute-start | bytes 196616 | tf_op jit(solution)/shard_map/ppermute | solution.py:35
  90.3 5.8 %collective-permute-start.6 = (f32[8,1,1024]{2,1,0:T(1,128)S(1)}, f32[8,1,1024]{2,1,0:T(1,128)S(1)}, u32[]{:S(2)}, u32[]{:S(2)}) collective-permute-start(f32[8,1,1024]{2,1,0:T(1,128)S(1)} %slice.206), channel_id=1, source_target_pairs={{1,0},{2,1},{3,2},{4,3},{5,4},{6,5},{7,6},{8,7},{9,8},{10,9},{11,1... | collective-permute-start | bytes 98312 | tf_op jit(solution)/shard_map/ppermute | solution.py:35
  104.1 10.8 %collective-permute-start.8 = (f32[8,1,1024]{2,1,0:T(1,128)S(1)}, f32[8,1,1024]{2,1,0:T(1,128)S(1)}, u32[]{:S(2)}, u32[]{:S(2)}) collective-permute-start(f32[8,1,1024]{2,1,0:T(1,128)S(1)} %slice.210), channel_id=1, source_target_pairs={{0,1},{1,2},{2,3},{3,4},{4,5},{5,6},{6,7},{7,8},{8,9},{9,10},{10,1... | collective-permute-start | bytes 98312 | tf_op jit(solution)/shard_map/ppermute | solution.py:35
  110.6 19.4 %collective-permute-start.7 = (f32[1,16,1024]{2,1,0:T(8,128)S(1)}, f32[1,16,1024]{2,1,0:T(8,128)S(1)}, u32[]{:S(2)}, u32[]{:S(2)}) collective-permute-start(f32[1,16,1024]{2,1,0:T(8,128)S(1)} %slice.208), channel_id=1, source_target_pairs={{0,16},{16,32},{32,48},{48,64},{64,80},{80,96},{96,112},{112,128},... | collective-permute-start | bytes 196616 | tf_op jit(solution)/shard_map/ppermute | solution.py:35

commit v2 on v0

v2 whole, which is shorter than its diff:
```python
import jax
import jax.numpy as jnp
from jax import lax
from jax.experimental import pallas as pl
from jax.experimental.pallas import tpu as pltpu
from jax.sharding import PartitionSpec as P

VIEWS = 4
BINS = 8
BAND = 6
ITERS = 2

LAYERS = 8
ROWS = 16
LANES = 1024
STEP = 0.1
Z_LAST = 31
X_LAST = 15


def call(kernel, out_shapes, flops, in_specs=None):
    return pl.pallas_call(
        kernel,
        out_shape=tuple(jax.ShapeDtypeStruct(shape, jnp.float32) for shape in out_shapes),
        in_specs=in_specs,
        compiler_params=pltpu.CompilerParams(vmem_limit_bytes=16 << 20),
        cost_estimate=pl.CostEstimate(flops=flops, transcendentals=0, bytes_accessed=4 << 20),
        name=kernel.__name__ if hasattr(kernel, "__name__") else kernel.func.__name__,
    )


VMEM = pl.BlockSpec(memory_space=pltpu.VMEM)
SMEM = pl.BlockSpec(memory_space=pltpu.SMEM)
ANY = pl.BlockSpec(memory_space=pl.ANY)


def row_ids():
    return lax.broadcasted_iota(jnp.int32, (ROWS, LANES), 0)


def lane_ids():
    return lax.broadcasted_iota(jnp.int32, (ROWS, LANES), 1)


def spread_row(row):
    return jnp.broadcast_to(row, (ROWS, LANES))


def dual_layer(here, ahead_z, ahead_row, dual_z, dual_x, dual_y, z_end):
    row, lane = row_ids(), lane_ids()
    x_end = (row == ROWS - 1) & (lax.axis_index("tile") == X_LAST)
    y_end = lane == LANES - 1
    ahead_x = jnp.where(row == ROWS - 1, spread_row(ahead_row), pltpu.roll(here, ROWS - 1, 0))
    ahead_y = pltpu.roll(here, LANES - 1, 1)
    moved_z = dual_z + 0.25 * jnp.where(z_end, 0.0, ahead_z - here)
    moved_x = dual_x + 0.25 * jnp.where(x_end, 0.0, ahead_x - here)
    moved_y = dual_y + 0.25 * jnp.where(y_end, 0.0, ahead_y - here)
    norm = moved_z * moved_z + moved_x * moved_x + moved_y * moved_y
    scale = 1.0 / jnp.sqrt(jnp.maximum(norm, 1.0))
    return (
        jnp.where(z_end, 0.0, moved_z * scale),
        jnp.where(x_end, 0.0, moved_x * scale),
        jnp.where(y_end, 0.0, moved_y * scale),
    )


def flux(dual_x, dual_y, before_row):
    before = jnp.where(row_ids() == 0, spread_row(before_row), pltpu.roll(dual_x, 1, 0))
    return (dual_x - before) + (dual_y - pltpu.roll(dual_y, 1, 1))


def first_layer(field, dual, ahead, message):
    here = field[0]
    dual_z, dual_x, dual_y = dual_layer(here, field[1], ahead[0:1, :], dual[0, 0], dual[1, 0], dual[2, 0], False)
    message[0:16, :] = here
    message[16:32, :] = here + 0.25 * (dual_z + flux(dual_x, dual_y, jnp.zeros((1, LANES), jnp.float32)))
    message[32:40, :] = dual_x[8:16, :]


def all_duals(field, dual, ahead, below, new_dual, top, side):
    slab_end = lax.axis_index("slab") == Z_LAST
    for layer in range(LAYERS):
        last = layer == LAYERS - 1
        dual_z, dual_x, dual_y = dual_layer(
            field[layer],
            below[0:16, :] if last else field[layer + 1],
            ahead[layer : layer + 1, :],
            dual[0, layer],
            dual[1, layer],
            dual[2, layer],
            slab_end if last else False,
        )
        new_dual[0, layer] = dual_z
        new_dual[1, layer] = dual_x
        new_dual[2, layer] = dual_y
        side[layer : layer + 1, :] = dual_x[15:16, :]
        if last:
            top[...] = dual_z
    side[8:16, :] = jnp.zeros((8, LANES), jnp.float32)
    side[8:9, :] = below[39:40, :]


def all_steps(field, dual, above, before, below, values):
    for layer in range(LAYERS):
        prev = above[...] if layer == 0 else dual[0, layer - 1]
        values[layer] = field[layer] + 0.25 * (
            (dual[0, layer] - prev) + flux(dual[1, layer], dual[2, layer], before[layer : layer + 1, :])
        )
    side = jnp.where(row_ids() == 0, spread_row(before[8:9, :]), 0.0)
    values[LAYERS] = below[16:32, :] - 0.25 * (dual[0, LAYERS - 1] + side)


def ramps(depth, base):
    away = depth - base
    return away * (0.5 * STEP * (BINS - 1) / BAND) + 0.5 * STEP * (BINS - 1), away * (STEP / BAND) + 2.0 * STEP


def votes(views, caps, layer):
    sums, places, weights = None, None, None
    for (place, weight), cap in zip(views, caps):
        q = jnp.clip(place - layer * (0.5 * STEP * (BINS - 1) / BAND), 0.0, STEP * (BINS - 1))
        w = jnp.minimum(jnp.maximum(weight - layer * (STEP / BAND), 0.0), cap)
        e = q + w
        parts = [jnp.maximum(q, jnp.minimum(e, STEP * index)) for index in range(1, BINS)]
        sums = parts if sums is None else [total + part for total, part in zip(sums, parts)]
        places = q if places is None else places + q
        weights = w if weights is None else weights + w
    return sums, places, weights


def proximal(values, sums, places, weights):
    high = values + 0.5 * weights
    best = jnp.maximum(jnp.minimum(high, -1.0), values - 0.5 * weights)
    high = high + places
    for index in range(1, BINS):
        best = jnp.maximum(best, jnp.minimum(high - sums[index - 1], -1.0 + 2.0 * index / (BINS - 1)))
    return best


def block_of(index):
    half, column = index // 8, index % 8
    return half, column, pl.ds(pl.multiple_of(half * 8, 8), 8), pl.ds(pl.multiple_of(column * 128, 128), 128)


def slab_base():
    return (lax.axis_index("slab") * LAYERS).astype(jnp.float32)


def first_update(visible, field, values, below, batches, updated, extra, side):
    base = slab_base()
    caps = [STEP * visible[view].astype(jnp.float32) for view in range(VIEWS)]

    def body(index, carry):
        half, column, rows, lanes = block_of(index)
        views = [ramps(batches[2 * view + half, column], base) for view in range(VIEWS)]
        for layer in range(LAYERS + 1):
            new = proximal(values[layer, rows, lanes], *votes(views, caps, float(layer)))
            if layer < LAYERS:
                updated[layer, rows, lanes] = new
                extra[layer, rows, lanes] = 2.0 * new - field[layer, rows, lanes]
            else:
                extra[layer, rows, lanes] = 2.0 * new - below[rows, lanes]
        return carry

    lax.fori_loop(0, 16, body, 0)
    for layer in range(LAYERS):
        side[layer : layer + 1, :] = extra[layer, 0:1, :]


def second_duals(extra, dual, ahead, new_dual, top, side):
    slab_end = lax.axis_index("slab") == Z_LAST
    for layer in range(LAYERS):
        last = layer == LAYERS - 1
        dual_z, dual_x, dual_y = dual_layer(
            extra[layer],
            extra[layer + 1],
            ahead[layer : layer + 1, :],
            dual[0, layer],
            dual[1, layer],
            dual[2, layer],
            slab_end if last else False,
        )
        new_dual[0, layer] = dual_z
        new_dual[1, layer] = dual_x
        new_dual[2, layer] = dual_y
        side[layer : layer + 1, :] = dual_x[15:16, :]
        if last:
            top[...] = dual_z


def all_votes(visible, batches, after, tally):
    base = slab_base()
    caps = [STEP * visible[view].astype(jnp.float32) for view in range(ITERS * VIEWS)]

    def body(index, carry):
        half, column, rows, lanes = block_of(index)
        views = [ramps(batches[2 * view + half, column], base) for view in range(ITERS * VIEWS)]
        for layer in range(LAYERS):
            sums, places, weights = votes(views, caps, float(layer))
            for slot, total in enumerate(sums + [places, weights]):
                tally[slot, layer, rows, lanes] = total
        return carry

    lax.fori_loop(0, 16, body, 0)


def last_update(current, dual, above, before, tally, updated):
    for layer in range(LAYERS):
        prev = above[...] if layer == 0 else dual[0, layer - 1]
        values = current[layer] + 0.25 * (
            (dual[0, layer] - prev) + flux(dual[1, layer], dual[2, layer], before[layer : layer + 1, :])
        )
        sums = [tally[slot, layer] for slot in range(BINS - 1)]
        updated[layer] = proximal(values, sums, tally[BINS - 1, layer], tally[BINS, layer])


def passed_along(value, axis, steps):
    count = lax.axis_size(axis)
    first, last = (max(0, -steps), min(count, count - steps))
    return lax.ppermute(value, axis, [(source, source + steps) for source in range(first, last)])


GROUPS = [[2 * place + half for place in range(16)] for half in range(2)]


def exchange(pieces):
    return lax.all_to_all(pieces, "slab", 0, 0, axis_index_groups=GROUPS)


def per_device(field, dual, depth, owner, visible):
    slab = lax.axis_index("slab")
    seen = visible.reshape(ITERS * VIEWS)
    block = (LAYERS, ROWS, LANES)

    pieces = depth.reshape(16, 8, 8, 128).transpose(0, 2, 1, 3)
    spread = exchange(pieces)

    ahead = passed_along(field[:, 0], "tile", -1)
    (message,) = call(first_layer, [(40, LANES)], 1 << 19, [VMEM] * 3)(field[0:2], dual[:, 0:1], ahead)

    root = owner[slab // 16]
    kept = lax.dynamic_index_in_dim(spread, root // 2, 0, keepdims=False)
    kept, _ = lax.optimization_barrier((kept, message))
    across = lax.ppermute(kept, "slab", [(index, index ^ 1) for index in range(32)])
    below = passed_along(message, "slab", -1)
    dual, top, side = call(all_duals, [(3,) + block, (ROWS, LANES), (ROWS, LANES)], 1 << 22, [VMEM] * 4)(
        field, dual, ahead, below
    )
    across, top, side = lax.optimization_barrier((across, top, side))
    kept = jnp.where(root % 2 == slab % 2, kept, across)
    batches = exchange(jnp.broadcast_to(kept[None], pieces.shape))
    before = passed_along(side, "tile", 1)
    above = passed_along(top, "slab", 1)
    (values,) = call(all_steps, [(LAYERS + 1, ROWS, LANES)], 1 << 21, [VMEM] * 5)(field, dual, above, before, below)

    current, extra, side = call(
        first_update, [block, (LAYERS + 1, ROWS, LANES), (LAYERS, LANES)], 1 << 24, [SMEM] + [VMEM] * 4
    )(seen, field, values, below, batches)
    ahead = passed_along(side, "tile", -1)
    dual, top, side = call(second_duals, [(3,) + block, (ROWS, LANES), (LAYERS, LANES)], 1 << 22, [VMEM] * 3)(
        extra, dual, ahead
    )
    before = passed_along(side, "tile", 1)
    above = passed_along(top, "slab", 1)
    (tally,) = call(all_votes, [(BINS + 1,) + block], 1 << 25, [SMEM, VMEM, ANY])(seen, batches, dual)
    (current,) = call(last_update, [block], 1 << 22, [VMEM] * 5)(current, dual, above, before, tally)
    return (current, dual)


def solution(mesh):
    placed = (
        P("slab", "tile", None),
        P(None, "slab", "tile", None),
        P("slab", None, None, "tile", None),
        P(),
        P(None, None, "tile"),
    )
    return jax.shard_map(
        per_device,
        mesh=mesh,
        in_specs=placed,
        out_specs=(P("slab", "tile", None), P(None, "slab", "tile", None)),
        check_vma=False,
    )
```

time: 673 us -> 111 us (0.16)
  the two profiles are of different devices: /device:TPU:31 before, /device:TPU:67 now
where the time goes in v2:
time: 111 us
  starting transfers between devices  59.4 us (54%)
  waiting for transfers between devices  26.9 us (24%)
  Pallas kernels  12.6 us (11%)
  local copies, waits for them, and re-layouts  7.7 us (7%)
  between operations  3.47 us (3%)
    ppermute x7, starting transfers between devices, passed_along(): lax.ppermute(value, axis, [(source, source + steps) for source in range(f...  46.1 us
    ppermute x1, waiting for transfers between devices, per_device(): lax.ppermute(kept, 'slab', [(index, index ^ 1) for index in range(32)])  14.8 us
    ppermute x7, waiting for transfers between devices, passed_along(): lax.ppermute(value, axis, [(source, source + steps) for source in range(f...  12.1 us
    all_to_all x2, starting transfers between devices, exchange(): return lax.all_to_all(pieces, 'slab', 0, 0, axis_index_groups=GROUPS)  11.3 us
    pallas_call x1, Pallas kernels, per_device(): call(all_votes, [(BINS + 1,) + block], 1 << 25, [SMEM, VMEM, ANY])  4.76 us
    pallas_call x1, Pallas kernels, per_device(): call(first_update, [block, (LAYERS + 1, ROWS, LANES), (LAYERS, LANES)], 1...  3.53 us
    unnamed x12, local copies, waits for them, and re-layouts  3.35 us
  transfers between devices with their start and end apart: 10, of which 6 were waited for; matrix products, arithmetic and copies ran while one was open for 4% of the time, Pallas kernels for 5%

profile of v2, /device:TPU:67, one launch (start us, length us, event | category | flops | bytes accessed | tf_op | source)
XLA Modules:
  0.0 110.7 jit_solution(9683150173385370995)
XLA Ops:
  0.6 0.0 copy-start.1
  0.6 0.0 copy-start.4
  0.7 7.1 %all-to-all-start = ((f32[16,8,8,128]{3,2,1,0:T(8,128)}), f32[16,8,8,128]{3,2,1,0:T(8,128)S(1)}, u32[]{:S(2)}, u32[]{:S(2)}) async-start(f32[16,8,8,128]{3,2,1,0:T(8,128)} %bitcast.10), calls=%async_computation | async-start | bytes 1048576 | tf_op jit(solution)/shard_map/all_to_all | solution.py:227
  7.7 1.0 slice.9
  8.7 3.1 %collective-permute-start = (f32[8,1024]{1,0:T(8,128)S(1)}, f32[8,1024]{1,0:T(8,128)S(1)}, u32[]{:S(2)}, u32[]{:S(2)}) collective-permute-start(f32[8,1024]{1,0:T(8,128)S(1)} %bitcast.11), channel_id=1, source_target_pairs={{1,0},{2,1},{3,2},{4,3},{5,4},{6,5},{7,6},{8,7},{9,8},{10,9},{11,1... | collective-permute-start | bytes 98312 | tf_op jit(solution)/shard_map/ppermute | solution.py:220
  11.9 0.9 slice.10.field
  12.8 0.9 slice.11.dual
  13.7 1.5 %collective-permute-done.ahead = f32[8,1024]{1,0:T(8,128)S(1)} collective-permute-done((f32[8,1024]{1,0:T(8,128)S(1)}, f32[8,1024]{1,0:T(8,128)S(1)}, u32[]{:S(2)}, u32[]{:S(2)}) %collective-permute-start) | collective-permute-done | bytes 32800 | tf_op jit(solution)/shard_map/ppermute | solution.py:220
  15.3 0.2 first_layer.1
  15.5 14.9 %collective-permute-start.1 = (f32[40,1024]{1,0:T(8,128)S(1)}, f32[40,1024]{1,0:T(8,128)S(1)}, u32[]{:S(2)}, u32[]{:S(2)}) collective-permute-start(f32[40,1024]{1,0:T(8,128)S(1)} %first_layer.1), channel_id=1, source_target_pairs={{16,0},{32,16},{48,32},{64,48},{80,64},{96,80},{112,96},{128,112},... | collective-permute-start | bytes 491528 | tf_op jit(solution)/shard_map/ppermute | solution.py:220
  30.3 0.0 copy-done.4
  30.3 0.6 dynamic_slice.7
  33.5 0.0 all-to-all-done
  33.6 1.9 %collective-permute-start.2 = (f32[8,8,128]{2,1,0:T(8,128)S(1)}, f32[8,8,128]{2,1,0:T(8,128)S(1)}, u32[]{:S(2)}, u32[]{:S(2)}) collective-permute-start(f32[8,8,128]{2,1,0:T(8,128)S(1)} %dynamic-slice_bitcast_fusion), channel_id=1, source_target_pairs={{0,16},{16,0},{32,48},{48,32},{64,80},{80,64},{96,112},{112,96},{1... | collective-permute-start | bytes 98312 | tf_op jit(solution)/shard_map/ppermute | solution.py:244
  35.5 0.6 collective-permute-done.1.below
  36.1 0.0 copy-done.1
  36.1 0.0 copy-start.2
  36.1 1.4 %copy-done.2 = f32[3,8,16,1024]{3,2,1,0:T(8,128)S(1)} copy-done((f32[3,8,16,1024]{3,2,1,0:T(8,128)S(1)}, f32[3,8,16,1024]{3,2,1,0:T(8,128)}, u32[]{:S(2)}) %copy-start.2) | copy-done | bytes 1572888
  37.5 0.0 copy-start.3
  37.5 0.6 all_duals.1
  38.1 14.8 %collective-permute-done.2 = f32[8,8,128]{2,1,0:T(8,128)S(1)} collective-permute-done((f32[8,8,128]{2,1,0:T(8,128)S(1)}, f32[8,8,128]{2,1,0:T(8,128)S(1)}, u32[]{:S(2)}, u32[]{:S(2)}) %collective-permute-start.2) | collective-permute-done | bytes 32800 | tf_op jit(solution)/shard_map/ppermute | solution.py:244
  52.9 0.8 broadcast_in_dim.2
  53.8 4.3 %all-to-all-start.1 = ((f32[16,8,8,128]{3,2,1,0:T(8,128)}), f32[16,8,8,128]{3,2,1,0:T(8,128)S(1)}, u32[]{:S(2)}, u32[]{:S(2)}) async-start(f32[16,8,8,128]{3,2,1,0:T(8,128)} %broadcast_in_dim.2), calls=%async_computation.1 | async-start | bytes 1048576 | tf_op jit(solution)/shard_map/all_to_all | solution.py:227
  58.0 9.1 %collective-permute-start.3 = (f32[16,1024]{1,0:T(8,128)S(1)}, f32[16,1024]{1,0:T(8,128)S(1)}, u32[]{:S(2)}, u32[]{:S(2)}) collective-permute-start(f32[16,1024]{1,0:T(8,128)S(1)} %get-tuple-element.19), channel_id=1, source_target_pairs={{0,16},{16,32},{32,48},{48,64},{64,80},{80,96},{96,112},{112,128},... | collective-permute-start | bytes 196616 | tf_op jit(solution)/shard_map/ppermute | solution.py:220
  67.1 3.8 %collective-permute-start.4 = (f32[16,1024]{1,0:T(8,128)S(1)}, f32[16,1024]{1,0:T(8,128)S(1)}, u32[]{:S(2)}, u32[]{:S(2)}) collective-permute-start(f32[16,1024]{1,0:T(8,128)S(1)} %get-tuple-element.20), channel_id=1, source_target_pairs={{0,1},{1,2},{2,3},{3,4},{4,5},{5,6},{6,7},{7,8},{8,9},{9,10},{10,1... | collective-permute-start | bytes 196616 | tf_op jit(solution)/shard_map/ppermute | solution.py:220
  70.9 0.5 broadcast.8
  71.4 0.0 copy-done.3
  71.4 0.7 reduce.3
  72.1 0.1 reshape.11.visible
  72.2 2.6 %collective-permute-done.3.above = f32[16,1024]{1,0:T(8,128)S(1)} collective-permute-done((f32[16,1024]{1,0:T(8,128)S(1)}, f32[16,1024]{1,0:T(8,128)S(1)}, u32[]{:S(2)}, u32[]{:S(2)}) %collective-permute-start.3) | collective-permute-done | bytes 65568 | tf_op jit(solution)/shard_map/ppermute | solution.py:220
  74.8 0.0 collective-permute-done.4.before
  74.8 0.3 all_steps.1.values
  75.1 0.0 all-to-all-done.1.batches
  75.1 3.5 %first_update.1 = (f32[8,16,1024]{2,1,0:T(8,128)S(1)}, f32[9,16,1024]{2,1,0:T(8,128)S(1)}, f32[8,1024]{1,0:T(8,128)S(1)}) custom-call(s32[8]{0:T(128)S(1)} %reshape.11.visible, f32[8,16,1024]{2,1,0:T(8,128)S(1)} %copy-done.1, f32[9,16,1024]{2,1,0:T(8,128)S(1)} %all_steps.1.values, f32[40,1024]{1,0:T(8,128)S(1)} %collective-permute-done.1.below, ...), custom_call_target="tpu_custom_call" | custom-call | flops 16777216 | bytes 4194304 | tf_op jit(solution)/shard_map/first_update/pallas_call | solution.py:256
  78.7 8.3 %collective-permute-start.5 = (f32[8,1024]{1,0:T(8,128)S(1)}, f32[8,1024]{1,0:T(8,128)S(1)}, u32[]{:S(2)}, u32[]{:S(2)}) collective-permute-start(f32[8,1024]{1,0:T(8,128)S(1)} %get-tuple-element.24), channel_id=1, source_target_pairs={{1,0},{2,1},{3,2},{4,3},{5,4},{6,5},{7,6},{8,7},{9,8},{10,9},{11,1... | collective-permute-start | bytes 98312 | tf_op jit(solution)/shard_map/ppermute | solution.py:220
  87.0 0.8 collective-permute-done.5.ahead
  87.8 1.8 %second_duals.1 = (f32[3,8,16,1024]{3,2,1,0:T(8,128)}, f32[16,1024]{1,0:T(8,128)S(1)}, f32[8,1024]{1,0:T(8,128)S(1)}) custom-call(f32[9,16,1024]{2,1,0:T(8,128)S(1)} %get-tuple-element.23.extra, f32[3,8,16,1024]{3,2,1,0:T(8,128)S(1)} %get-tuple-element.15.dual, f32[8,1024]{1,0:T(8,128)S(1)} %collective-permute-done.5.ahead), custom_call_target="tpu_custom_call" | custom-call | flops 4194304 | bytes 4194304 | tf_op jit(solution)/shard_map/second_duals/pallas_call | solution.py:260
  89.6 4.8 %collective-permute-start.6 = (f32[16,1024]{1,0:T(8,128)S(1)}, f32[16,1024]{1,0:T(8,128)S(1)}, u32[]{:S(2)}, u32[]{:S(2)}) collective-permute-start(f32[16,1024]{1,0:T(8,128)S(1)} %get-tuple-element.26), channel_id=1, source_target_pairs={{0,16},{16,32},{32,48},{48,64},{64,80},{80,96},{96,112},{112,128},... | collective-permute-start | bytes 196616 | tf_op jit(solution)/shard_map/ppermute | solution.py:220
  94.4 2.2 %collective-permute-start.7 = (f32[8,1024]{1,0:T(8,128)S(1)}, f32[8,1024]{1,0:T(8,128)S(1)}, u32[]{:S(2)}, u32[]{:S(2)}) collective-permute-start(f32[8,1024]{1,0:T(8,128)S(1)} %get-tuple-element.27), channel_id=1, source_target_pairs={{0,1},{1,2},{2,3},{3,4},{4,5},{5,6},{6,7},{7,8},{8,9},{9,10},{10,1... | collective-permute-start | bytes 98312 | tf_op jit(solution)/shard_map/ppermute | solution.py:220
  96.5 0.0 copy-start
  96.5 1.4 %copy-done = f32[3,8,16,1024]{3,2,1,0:T(8,128)S(1)} copy-done((f32[3,8,16,1024]{3,2,1,0:T(8,128)S(1)}, f32[3,8,16,1024]{3,2,1,0:T(8,128)}, u32[]{:S(2)}) %copy-start) | copy-done | bytes 1572888
  97.9 4.8 %all_votes.1.tally = f32[9,8,16,1024]{3,2,1,0:T(8,128)S(1)} custom-call(s32[8]{0:T(128)S(1)} %reshape.11.visible, f32[16,8,8,128]{3,2,1,0:T(8,128)S(1)} %all-to-all-done.1.batches, f32[3,8,16,1024]{3,2,1,0:T(8,128)S(1)} %copy-done), custom_call_target="tpu_custom_call" | custom-call | flops 33554432 | bytes 4194304 | tf_op jit(solution)/shard_map/all_votes/pallas_call | solution.py:265
  102.7 0.0 collective-permute-done.7.before
  102.7 6.5 %collective-permute-done.6.above = f32[16,1024]{1,0:T(8,128)S(1)} collective-permute-done((f32[16,1024]{1,0:T(8,128)S(1)}, f32[16,1024]{1,0:T(8,128)S(1)}, u32[]{:S(2)}, u32[]{:S(2)}) %collective-permute-start.6) | collective-permute-done | bytes 65568 | tf_op jit(solution)/shard_map/ppermute | solution.py:220
  109.2 1.6 %last_update.1 = f32[8,16,1024]{2,1,0:T(8,128)} custom-call(f32[8,16,1024]{2,1,0:T(8,128)S(1)} %get-tuple-element.22.current, f32[3,8,16,1024]{3,2,1,0:T(8,128)S(1)} %copy-done, f32[16,1024]{1,0:T(8,128)S(1)} %collective-permute-done.6.above, f32[8,1024]{1,0:T(8,128)S(1)} %collective-permute-done.7.before, f32[9,8,16,1024]{3,2,1,0:T(8,128)S(1)} %all_votes.1.tally), custom_call_target="tpu_custom_call" | custom-call | flops 4194304 | bytes 4194304 | tf_op jit(solution)/shard_map/last_update/pallas_call | solution.py:266
  (3 shorter events, 0.0 us)
Async XLA Ops:
  0.6 35.5 %copy-start.1 = (f32[8,16,1024]{2,1,0:T(8,128)S(1)}, f32[8,16,1024]{2,1,0:T(8,128)}, u32[]{:S(2)}) copy-start(f32[8,16,1024]{2,1,0:T(8,128)} %field.5) | copy-start | bytes 1572868
  0.6 29.7 %copy-start.4 = (s32[2]{0:T(128)S(1)}, s32[2]{0:T(128)}, u32[]{:S(2)}) copy-start(s32[2]{0:T(128)} %param.8) | copy-start | bytes 28
  0.7 32.9 %all-to-all-start = ((f32[16,8,8,128]{3,2,1,0:T(8,128)}), f32[16,8,8,128]{3,2,1,0:T(8,128)S(1)}, u32[]{:S(2)}, u32[]{:S(2)}) async-start(f32[16,8,8,128]{3,2,1,0:T(8,128)} %bitcast.10), calls=%async_computation | async-start | bytes 1048576 | tf_op jit(solution)/shard_map/all_to_all | solution.py:227
  8.7 6.6 %collective-permute-start = (f32[8,1024]{1,0:T(8,128)S(1)}, f32[8,1024]{1,0:T(8,128)S(1)}, u32[]{:S(2)}, u32[]{:S(2)}) collective-permute-start(f32[8,1024]{1,0:T(8,128)S(1)} %bitcast.11), channel_id=1, source_target_pairs={{1,0},{2,1},{3,2},{4,3},{5,4},{6,5},{7,6},{8,7},{9,8},{10,9},{11,1... | collective-permute-start | bytes 98312 | tf_op jit(solution)/shard_map/ppermute | solution.py:220
  15.5 20.6 %collective-permute-start.1 = (f32[40,1024]{1,0:T(8,128)S(1)}, f32[40,1024]{1,0:T(8,128)S(1)}, u32[]{:S(2)}, u32[]{:S(2)}) collective-permute-start(f32[40,1024]{1,0:T(8,128)S(1)} %first_layer.1), channel_id=1, source_target_pairs={{16,0},{32,16},{48,32},{64,48},{80,64},{96,80},{112,96},{128,112},... | collective-permute-start | bytes 491528 | tf_op jit(solution)/shard_map/ppermute | solution.py:220
  33.6 19.3 %collective-permute-start.2 = (f32[8,8,128]{2,1,0:T(8,128)S(1)}, f32[8,8,128]{2,1,0:T(8,128)S(1)}, u32[]{:S(2)}, u32[]{:S(2)}) collective-permute-start(f32[8,8,128]{2,1,0:T(8,128)S(1)} %dynamic-slice_bitcast_fusion), channel_id=1, source_target_pairs={{0,16},{16,0},{32,48},{48,32},{64,80},{80,64},{96,112},{112,96},{1... | collective-permute-start | bytes 98312 | tf_op jit(solution)/shard_map/ppermute | solution.py:244
  36.1 1.4 %copy-start.2 = (f32[3,8,16,1024]{3,2,1,0:T(8,128)S(1)}, f32[3,8,16,1024]{3,2,1,0:T(8,128)}, u32[]{:S(2)}) copy-start(f32[3,8,16,1024]{3,2,1,0:T(8,128)} %dual.1) | copy-start | bytes 4718596
  37.5 33.9 %copy-start.3 = (s32[2,4,1]{1,2,0:T(1,128)S(1)}, s32[2,4,1]{1,2,0:T(1,128)}, u32[]{:S(2)}) copy-start(s32[2,4,1]{1,2,0:T(1,128)} %param.9) | copy-start | bytes 100
  53.8 21.3 %all-to-all-start.1 = ((f32[16,8,8,128]{3,2,1,0:T(8,128)}), f32[16,8,8,128]{3,2,1,0:T(8,128)S(1)}, u32[]{:S(2)}, u32[]{:S(2)}) async-start(f32[16,8,8,128]{3,2,1,0:T(8,128)} %broadcast_in_dim.2), calls=%async_computation.1 | async-start | bytes 1048576 | tf_op jit(solution)/shard_map/all_to_all | solution.py:227
  58.0 16.8 %collective-permute-start.3 = (f32[16,1024]{1,0:T(8,128)S(1)}, f32[16,1024]{1,0:T(8,128)S(1)}, u32[]{:S(2)}, u32[]{:S(2)}) collective-permute-start(f32[16,1024]{1,0:T(8,128)S(1)} %get-tuple-element.19), channel_id=1, source_target_pairs={{0,16},{16,32},{32,48},{48,64},{64,80},{80,96},{96,112},{112,128},... | collective-permute-start | bytes 196616 | tf_op jit(solution)/shard_map/ppermute | solution.py:220
  67.1 7.7 %collective-permute-start.4 = (f32[16,1024]{1,0:T(8,128)S(1)}, f32[16,1024]{1,0:T(8,128)S(1)}, u32[]{:S(2)}, u32[]{:S(2)}) collective-permute-start(f32[16,1024]{1,0:T(8,128)S(1)} %get-tuple-element.20), channel_id=1, source_target_pairs={{0,1},{1,2},{2,3},{3,4},{4,5},{5,6},{6,7},{7,8},{8,9},{9,10},{10,1... | collective-permute-start | bytes 196616 | tf_op jit(solution)/shard_map/ppermute | solution.py:220
  78.7 9.2 %collective-permute-start.5 = (f32[8,1024]{1,0:T(8,128)S(1)}, f32[8,1024]{1,0:T(8,128)S(1)}, u32[]{:S(2)}, u32[]{:S(2)}) collective-permute-start(f32[8,1024]{1,0:T(8,128)S(1)} %get-tuple-element.24), channel_id=1, source_target_pairs={{1,0},{2,1},{3,2},{4,3},{5,4},{6,5},{7,6},{8,7},{9,8},{10,9},{11,1... | collective-permute-start | bytes 98312 | tf_op jit(solution)/shard_map/ppermute | solution.py:220
  89.6 19.6 %collective-permute-start.6 = (f32[16,1024]{1,0:T(8,128)S(1)}, f32[16,1024]{1,0:T(8,128)S(1)}, u32[]{:S(2)}, u32[]{:S(2)}) collective-permute-start(f32[16,1024]{1,0:T(8,128)S(1)} %get-tuple-element.26), channel_id=1, source_target_pairs={{0,16},{16,32},{32,48},{48,64},{64,80},{80,96},{96,112},{112,128},... | collective-permute-start | bytes 196616 | tf_op jit(solution)/shard_map/ppermute | solution.py:220
  94.4 8.4 %collective-permute-start.7 = (f32[8,1024]{1,0:T(8,128)S(1)}, f32[8,1024]{1,0:T(8,128)S(1)}, u32[]{:S(2)}, u32[]{:S(2)}) collective-permute-start(f32[8,1024]{1,0:T(8,128)S(1)} %get-tuple-element.27), channel_id=1, source_target_pairs={{0,1},{1,2},{2,3},{3,4},{4,5},{5,6},{6,7},{7,8},{8,9},{9,10},{10,1... | collective-permute-start | bytes 98312 | tf_op jit(solution)/shard_map/ppermute | solution.py:220
  96.5 1.4 %copy-start = (f32[3,8,16,1024]{3,2,1,0:T(8,128)S(1)}, f32[3,8,16,1024]{3,2,1,0:T(8,128)}, u32[]{:S(2)}) copy-start(f32[3,8,16,1024]{3,2,1,0:T(8,128)} %get-tuple-element.14.after.dual) | copy-start | bytes 4718596

commit v3 on v2

--- a/solution.py
+++ b/solution.py
@@ -18,14 +18,15 @@
 X_LAST = 15
 
 
-def call(kernel, out_shapes, flops, in_specs=None):
+def call(kernel, out_shapes, cost_us, in_specs, **more):
     return pl.pallas_call(
         kernel,
         out_shape=tuple(jax.ShapeDtypeStruct(shape, jnp.float32) for shape in out_shapes),
         in_specs=in_specs,
         compiler_params=pltpu.CompilerParams(vmem_limit_bytes=16 << 20),
-        cost_estimate=pl.CostEstimate(flops=flops, transcendentals=0, bytes_accessed=4 << 20),
-        name=kernel.__name__ if hasattr(kernel, "__name__") else kernel.func.__name__,
+        cost_estimate=pl.CostEstimate(flops=0, transcendentals=0, bytes_accessed=int(cost_us * 3.0e6)),
+        name=kernel.__name__,
+        **more,
     )
 
 
@@ -100,16 +101,6 @@
     side[8:9, :] = below[39:40, :]
 
 
-def all_steps(field, dual, above, before, below, values):
-    for layer in range(LAYERS):
-        prev = above[...] if layer == 0 else dual[0, layer - 1]
-        values[layer] = field[layer] + 0.25 * (
-            (dual[0, layer] - prev) + flux(dual[1, layer], dual[2, layer], before[layer : layer + 1, :])
-        )
-    side = jnp.where(row_ids() == 0, spread_row(before[8:9, :]), 0.0)
-    values[LAYERS] = below[16:32, :] - 0.25 * (dual[0, LAYERS - 1] + side)
-
-
 def ramps(depth, base):
     away = depth - base
     return away * (0.5 * STEP * (BINS - 1) / BAND) + 0.5 * STEP * (BINS - 1), away * (STEP / BAND) + 2.0 * STEP
@@ -146,7 +137,7 @@
     return (lax.axis_index("slab") * LAYERS).astype(jnp.float32)
 
 
-def first_update(visible, field, values, below, batches, updated, extra, side):
+def first_votes(visible, batches, tally):
     base = slab_base()
     caps = [STEP * visible[view].astype(jnp.float32) for view in range(VIEWS)]
 
@@ -154,20 +145,63 @@
         half, column, rows, lanes = block_of(index)
         views = [ramps(batches[2 * view + half, column], base) for view in range(VIEWS)]
         for layer in range(LAYERS + 1):
-            new = proximal(values[layer, rows, lanes], *votes(views, caps, float(layer)))
-            if layer < LAYERS:
-                updated[layer, rows, lanes] = new
-                extra[layer, rows, lanes] = 2.0 * new - field[layer, rows, lanes]
-            else:
-                extra[layer, rows, lanes] = 2.0 * new - below[rows, lanes]
+            sums, places, weights = votes(views, caps, float(layer))
+            for slot, total in enumerate(sums + [places, weights]):
+                tally[slot, layer, rows, lanes] = total
         return carry
 
     lax.fori_loop(0, 16, body, 0)
+
+
+def second_votes(visible, batches, tally, after, new_tally):
+    base = slab_base()
+    caps = [STEP * visible[VIEWS + view].astype(jnp.float32) for view in range(VIEWS)]
+
+    def body(index, carry):
+        half, column, rows, lanes = block_of(index)
+        views = [ramps(batches[2 * (VIEWS + view) + half, column], base) for view in range(VIEWS)]
+        for layer in range(LAYERS):
+            sums, places, weights = votes(views, caps, float(layer))
+            for slot, total in enumerate(sums + [places, weights]):
+                new_tally[slot, layer, rows, lanes] = tally[slot, layer, rows, lanes] + total
+        return carry
+
+    lax.fori_loop(0, 16, body, 0)
+
+
+def counted(values, tally, layer):
+    sums = [tally[slot, layer] for slot in range(BINS - 1)]
+    return proximal(values, sums, tally[BINS - 1, layer], tally[BINS, layer])
+
+
+def stepped(field, dual, above, before, layer):
+    prev = above[...] if layer == 0 else dual[0, layer - 1]
+    return field[layer] + 0.25 * (
+        (dual[0, layer] - prev) + flux(dual[1, layer], dual[2, layer], before[layer : layer + 1, :])
+    )
+
+
+def first_update(field, dual, above, before, below, tally, updated, extra, side):
     for layer in range(LAYERS):
-        side[layer : layer + 1, :] = extra[layer, 0:1, :]
-
-
-def second_duals(extra, dual, ahead, new_dual, top, side):
+        new = counted(stepped(field, dual, above, before, layer), tally, layer)
+        updated[layer] = new
+        new = 2.0 * new - field[layer]
+        extra[layer] = new
+        side[layer : layer + 1, :] = new[0:1, :]
+    past = jnp.where(row_ids() == 0, spread_row(before[8:9, :]), 0.0)
+    values = below[16:32, :] - 0.25 * (dual[0, LAYERS - 1] + past)
+    extra[LAYERS] = 2.0 * counted(values, tally, LAYERS) - below[0:16, :]
+
+
+def top_dual(extra, dual, ahead, top):
+    layer = LAYERS - 1
+    slab_end = lax.axis_index("slab") == Z_LAST
+    top[...] = dual_layer(
+        extra[0], extra[1], ahead[layer : layer + 1, :], dual[0, 0], dual[1, 0], dual[2, 0], slab_end
+    )[0]
+
+
+def second_duals(extra, dual, ahead, after, new_dual, side):
     slab_end = lax.axis_index("slab") == Z_LAST
     for layer in range(LAYERS):
         last = layer == LAYERS - 1
@@ -184,34 +218,15 @@
         new_dual[1, layer] = dual_x
         new_dual[2, layer] = dual_y
         side[layer : layer + 1, :] = dual_x[15:16, :]
-        if last:
-            top[...] = dual_z
-
-
-def all_votes(visible, batches, after, tally):
-    base = slab_base()
-    caps = [STEP * visible[view].astype(jnp.float32) for view in range(ITERS * VIEWS)]
-
-    def body(index, carry):
-        half, column, rows, lanes = block_of(index)
-        views = [ramps(batches[2 * view + half, column], base) for view in range(ITERS * VIEWS)]
-        for layer in range(LAYERS):
-            sums, places, weights = votes(views, caps, float(layer))
-            for slot, total in enumerate(sums + [places, weights]):
-                tally[slot, layer, rows, lanes] = total
-        return carry
-
-    lax.fori_loop(0, 16, body, 0)
-
-
-def last_update(current, dual, above, before, tally, updated):
-    for layer in range(LAYERS):
-        prev = above[...] if layer == 0 else dual[0, layer - 1]
-        values = current[layer] + 0.25 * (
-            (dual[0, layer] - prev) + flux(dual[1, layer], dual[2, layer], before[layer : layer + 1, :])
-        )
-        sums = [tally[slot, layer] for slot in range(BINS - 1)]
-        updated[layer] = proximal(values, sums, tally[BINS - 1, layer], tally[BINS, layer])
+
+
+def last_layers(current, dual, before, tally, updated):
+    for layer in range(1, LAYERS):
+        updated[layer] = counted(stepped(current, dual, None, before, layer), tally, layer)
+
+
+def last_layer(current, dual, above, before, tally, updated_in, updated):
+    updated[0] = counted(stepped(current, dual, above, before, 0), tally, 0)
 
 
 def passed_along(value, axis, steps):
@@ -232,18 +247,23 @@
     seen = visible.reshape(ITERS * VIEWS)
     block = (LAYERS, ROWS, LANES)
 
+    first_one = pl.BlockSpec((1, ROWS, LANES), lambda step: (0, 0, 0))
+    first_one_dual = pl.BlockSpec((3, 1, ROWS, LANES), lambda step: (0, 0, 0, 0))
+    tally_one = pl.BlockSpec((BINS + 1, 1, ROWS, LANES), lambda step: (0, 0, 0, 0))
+    first = pl.BlockSpec((2, ROWS, LANES), lambda step: (0, 0, 0))
+
     pieces = depth.reshape(16, 8, 8, 128).transpose(0, 2, 1, 3)
     spread = exchange(pieces)
 
     ahead = passed_along(field[:, 0], "tile", -1)
-    (message,) = call(first_layer, [(40, LANES)], 1 << 19, [VMEM] * 3)(field[0:2], dual[:, 0:1], ahead)
+    (message,) = call(first_layer, [(40, LANES)], 1, [first, first_one_dual, VMEM], grid=(1,))(field, dual, ahead)
 
     root = owner[slab // 16]
     kept = lax.dynamic_index_in_dim(spread, root // 2, 0, keepdims=False)
     kept, _ = lax.optimization_barrier((kept, message))
     across = lax.ppermute(kept, "slab", [(index, index ^ 1) for index in range(32)])
     below = passed_along(message, "slab", -1)
-    dual, top, side = call(all_duals, [(3,) + block, (ROWS, LANES), (ROWS, LANES)], 1 << 22, [VMEM] * 4)(
+    dual, top, side = call(all_duals, [(3,) + block, (ROWS, LANES), (ROWS, LANES)], 1, [VMEM] * 4)(
         field, dual, ahead, below
     )
     across, top, side = lax.optimization_barrier((across, top, side))
@@ -251,19 +271,24 @@
     batches = exchange(jnp.broadcast_to(kept[None], pieces.shape))
     before = passed_along(side, "tile", 1)
     above = passed_along(top, "slab", 1)
-    (values,) = call(all_steps, [(LAYERS + 1, ROWS, LANES)], 1 << 21, [VMEM] * 5)(field, dual, above, before, below)
-
-    current, extra, side = call(
-        first_update, [block, (LAYERS + 1, ROWS, LANES), (LAYERS, LANES)], 1 << 24, [SMEM] + [VMEM] * 4
-    )(seen, field, values, below, batches)
+
+    (tally,) = call(first_votes, [(BINS + 1, LAYERS + 1, ROWS, LANES)], 4, [SMEM, VMEM])(seen, batches)
+    above, before, tally = lax.optimization_barrier((above, before, tally))
+    current, extra, side = call(first_update, [block, (LAYERS + 1, ROWS, LANES), (LAYERS, LANES)], 1, [VMEM] * 6)(
+        field, dual, above, before, below, tally
+    )
     ahead = passed_along(side, "tile", -1)
-    dual, top, side = call(second_duals, [(3,) + block, (ROWS, LANES), (LAYERS, LANES)], 1 << 22, [VMEM] * 3)(
-        extra, dual, ahead
-    )
+    (top,) = call(top_dual, [(ROWS, LANES)], 1, [VMEM] * 3)(extra[7:9], dual[:, 7:8], ahead)
+    above = passed_along(top, "slab", 1)
+    dual, side = call(second_duals, [(3,) + block, (LAYERS, LANES)], 1, [VMEM] * 3 + [ANY])(extra, dual, ahead, top)
     before = passed_along(side, "tile", 1)
-    above = passed_along(top, "slab", 1)
-    (tally,) = call(all_votes, [(BINS + 1,) + block], 1 << 25, [SMEM, VMEM, ANY])(seen, batches, dual)
-    (current,) = call(last_update, [block], 1 << 22, [VMEM] * 5)(current, dual, above, before, tally)
+    (tally,) = call(second_votes, [(BINS + 1,) + block], 3, [SMEM, VMEM, VMEM, ANY])(seen, batches, tally, dual)
+    (rest,) = call(last_layers, [block], 1, [VMEM] * 4)(current, dual, before, tally)
+    above, rest = lax.optimization_barrier((above, rest))
+    (current,) = call(
+        last_layer, [block], 1, [first_one, first_one_dual, VMEM, VMEM, tally_one, ANY], grid=(1,),
+        out_specs=(first_one,), input_output_aliases={5: 0},
+    )(current, dual, above, before, tally, rest)
     return (current, dual)
 
 

time: 111 us -> 108 us (0.973)
  the two profiles are of different devices: /device:TPU:67 before, /device:TPU:35 now
where the time goes in v3:
time: 108 us
  starting transfers between devices  57 us (53%)
  waiting for transfers between devices  27 us (25%)
  Pallas kernels  11.6 us (11%)
  local copies, waits for them, and re-layouts  7.95 us (7%)
  between operations  3.49 us (3%)
    ppermute x7, starting transfers between devices, passed_along(): lax.ppermute(value, axis, [(source, source + steps) for source in range(f...  43.9 us
    ppermute x7, waiting for transfers between devices, passed_along(): lax.ppermute(value, axis, [(source, source + steps) for source in range(f...  26.9 us
    all_to_all x2, starting transfers between devices, exchange(): return lax.all_to_all(pieces, 'slab', 0, 0, axis_index_groups=GROUPS)  11.2 us
    unnamed x18, local copies, waits for them, and re-layouts  5.43 us
    pallas_call x1, Pallas kernels, per_device(): call(first_votes, [(BINS + 1, LAYERS + 1, ROWS, LANES)], 4, [SMEM, VMEM])  2.92 us
    pallas_call x1, Pallas kernels, per_device(): call(second_votes, [(BINS + 1,) + block], 3, [SMEM, VMEM, VMEM, ANY])  2.84 us
  transfers between devices with their start and end apart: 10, of which 5 were waited for; matrix products, arithmetic and copies ran while one was open for 3% of the time, Pallas kernels for 9%

profile of v3, /device:TPU:35, one launch (start us, length us, event | category | flops | bytes accessed | tf_op | source)
XLA Modules:
  0.0 107.6 jit_solution(9200221972119307267)
XLA Ops:
  0.6 0.0 copy-start.7
  0.6 6.9 %all-to-all-start = ((f32[16,8,8,128]{3,2,1,0:T(8,128)}), f32[16,8,8,128]{3,2,1,0:T(8,128)S(1)}, u32[]{:S(2)}, u32[]{:S(2)}) async-start(f32[16,8,8,128]{3,2,1,0:T(8,128)} %bitcast.10), calls=%async_computation | async-start | bytes 1048576 | tf_op jit(solution)/shard_map/all_to_all | solution.py:242
  7.6 1.0 slice.9
  8.6 3.1 %collective-permute-start = (f32[8,1024]{1,0:T(8,128)S(1)}, f32[8,1024]{1,0:T(8,128)S(1)}, u32[]{:S(2)}, u32[]{:S(2)}) collective-permute-start(f32[8,1024]{1,0:T(8,128)S(1)} %bitcast.11), channel_id=1, source_target_pairs={{1,0},{2,1},{3,2},{4,3},{5,4},{6,5},{7,6},{8,7},{9,8},{10,9},{11,1... | collective-permute-start | bytes 98312 | tf_op jit(solution)/shard_map/ppermute | solution.py:235
  11.7 3.4 %collective-permute-done.ahead = f32[8,1024]{1,0:T(8,128)S(1)} collective-permute-done((f32[8,1024]{1,0:T(8,128)S(1)}, f32[8,1024]{1,0:T(8,128)S(1)}, u32[]{:S(2)}, u32[]{:S(2)}) %collective-permute-start) | collective-permute-done | bytes 32800 | tf_op jit(solution)/shard_map/ppermute | solution.py:235
  15.1 0.0 copy-start.1
  15.1 1.4 %copy-done.1 = f32[3,8,16,1024]{3,2,1,0:T(8,128)S(1)} copy-done((f32[3,8,16,1024]{3,2,1,0:T(8,128)S(1)}, f32[3,8,16,1024]{3,2,1,0:T(8,128)}, u32[]{:S(2)}) %copy-start.1) | copy-done | bytes 1572888
  16.5 0.0 copy-start.3
  16.5 1.0 copy-done.3
  17.6 0.0 copy-start.2
  17.6 0.2 first_layer.1
  17.8 15.9 %collective-permute-start.1 = (f32[40,1024]{1,0:T(8,128)S(1)}, f32[40,1024]{1,0:T(8,128)S(1)}, u32[]{:S(2)}, u32[]{:S(2)}) collective-permute-start(f32[40,1024]{1,0:T(8,128)S(1)} %first_layer.1), channel_id=1, source_target_pairs={{16,0},{32,16},{48,32},{64,48},{80,64},{96,80},{112,96},{128,112},... | collective-permute-start | bytes 491528 | tf_op jit(solution)/shard_map/ppermute | solution.py:235
  33.7 0.0 copy-done.7
  33.7 0.6 dynamic_slice.7
  36.9 0.0 all-to-all-done
  36.9 1.9 %collective-permute-start.2 = (f32[8,8,128]{2,1,0:T(8,128)S(1)}, f32[8,8,128]{2,1,0:T(8,128)S(1)}, u32[]{:S(2)}, u32[]{:S(2)}) collective-permute-start(f32[8,8,128]{2,1,0:T(8,128)S(1)} %dynamic-slice_bitcast_fusion), channel_id=1, source_target_pairs={{0,16},{16,0},{32,48},{48,32},{64,80},{80,64},{96,112},{112,96},{1... | collective-permute-start | bytes 98312 | tf_op jit(solution)/shard_map/ppermute | solution.py:264
  38.9 10.9 %collective-permute-done.1.below = f32[40,1024]{1,0:T(8,128)S(1)} collective-permute-done((f32[40,1024]{1,0:T(8,128)S(1)}, f32[40,1024]{1,0:T(8,128)S(1)}, u32[]{:S(2)}, u32[]{:S(2)}) %collective-permute-start.1) | collective-permute-done | bytes 163872 | tf_op jit(solution)/shard_map/ppermute | solution.py:235
  49.8 0.0 copy-done.2
  49.8 1.0 copy-done.4
  50.8 0.6 all_duals.1
  51.4 0.0 collective-permute-done.2
  51.4 0.8 broadcast_in_dim.2
  52.3 4.3 %all-to-all-start.1 = ((f32[16,8,8,128]{3,2,1,0:T(8,128)}), f32[16,8,8,128]{3,2,1,0:T(8,128)S(1)}, u32[]{:S(2)}, u32[]{:S(2)}) async-start(f32[16,8,8,128]{3,2,1,0:T(8,128)} %broadcast_in_dim.2), calls=%async_computation.1 | async-start | bytes 1048576 | tf_op jit(solution)/shard_map/all_to_all | solution.py:242
  56.5 15.6 %collective-permute-start.3 = (f32[16,1024]{1,0:T(8,128)S(1)}, f32[16,1024]{1,0:T(8,128)S(1)}, u32[]{:S(2)}, u32[]{:S(2)}) collective-permute-start(f32[16,1024]{1,0:T(8,128)S(1)} %get-tuple-element.23), channel_id=1, source_target_pairs={{0,16},{16,32},{32,48},{48,64},{64,80},{80,96},{96,112},{112,128},... | collective-permute-start | bytes 196616 | tf_op jit(solution)/shard_map/ppermute | solution.py:235
  72.2 1.9 %collective-permute-start.4 = (f32[16,1024]{1,0:T(8,128)S(1)}, f32[16,1024]{1,0:T(8,128)S(1)}, u32[]{:S(2)}, u32[]{:S(2)}) collective-permute-start(f32[16,1024]{1,0:T(8,128)S(1)} %get-tuple-element.24), channel_id=1, source_target_pairs={{0,1},{1,2},{2,3},{3,4},{4,5},{5,6},{6,7},{7,8},{8,9},{9,10},{10,1... | collective-permute-start | bytes 196616 | tf_op jit(solution)/shard_map/ppermute | solution.py:235
  74.1 0.5 broadcast.8
  74.6 0.0 copy-done.6
  74.6 0.7 reduce.3
  75.3 0.1 reshape.12.visible
  75.4 0.0 all-to-all-done.1.batches
  75.4 2.9 %first_votes.1.tally = f32[9,9,16,1024]{3,2,1,0:T(8,128)S(1)} custom-call(s32[8]{0:T(128)S(1)} %reshape.12.visible, f32[16,8,8,128]{3,2,1,0:T(8,128)S(1)} %all-to-all-done.1.batches), custom_call_target="tpu_custom_call" | custom-call | bytes 12000000 | tf_op jit(solution)/shard_map/first_votes/pallas_call | solution.py:275
  78.3 0.2 collective-permute-done.3.above
  78.5 0.0 collective-permute-done.4.before
  78.5 0.0 copy-done.5
  78.5 1.0 first_update.1
  79.5 2.2 %collective-permute-start.5 = (f32[8,1024]{1,0:T(8,128)S(1)}, f32[8,1024]{1,0:T(8,128)S(1)}, u32[]{:S(2)}, u32[]{:S(2)}) collective-permute-start(f32[8,1024]{1,0:T(8,128)S(1)} %get-tuple-element.31), channel_id=1, source_target_pairs={{1,0},{2,1},{3,2},{4,3},{5,4},{6,5},{7,6},{8,7},{9,8},{10,9},{11,1... | collective-permute-start | bytes 98312 | tf_op jit(solution)/shard_map/ppermute | solution.py:235
  81.8 8.2 %collective-permute-done.5.ahead = f32[8,1024]{1,0:T(8,128)S(1)} collective-permute-done((f32[8,1024]{1,0:T(8,128)S(1)}, f32[8,1024]{1,0:T(8,128)S(1)}, u32[]{:S(2)}, u32[]{:S(2)}) %collective-permute-start.5) | collective-permute-done | bytes 32800 | tf_op jit(solution)/shard_map/ppermute | solution.py:235
  90.0 0.1 top_dual.1.after
  90.1 2.9 %collective-permute-start.6 = (f32[16,1024]{1,0:T(8,128)S(1)}, f32[16,1024]{1,0:T(8,128)S(1)}, u32[]{:S(2)}, u32[]{:S(2)}) collective-permute-start(f32[16,1024]{1,0:T(8,128)S(1)} %top_dual.1.after), channel_id=1, source_target_pairs={{0,16},{16,32},{32,48},{48,64},{64,80},{80,96},{96,112},{112,128},... | collective-permute-start | bytes 196616 | tf_op jit(solution)/shard_map/ppermute | solution.py:235
  93.0 1.7 %second_duals.1 = (f32[3,8,16,1024]{3,2,1,0:T(8,128)}, f32[8,1024]{1,0:T(8,128)S(1)}) custom-call(f32[9,16,1024]{2,1,0:T(8,128)S(1)} %get-tuple-element.30.extra, f32[3,8,16,1024]{3,2,1,0:T(8,128)S(1)} %get-tuple-element.19.dual, f32[8,1024]{1,0:T(8,128)S(1)} %collective-permute-done.5.ahead, f32[16,1024]{1,0:T(8,128)S(1)} %top_dual.1.after), custom_call_target="tpu_custom_call" | custom-call | bytes 3000000 | tf_op jit(solution)/shard_map/second_duals/pallas_call | solution.py:283
  94.7 2.2 %collective-permute-start.7 = (f32[8,1024]{1,0:T(8,128)S(1)}, f32[8,1024]{1,0:T(8,128)S(1)}, u32[]{:S(2)}, u32[]{:S(2)}) collective-permute-start(f32[8,1024]{1,0:T(8,128)S(1)} %get-tuple-element.33), channel_id=1, source_target_pairs={{0,1},{1,2},{2,3},{3,4},{4,5},{5,6},{6,7},{7,8},{8,9},{9,10},{10,1... | collective-permute-start | bytes 98312 | tf_op jit(solution)/shard_map/ppermute | solution.py:235
  96.9 0.0 copy-start
  96.9 1.4 %copy-done = f32[3,8,16,1024]{3,2,1,0:T(8,128)S(1)} copy-done((f32[3,8,16,1024]{3,2,1,0:T(8,128)S(1)}, f32[3,8,16,1024]{3,2,1,0:T(8,128)}, u32[]{:S(2)}) %copy-start) | copy-done | bytes 1572888
  98.3 2.8 %second_votes.1.tally = f32[9,8,16,1024]{3,2,1,0:T(8,128)S(1)} custom-call(s32[8]{0:T(128)S(1)} %reshape.12.visible, f32[16,8,8,128]{3,2,1,0:T(8,128)S(1)} %all-to-all-done.1.batches, f32[9,9,16,1024]{3,2,1,0:T(8,128)S(1)} %first_votes.1.tally, f32[3,8,16,1024]{3,2,1,0:T(8,128)S(1)} %copy-done), custom_call_target="tpu_custom_call" | custom-call | bytes 9000000 | tf_op jit(solution)/shard_map/second_votes/pallas_call | solution.py:285
  101.1 0.0 collective-permute-done.7.before
  101.2 1.5 %last_layers.1.updated_in = f32[8,16,1024]{2,1,0:T(8,128)} custom-call(f32[8,16,1024]{2,1,0:T(8,128)S(1)} %get-tuple-element.29.current, f32[3,8,16,1024]{3,2,1,0:T(8,128)S(1)} %copy-done, f32[8,1024]{1,0:T(8,128)S(1)} %collective-permute-done.7.before, f32[9,8,16,1024]{3,2,1,0:T(8,128)S(1)} %second_votes.1.tally), custom_call_target="tpu_custom_call" | custom-call | bytes 3000000 | tf_op jit(solution)/shard_map/last_layers/pallas_call | solution.py:286
  102.6 4.2 %collective-permute-done.6.above = f32[16,1024]{1,0:T(8,128)S(1)} collective-permute-done((f32[16,1024]{1,0:T(8,128)S(1)}, f32[16,1024]{1,0:T(8,128)S(1)}, u32[]{:S(2)}, u32[]{:S(2)}) %collective-permute-start.6) | collective-permute-done | bytes 65568 | tf_op jit(solution)/shard_map/ppermute | solution.py:235
  106.8 0.8 last_layer.1
  (8 shorter events, 0.1 us)
Async XLA Ops:
  0.6 33.0 %copy-start.7 = (s32[2]{0:T(128)S(1)}, s32[2]{0:T(128)}, u32[]{:S(2)}) copy-start(s32[2]{0:T(128)} %param.8) | copy-start | bytes 28
  0.6 36.2 %all-to-all-start = ((f32[16,8,8,128]{3,2,1,0:T(8,128)}), f32[16,8,8,128]{3,2,1,0:T(8,128)S(1)}, u32[]{:S(2)}, u32[]{:S(2)}) async-start(f32[16,8,8,128]{3,2,1,0:T(8,128)} %bitcast.10), calls=%async_computation | async-start | bytes 1048576 | tf_op jit(solution)/shard_map/all_to_all | solution.py:242
  8.6 6.6 %collective-permute-start = (f32[8,1024]{1,0:T(8,128)S(1)}, f32[8,1024]{1,0:T(8,128)S(1)}, u32[]{:S(2)}, u32[]{:S(2)}) collective-permute-start(f32[8,1024]{1,0:T(8,128)S(1)} %bitcast.11), channel_id=1, source_target_pairs={{1,0},{2,1},{3,2},{4,3},{5,4},{6,5},{7,6},{8,7},{9,8},{10,9},{11,1... | collective-permute-start | bytes 98312 | tf_op jit(solution)/shard_map/ppermute | solution.py:235
  15.1 1.4 %copy-start.1 = (f32[3,8,16,1024]{3,2,1,0:T(8,128)S(1)}, f32[3,8,16,1024]{3,2,1,0:T(8,128)}, u32[]{:S(2)}) copy-start(f32[3,8,16,1024]{3,2,1,0:T(8,128)} %dual.3) | copy-start | bytes 4718596
  16.5 1.0 copy-start.3
  17.6 32.2 %copy-start.2 = (f32[3,8,16,1024]{3,2,1,0:T(8,128)S(1)}, f32[3,8,16,1024]{3,2,1,0:T(8,128)}, u32[]{:S(2)}) copy-start(f32[3,8,16,1024]{3,2,1,0:T(8,128)} %dual.3) | copy-start | bytes 4718596
  17.8 32.0 %collective-permute-start.1 = (f32[40,1024]{1,0:T(8,128)S(1)}, f32[40,1024]{1,0:T(8,128)S(1)}, u32[]{:S(2)}, u32[]{:S(2)}) collective-permute-start(f32[40,1024]{1,0:T(8,128)S(1)} %first_layer.1), channel_id=1, source_target_pairs={{16,0},{32,16},{48,32},{64,48},{80,64},{96,80},{112,96},{128,112},... | collective-permute-start | bytes 491528 | tf_op jit(solution)/shard_map/ppermute | solution.py:235
  36.9 14.5 %collective-permute-start.2 = (f32[8,8,128]{2,1,0:T(8,128)S(1)}, f32[8,8,128]{2,1,0:T(8,128)S(1)}, u32[]{:S(2)}, u32[]{:S(2)}) collective-permute-start(f32[8,8,128]{2,1,0:T(8,128)S(1)} %dynamic-slice_bitcast_fusion), channel_id=1, source_target_pairs={{0,16},{16,0},{32,48},{48,32},{64,80},{80,64},{96,112},{112,96},{1... | collective-permute-start | bytes 98312 | tf_op jit(solution)/shard_map/ppermute | solution.py:264
  49.8 1.0 copy-start.4
  50.8 23.8 %copy-start.6 = (s32[2,4,1]{1,2,0:T(1,128)S(1)}, s32[2,4,1]{1,2,0:T(1,128)}, u32[]{:S(2)}) copy-start(s32[2,4,1]{1,2,0:T(1,128)} %param.9) | copy-start | bytes 100
  52.3 23.1 %all-to-all-start.1 = ((f32[16,8,8,128]{3,2,1,0:T(8,128)}), f32[16,8,8,128]{3,2,1,0:T(8,128)S(1)}, u32[]{:S(2)}, u32[]{:S(2)}) async-start(f32[16,8,8,128]{3,2,1,0:T(8,128)} %broadcast_in_dim.2), calls=%async_computation.1 | async-start | bytes 1048576 | tf_op jit(solution)/shard_map/all_to_all | solution.py:242
  56.5 22.0 %collective-permute-start.3 = (f32[16,1024]{1,0:T(8,128)S(1)}, f32[16,1024]{1,0:T(8,128)S(1)}, u32[]{:S(2)}, u32[]{:S(2)}) collective-permute-start(f32[16,1024]{1,0:T(8,128)S(1)} %get-tuple-element.23), channel_id=1, source_target_pairs={{0,16},{16,32},{32,48},{48,64},{64,80},{80,96},{96,112},{112,128},... | collective-permute-start | bytes 196616 | tf_op jit(solution)/shard_map/ppermute | solution.py:235
  72.2 6.3 %collective-permute-start.4 = (f32[16,1024]{1,0:T(8,128)S(1)}, f32[16,1024]{1,0:T(8,128)S(1)}, u32[]{:S(2)}, u32[]{:S(2)}) collective-permute-start(f32[16,1024]{1,0:T(8,128)S(1)} %get-tuple-element.24), channel_id=1, source_target_pairs={{0,1},{1,2},{2,3},{3,4},{4,5},{5,6},{6,7},{7,8},{8,9},{9,10},{10,1... | collective-permute-start | bytes 196616 | tf_op jit(solution)/shard_map/ppermute | solution.py:235
  75.4 3.1 %copy-start.5 = (f32[8,16,1024]{2,1,0:T(8,128)S(1)}, f32[8,16,1024]{2,1,0:T(8,128)}, u32[]{:S(2)}) copy-start(f32[8,16,1024]{2,1,0:T(8,128)} %field.5) | copy-start | bytes 1572868
  79.5 10.5 %collective-permute-start.5 = (f32[8,1024]{1,0:T(8,128)S(1)}, f32[8,1024]{1,0:T(8,128)S(1)}, u32[]{:S(2)}, u32[]{:S(2)}) collective-permute-start(f32[8,1024]{1,0:T(8,128)S(1)} %get-tuple-element.31), channel_id=1, source_target_pairs={{1,0},{2,1},{3,2},{4,3},{5,4},{6,5},{7,6},{8,7},{9,8},{10,9},{11,1... | collective-permute-start | bytes 98312 | tf_op jit(solution)/shard_map/ppermute | solution.py:235
  90.1 16.7 %collective-permute-start.6 = (f32[16,1024]{1,0:T(8,128)S(1)}, f32[16,1024]{1,0:T(8,128)S(1)}, u32[]{:S(2)}, u32[]{:S(2)}) collective-permute-start(f32[16,1024]{1,0:T(8,128)S(1)} %top_dual.1.after), channel_id=1, source_target_pairs={{0,16},{16,32},{32,48},{48,64},{64,80},{80,96},{96,112},{112,128},... | collective-permute-start | bytes 196616 | tf_op jit(solution)/shard_map/ppermute | solution.py:235
  94.7 6.5 %collective-permute-start.7 = (f32[8,1024]{1,0:T(8,128)S(1)}, f32[8,1024]{1,0:T(8,128)S(1)}, u32[]{:S(2)}, u32[]{:S(2)}) collective-permute-start(f32[8,1024]{1,0:T(8,128)S(1)} %get-tuple-element.33), channel_id=1, source_target_pairs={{0,1},{1,2},{2,3},{3,4},{4,5},{5,6},{6,7},{7,8},{8,9},{9,10},{10,1... | collective-permute-start | bytes 98312 | tf_op jit(solution)/shard_map/ppermute | solution.py:235
  96.9 1.4 %copy-start = (f32[3,8,16,1024]{3,2,1,0:T(8,128)S(1)}, f32[3,8,16,1024]{3,2,1,0:T(8,128)}, u32[]{:S(2)}) copy-start(f32[3,8,16,1024]{3,2,1,0:T(8,128)} %get-tuple-element.18.after.dual) | copy-start | bytes 4718596

commit v4 on v3

--- a/solution.py
+++ b/solution.py
@@ -32,6 +32,7 @@
 
 VMEM = pl.BlockSpec(memory_space=pltpu.VMEM)
 SMEM = pl.BlockSpec(memory_space=pltpu.SMEM)
+HBM = pl.BlockSpec(memory_space=pltpu.HBM)
 ANY = pl.BlockSpec(memory_space=pl.ANY)
 
 
@@ -47,15 +48,23 @@
     return jnp.broadcast_to(row, (ROWS, LANES))
 
 
-def dual_layer(here, ahead_z, ahead_row, dual_z, dual_x, dual_y, z_end):
+def ends():
     row, lane = row_ids(), lane_ids()
-    x_end = (row == ROWS - 1) & (lax.axis_index("tile") == X_LAST)
-    y_end = lane == LANES - 1
+    return row, (row == ROWS - 1) & (lax.axis_index("tile") == X_LAST), lane == LANES - 1
+
+
+def moved_sides(here, ahead_row, dual_x, dual_y):
+    row, x_end, y_end = ends()
     ahead_x = jnp.where(row == ROWS - 1, spread_row(ahead_row), pltpu.roll(here, ROWS - 1, 0))
     ahead_y = pltpu.roll(here, LANES - 1, 1)
+    moved_x = dual_x + 0.25 * jnp.where(x_end, 0.0, ahead_x - here)
+    return moved_x, dual_y + 0.25 * jnp.where(y_end, 0.0, ahead_y - here)
+
+
+def dual_layer(here, ahead_z, ahead_row, dual_z, dual_x, dual_y, z_end):
+    _, x_end, y_end = ends()
     moved_z = dual_z + 0.25 * jnp.where(z_end, 0.0, ahead_z - here)
-    moved_x = dual_x + 0.25 * jnp.where(x_end, 0.0, ahead_x - here)
-    moved_y = dual_y + 0.25 * jnp.where(y_end, 0.0, ahead_y - here)
+    moved_x, moved_y = moved_sides(here, ahead_row, dual_x, dual_y)
     norm = moved_z * moved_z + moved_x * moved_x + moved_y * moved_y
     scale = 1.0 / jnp.sqrt(jnp.maximum(norm, 1.0))
     return (
@@ -70,15 +79,46 @@
     return (dual_x - before) + (dual_y - pltpu.roll(dual_y, 1, 1))
 
 
-def first_layer(field, dual, ahead, message):
-    here = field[0]
-    dual_z, dual_x, dual_y = dual_layer(here, field[1], ahead[0:1, :], dual[0, 0], dual[1, 0], dual[2, 0], False)
-    message[0:16, :] = here
-    message[16:32, :] = here + 0.25 * (dual_z + flux(dual_x, dual_y, jnp.zeros((1, LANES), jnp.float32)))
-    message[32:40, :] = dual_x[8:16, :]
-
-
-def all_duals(field, dual, ahead, below, new_dual, top, side):
+def pick(owner, spread, kept):
+    kept[...] = spread[lax.shift_right_logical(owner[lax.shift_right_logical(lax.axis_index("slab"), 4)], 1)]
+
+
+def copies_of(owner, kept, across, copies):
+    slab = lax.axis_index("slab")
+    here = (owner[lax.shift_right_logical(slab, 4)] & 1) == (slab & 1)
+    piece = jnp.where(here, kept[...], across[...])
+    for place in range(16):
+        copies[place] = piece
+
+
+def end_layers(field, dual, ahead, down, up, layers, duals, sems):
+    copies = [
+        pltpu.make_async_copy(field.at[0:2], layers.at[0:2], sems.at[0]),
+        pltpu.make_async_copy(dual.at[:, 0], duals.at[0], sems.at[1]),
+        pltpu.make_async_copy(field.at[LAYERS - 1], layers.at[2], sems.at[2]),
+        pltpu.make_async_copy(dual.at[:, LAYERS - 1], duals.at[1], sems.at[3]),
+    ]
+    for copy in copies:
+        copy.start()
+    for copy in copies:
+        copy.wait()
+    here = layers[0]
+    dual_z, dual_x, dual_y = dual_layer(here, layers[1], ahead[0:1, :], duals[0, 0], duals[0, 1], duals[0, 2], False)
+    down[0:16, :] = here
+    down[16:32, :] = here + 0.25 * (dual_z + flux(dual_x, dual_y, jnp.zeros((1, LANES), jnp.float32)))
+    down[32:40, :] = dual_x[8:16, :]
+    moved_x, moved_y = moved_sides(layers[2], ahead[7:8, :], duals[1, 1], duals[1, 2])
+    up[0:16, :] = duals[1, 0] - 0.25 * layers[2]
+    up[16:32, :] = moved_x * moved_x + moved_y * moved_y
+
+
+def top_of(up, here):
+    moved = up[0:16, :] + 0.25 * here
+    scale = 1.0 / jnp.sqrt(jnp.maximum(moved * moved + up[16:32, :], 1.0))
+    return jnp.where(lax.axis_index("slab") == 0, 0.0, moved * scale)
+
+
+def all_duals(field, dual, ahead, below, up, new_dual, top, side):
     slab_end = lax.axis_index("slab") == Z_LAST
     for layer in range(LAYERS):
         last = layer == LAYERS - 1
@@ -95,8 +135,7 @@
         new_dual[1, layer] = dual_x
         new_dual[2, layer] = dual_y
         side[layer : layer + 1, :] = dual_x[15:16, :]
-        if last:
-            top[...] = dual_z
+    top[...] = top_of(up, field[0])
     side[8:16, :] = jnp.zeros((8, LANES), jnp.float32)
     side[8:9, :] = below[39:40, :]
 
@@ -139,7 +178,7 @@
 
 def first_votes(visible, batches, tally):
     base = slab_base()
-    caps = [STEP * visible[view].astype(jnp.float32) for view in range(VIEWS)]
+    caps = [STEP * visible[0, view, 0].astype(jnp.float32) for view in range(VIEWS)]
 
     def body(index, carry):
         half, column, rows, lanes = block_of(index)
@@ -155,7 +194,7 @@
 
 def second_votes(visible, batches, tally, after, new_tally):
     base = slab_base()
-    caps = [STEP * visible[VIEWS + view].astype(jnp.float32) for view in range(VIEWS)]
+    caps = [STEP * visible[1, view, 0].astype(jnp.float32) for view in range(VIEWS)]
 
     def body(index, carry):
         half, column, rows, lanes = block_of(index)
@@ -243,37 +282,40 @@
 
 
 def per_device(field, dual, depth, owner, visible):
-    slab = lax.axis_index("slab")
-    seen = visible.reshape(ITERS * VIEWS)
     block = (LAYERS, ROWS, LANES)
 
     first_one = pl.BlockSpec((1, ROWS, LANES), lambda step: (0, 0, 0))
     first_one_dual = pl.BlockSpec((3, 1, ROWS, LANES), lambda step: (0, 0, 0, 0))
     tally_one = pl.BlockSpec((BINS + 1, 1, ROWS, LANES), lambda step: (0, 0, 0, 0))
-    first = pl.BlockSpec((2, ROWS, LANES), lambda step: (0, 0, 0))
 
     pieces = depth.reshape(16, 8, 8, 128).transpose(0, 2, 1, 3)
     spread = exchange(pieces)
 
     ahead = passed_along(field[:, 0], "tile", -1)
-    (message,) = call(first_layer, [(40, LANES)], 1, [first, first_one_dual, VMEM], grid=(1,))(field, dual, ahead)
-
-    root = owner[slab // 16]
-    kept = lax.dynamic_index_in_dim(spread, root // 2, 0, keepdims=False)
-    kept, _ = lax.optimization_barrier((kept, message))
+    down, up = call(
+        end_layers, [(40, LANES), (32, LANES)], 1, [HBM, HBM, VMEM],
+        scratch_shapes=[
+            pltpu.VMEM((3, ROWS, LANES), jnp.float32),
+            pltpu.VMEM((2, 3, ROWS, LANES), jnp.float32),
+            pltpu.SemaphoreType.DMA((4,)),
+        ],
+    )(pltpu.with_memory_space_constraint(field, pltpu.HBM), pltpu.with_memory_space_constraint(dual, pltpu.HBM), ahead)
+    (kept,) = call(pick, [(8, 8, 128)], 1, [SMEM, VMEM])(owner, spread)
+    kept, _ = lax.optimization_barrier((kept, down))
     across = lax.ppermute(kept, "slab", [(index, index ^ 1) for index in range(32)])
-    below = passed_along(message, "slab", -1)
-    dual, top, side = call(all_duals, [(3,) + block, (ROWS, LANES), (ROWS, LANES)], 1, [VMEM] * 4)(
-        field, dual, ahead, below
-    )
-    across, top, side = lax.optimization_barrier((across, top, side))
-    kept = jnp.where(root % 2 == slab % 2, kept, across)
-    batches = exchange(jnp.broadcast_to(kept[None], pieces.shape))
+    below = passed_along(down, "slab", -1)
+    above = passed_along(up, "slab", 1)
+    across, below, above = lax.optimization_barrier((across, below, above))
+    (copies,) = call(copies_of, [pieces.shape], 1, [SMEM, VMEM, VMEM])(owner, kept, across)
+    batches = exchange(copies)
+    below, _ = lax.optimization_barrier((below, copies))
+    dual, above, side = call(all_duals, [(3,) + block, (ROWS, LANES), (ROWS, LANES)], 1, [VMEM] * 5)(
+        field, dual, ahead, below, above
+    )
     before = passed_along(side, "tile", 1)
-    above = passed_along(top, "slab", 1)
-
-    (tally,) = call(first_votes, [(BINS + 1, LAYERS + 1, ROWS, LANES)], 4, [SMEM, VMEM])(seen, batches)
-    above, before, tally = lax.optimization_barrier((above, before, tally))
+
+    (tally,) = call(first_votes, [(BINS + 1, LAYERS + 1, ROWS, LANES)], 4, [SMEM, VMEM])(visible, batches)
+    before, tally = lax.optimization_barrier((before, tally))
     current, extra, side = call(first_update, [block, (LAYERS + 1, ROWS, LANES), (LAYERS, LANES)], 1, [VMEM] * 6)(
         field, dual, above, before, below, tally
     )
@@ -282,7 +324,7 @@
     above = passed_along(top, "slab", 1)
     dual, side = call(second_duals, [(3,) + block, (LAYERS, LANES)], 1, [VMEM] * 3 + [ANY])(extra, dual, ahead, top)
     before = passed_along(side, "tile", 1)
-    (tally,) = call(second_votes, [(BINS + 1,) + block], 3, [SMEM, VMEM, VMEM, ANY])(seen, batches, tally, dual)
+    (tally,) = call(second_votes, [(BINS + 1,) + block], 3, [SMEM, VMEM, VMEM, ANY])(visible, batches, tally, side)
     (rest,) = call(last_layers, [block], 1, [VMEM] * 4)(current, dual, before, tally)
     above, rest = lax.optimization_barrier((above, rest))
     (current,) = call(

time: 108 us -> 112 us (1.037)
  the two profiles are of different devices: /device:TPU:35 before, /device:TPU:3 now
where the time goes in v4:
time: 112 us
  starting transfers between devices  63 us (56%)
  waiting for transfers between devices  29.2 us (26%)
  Pallas kernels  16.3 us (15%)
  local copies, waits for them, and re-layouts  2.16 us (2%)
    ppermute x7, starting transfers between devices, passed_along(): lax.ppermute(value, axis, [(source, source + steps) for source in range(f...  38.6 us
    ppermute x7, waiting for transfers between devices, passed_along(): lax.ppermute(value, axis, [(source, source + steps) for source in range(f...  24.7 us
    all_to_all x2, starting transfers between devices, exchange(): return lax.all_to_all(pieces, 'slab', 0, 0, axis_index_groups=GROUPS)  13.5 us
    ppermute x1, starting transfers between devices, per_device(): lax.ppermute(kept, 'slab', [(index, index ^ 1) for index in range(32)])  10.9 us
    all_to_all x2, waiting for transfers between devices, exchange(): return lax.all_to_all(pieces, 'slab', 0, 0, axis_index_groups=GROUPS)  4.58 us
    pallas_call x1, Pallas kernels, per_device(): call(first_votes, [(BINS + 1, LAYERS + 1, ROWS, LANES)], 4, [SMEM, VMEM])  3.43 us
    pallas_call x1, Pallas kernels, per_device(): call(second_votes, [(BINS + 1,) + block], 3, [SMEM, VMEM, VMEM, ANY])  3.36 us
  transfers between devices with their start and end apart: 10, of which 5 were waited for; matrix products, arithmetic and copies ran while one was open for 1% of the time, Pallas kernels for 12%

profile of v4, /device:TPU:3, one launch (start us, length us, event | category | flops | bytes accessed | tf_op | source)
XLA Modules:
  0.0 111.5 jit_solution(3293357930616708995)
XLA Ops:
  0.6 0.0 copy-start.4
  0.6 6.9 %all-to-all-start = ((f32[16,8,8,128]{3,2,1,0:T(8,128)}), f32[16,8,8,128]{3,2,1,0:T(8,128)S(1)}, u32[]{:S(2)}, u32[]{:S(2)}) async-start(f32[16,8,8,128]{3,2,1,0:T(8,128)} %bitcast.6), calls=%async_computation | async-start | bytes 1048576 | tf_op jit(solution)/shard_map/all_to_all | solution.py:281
  7.6 1.0 slice.9
  8.6 5.0 %collective-permute-start = (f32[8,1024]{1,0:T(8,128)S(1)}, f32[8,1024]{1,0:T(8,128)S(1)}, u32[]{:S(2)}, u32[]{:S(2)}) collective-permute-start(f32[8,1024]{1,0:T(8,128)S(1)} %bitcast.7), channel_id=1, source_target_pairs={{1,0},{2,1},{3,2},{4,3},{5,4},{6,5},{7,6},{8,7},{9,8},{10,9},{11,1... | collective-permute-start | bytes 98312 | tf_op jit(solution)/shard_map/ppermute | solution.py:274
  13.5 1.6 %collective-permute-done.ahead = f32[8,1024]{1,0:T(8,128)S(1)} collective-permute-done((f32[8,1024]{1,0:T(8,128)S(1)}, f32[8,1024]{1,0:T(8,128)S(1)}, u32[]{:S(2)}, u32[]{:S(2)}) %collective-permute-start) | collective-permute-done | bytes 32800 | tf_op jit(solution)/shard_map/ppermute | solution.py:274
  15.1 1.4 %end_layers.1 = (f32[40,1024]{1,0:T(8,128)S(1)}, f32[32,1024]{1,0:T(8,128)S(1)}) custom-call(f32[8,16,1024]{2,1,0:T(8,128)} %field.5, f32[3,8,16,1024]{3,2,1,0:T(8,128)} %dual.3, f32[8,1024]{1,0:T(8,128)S(1)} %collective-permute-done.ahead), custom_call_target="tpu_custom_call" | custom-call | bytes 3000000 | tf_op jit(solution)/shard_map/end_layers/pallas_call | solution.py:295
  16.5 0.0 copy-start
  16.5 16.8 %collective-permute-start.2 = (f32[40,1024]{1,0:T(8,128)S(1)}, f32[40,1024]{1,0:T(8,128)S(1)}, u32[]{:S(2)}, u32[]{:S(2)}) collective-permute-start(f32[40,1024]{1,0:T(8,128)S(1)} %get-tuple-element.21), channel_id=1, source_target_pairs={{16,0},{32,16},{48,32},{64,48},{80,64},{96,80},{112,96},{128,112},... | collective-permute-start | bytes 491528 | tf_op jit(solution)/shard_map/ppermute | solution.py:274
  33.3 1.9 %collective-permute-start.3 = (f32[32,1024]{1,0:T(8,128)S(1)}, f32[32,1024]{1,0:T(8,128)S(1)}, u32[]{:S(2)}, u32[]{:S(2)}) collective-permute-start(f32[32,1024]{1,0:T(8,128)S(1)} %get-tuple-element.23), channel_id=1, source_target_pairs={{0,16},{16,32},{32,48},{48,64},{64,80},{80,96},{96,112},{112,128},... | collective-permute-start | bytes 393224 | tf_op jit(solution)/shard_map/ppermute | solution.py:274
  35.2 0.0 all-to-all-done.spread
  35.2 0.0 copy-done.4
  35.2 0.6 pick.1.kept
  35.8 10.9 %collective-permute-start.1 = (f32[8,8,128]{2,1,0:T(8,128)S(1)}, f32[8,8,128]{2,1,0:T(8,128)S(1)}, u32[]{:S(2)}, u32[]{:S(2)}) collective-permute-start(f32[8,8,128]{2,1,0:T(8,128)S(1)} %pick.1.kept), channel_id=1, source_target_pairs={{0,16},{16,0},{32,48},{48,32},{64,80},{80,64},{96,112},{112,96},{1... | collective-permute-start | bytes 98312 | tf_op jit(solution)/shard_map/ppermute | solution.py:305
  46.7 18.8 %collective-permute-done.3.up = f32[32,1024]{1,0:T(8,128)S(1)} collective-permute-done((f32[32,1024]{1,0:T(8,128)S(1)}, f32[32,1024]{1,0:T(8,128)S(1)}, u32[]{:S(2)}, u32[]{:S(2)}) %collective-permute-start.3) | collective-permute-done | bytes 131104 | tf_op jit(solution)/shard_map/ppermute | solution.py:274
  65.5 0.0 collective-permute-done.2.below
  65.5 0.0 collective-permute-done.1.across
  65.5 1.4 %copies_of.1 = f32[16,8,8,128]{3,2,1,0:T(8,128)} custom-call(s32[2]{0:T(128)S(1)} %copy-done.4, f32[8,8,128]{2,1,0:T(8,128)S(1)} %pick.1.kept, f32[8,8,128]{2,1,0:T(8,128)S(1)} %collective-permute-done.1.across), custom_call_target="tpu_custom_call" | custom-call | bytes 3000000 | tf_op jit(solution)/shard_map/copies_of/pallas_call | solution.py:309
  66.9 0.0 copy-start.5
  66.9 6.6 %all-to-all-start.1 = ((f32[16,8,8,128]{3,2,1,0:T(8,128)}), f32[16,8,8,128]{3,2,1,0:T(8,128)}, u32[]{:S(2)}, u32[]{:S(2)}) async-start(f32[16,8,8,128]{3,2,1,0:T(8,128)} %copies_of.1), calls=%async_computation.1 | async-start | bytes 1048576 | tf_op jit(solution)/shard_map/all_to_all | solution.py:281
  73.5 0.0 copy-done
  73.5 0.0 copy-start.2
  73.5 1.0 copy-done.2
  74.5 1.2 %all_duals.1 = (f32[3,8,16,1024]{3,2,1,0:T(8,128)S(1)}, f32[16,1024]{1,0:T(8,128)S(1)}, f32[16,1024]{1,0:T(8,128)}) custom-call(f32[8,16,1024]{2,1,0:T(8,128)S(1)} %copy-done.2, f32[3,8,16,1024]{3,2,1,0:T(8,128)S(1)} %copy-done, f32[8,1024]{1,0:T(8,128)S(1)} %collective-permute-done.ahead, f32[40,1024]{1,0:T(8,128)S(1)} %collective-permute-done.2.below, ...), custom_call_target="tpu_custom_call" | custom-call | bytes 3000000 | tf_op jit(solution)/shard_map/all_duals/pallas_call | solution.py:312
  75.8 1.9 %collective-permute-start.4 = (f32[16,1024]{1,0:T(8,128)}, f32[16,1024]{1,0:T(8,128)S(1)}, u32[]{:S(2)}, u32[]{:S(2)}) collective-permute-start(f32[16,1024]{1,0:T(8,128)} %get-tuple-element.30), channel_id=1, source_target_pairs={{0,1},{1,2},{2,3},{3,4},{4,5},{5,6},{6,7},{7,8},{8,9},{9,10},{10,1... | collective-permute-start | bytes 196616 | tf_op jit(solution)/shard_map/ppermute | solution.py:274
  77.7 0.0 copy-done.5
  77.7 0.1 copy.9.visible
  77.8 0.0 copy-start.3
  77.8 4.6 %all-to-all-done.1.batches = f32[16,8,8,128]{3,2,1,0:T(8,128)} async-done(((f32[16,8,8,128]{3,2,1,0:T(8,128)}), f32[16,8,8,128]{3,2,1,0:T(8,128)}, u32[]{:S(2)}, u32[]{:S(2)}) %all-to-all-start.1) | async-done | bytes 524320 | tf_op jit(solution)/shard_map/all_to_all | solution.py:281
  82.4 3.4 %first_votes.1.tally = f32[9,9,16,1024]{3,2,1,0:T(8,128)S(1)} custom-call(s32[2,4,1]{2,1,0:T(4,128)S(1)} %copy.9.visible, f32[16,8,8,128]{3,2,1,0:T(8,128)} %all-to-all-done.1.batches), custom_call_target="tpu_custom_call" | custom-call | bytes 12000000 | tf_op jit(solution)/shard_map/first_votes/pallas_call | solution.py:317
  85.8 0.0 collective-permute-done.4.before
  85.8 0.0 copy-done.3
  85.8 0.9 first_update.1
  86.7 3.6 %collective-permute-start.5 = (f32[8,1024]{1,0:T(8,128)S(1)}, f32[8,1024]{1,0:T(8,128)S(1)}, u32[]{:S(2)}, u32[]{:S(2)}) collective-permute-start(f32[8,1024]{1,0:T(8,128)S(1)} %get-tuple-element.35), channel_id=1, source_target_pairs={{1,0},{2,1},{3,2},{4,3},{5,4},{6,5},{7,6},{8,7},{9,8},{10,9},{11,1... | collective-permute-start | bytes 98312 | tf_op jit(solution)/shard_map/ppermute | solution.py:274
  90.4 1.6 %collective-permute-done.5.ahead = f32[8,1024]{1,0:T(8,128)S(1)} collective-permute-done((f32[8,1024]{1,0:T(8,128)S(1)}, f32[8,1024]{1,0:T(8,128)S(1)}, u32[]{:S(2)}, u32[]{:S(2)}) %collective-permute-start.5) | collective-permute-done | bytes 32800 | tf_op jit(solution)/shard_map/ppermute | solution.py:274
  91.9 0.1 top_dual.1.after
  92.1 7.1 %collective-permute-start.6 = (f32[16,1024]{1,0:T(8,128)S(1)}, f32[16,1024]{1,0:T(8,128)S(1)}, u32[]{:S(2)}, u32[]{:S(2)}) collective-permute-start(f32[16,1024]{1,0:T(8,128)S(1)} %top_dual.1.after), channel_id=1, source_target_pairs={{0,16},{16,32},{32,48},{48,64},{64,80},{80,96},{96,112},{112,128},... | collective-permute-start | bytes 196616 | tf_op jit(solution)/shard_map/ppermute | solution.py:274
  99.2 1.7 %second_duals.1 = (f32[3,8,16,1024]{3,2,1,0:T(8,128)}, f32[8,1024]{1,0:T(8,128)S(1)}) custom-call(f32[9,16,1024]{2,1,0:T(8,128)S(1)} %get-tuple-element.34.extra, f32[3,8,16,1024]{3,2,1,0:T(8,128)S(1)} %get-tuple-element.28.dual, f32[8,1024]{1,0:T(8,128)S(1)} %collective-permute-done.5.ahead, f32[16,1024]{1,0:T(8,128)S(1)} %top_dual.1.after), custom_call_target="tpu_custom_call" | custom-call | bytes 3000000 | tf_op jit(solution)/shard_map/second_duals/pallas_call | solution.py:325
  100.9 0.0 copy-start.1
  100.9 2.3 %collective-permute-start.7 = (f32[8,1024]{1,0:T(8,128)S(1)}, f32[8,1024]{1,0:T(8,128)S(1)}, u32[]{:S(2)}, u32[]{:S(2)}) collective-permute-start(f32[8,1024]{1,0:T(8,128)S(1)} %get-tuple-element.37.after), channel_id=1, source_target_pairs={{0,1},{1,2},{2,3},{3,4},{4,5},{5,6},{6,7},{7,8},{8,9},{9,10},{10,1... | collective-permute-start | bytes 98312 | tf_op jit(solution)/shard_map/ppermute | solution.py:274
  103.2 3.4 %second_votes.1.tally = f32[9,8,16,1024]{3,2,1,0:T(8,128)S(1)} custom-call(s32[2,4,1]{2,1,0:T(4,128)S(1)} %copy.9.visible, f32[16,8,8,128]{3,2,1,0:T(8,128)} %all-to-all-done.1.batches, f32[9,9,16,1024]{3,2,1,0:T(8,128)S(1)} %first_votes.1.tally, f32[8,1024]{1,0:T(8,128)S(1)} %get-tuple-element.37.after), custom_call_target="tpu_custom_call" | custom-call | bytes 9000000 | tf_op jit(solution)/shard_map/second_votes/pallas_call | solution.py:327
  106.6 0.0 collective-permute-done.7.before
  106.6 0.0 copy-done.1
  106.6 1.4 %last_layers.1.updated_in = f32[8,16,1024]{2,1,0:T(8,128)} custom-call(f32[8,16,1024]{2,1,0:T(8,128)S(1)} %get-tuple-element.33.current, f32[3,8,16,1024]{3,2,1,0:T(8,128)S(1)} %copy-done.1, f32[8,1024]{1,0:T(8,128)S(1)} %collective-permute-done.7.before, f32[9,8,16,1024]{3,2,1,0:T(8,128)S(1)} %second_votes.1.tally), custom_call_target="tpu_custom_call" | custom-call | bytes 3000000 | tf_op jit(solution)/shard_map/last_layers/pallas_call | solution.py:328
  108.0 2.7 %collective-permute-done.6.above = f32[16,1024]{1,0:T(8,128)S(1)} collective-permute-done((f32[16,1024]{1,0:T(8,128)S(1)}, f32[16,1024]{1,0:T(8,128)S(1)}, u32[]{:S(2)}, u32[]{:S(2)}) %collective-permute-start.6) | collective-permute-done | bytes 65568 | tf_op jit(solution)/shard_map/ppermute | solution.py:274
  110.7 0.8 last_layer.1
  (3 shorter events, 0.0 us)
Async XLA Ops:
  0.6 34.6 %copy-start.4 = (s32[2]{0:T(128)S(1)}, s32[2]{0:T(128)}, u32[]{:S(2)}) copy-start(s32[2]{0:T(128)} %owner.3) | copy-start | bytes 28
  0.6 34.6 %all-to-all-start = ((f32[16,8,8,128]{3,2,1,0:T(8,128)}), f32[16,8,8,128]{3,2,1,0:T(8,128)S(1)}, u32[]{:S(2)}, u32[]{:S(2)}) async-start(f32[16,8,8,128]{3,2,1,0:T(8,128)} %bitcast.6), calls=%async_computation | async-start | bytes 1048576 | tf_op jit(solution)/shard_map/all_to_all | solution.py:281
  8.6 6.6 %collective-permute-start = (f32[8,1024]{1,0:T(8,128)S(1)}, f32[8,1024]{1,0:T(8,128)S(1)}, u32[]{:S(2)}, u32[]{:S(2)}) collective-permute-start(f32[8,1024]{1,0:T(8,128)S(1)} %bitcast.7), channel_id=1, source_target_pairs={{1,0},{2,1},{3,2},{4,3},{5,4},{6,5},{7,6},{8,7},{9,8},{10,9},{11,1... | collective-permute-start | bytes 98312 | tf_op jit(solution)/shard_map/ppermute | solution.py:274
  16.5 57.0 %copy-start = (f32[3,8,16,1024]{3,2,1,0:T(8,128)S(1)}, f32[3,8,16,1024]{3,2,1,0:T(8,128)}, u32[]{:S(2)}) copy-start(f32[3,8,16,1024]{3,2,1,0:T(8,128)} %dual.3) | copy-start | bytes 4718596
  16.5 49.0 %collective-permute-start.2 = (f32[40,1024]{1,0:T(8,128)S(1)}, f32[40,1024]{1,0:T(8,128)S(1)}, u32[]{:S(2)}, u32[]{:S(2)}) collective-permute-start(f32[40,1024]{1,0:T(8,128)S(1)} %get-tuple-element.21), channel_id=1, source_target_pairs={{16,0},{32,16},{48,32},{64,48},{80,64},{96,80},{112,96},{128,112},... | collective-permute-start | bytes 491528 | tf_op jit(solution)/shard_map/ppermute | solution.py:274
  33.3 32.2 %collective-permute-start.3 = (f32[32,1024]{1,0:T(8,128)S(1)}, f32[32,1024]{1,0:T(8,128)S(1)}, u32[]{:S(2)}, u32[]{:S(2)}) collective-permute-start(f32[32,1024]{1,0:T(8,128)S(1)} %get-tuple-element.23), channel_id=1, source_target_pairs={{0,16},{16,32},{32,48},{48,64},{64,80},{80,96},{96,112},{112,128},... | collective-permute-start | bytes 393224 | tf_op jit(solution)/shard_map/ppermute | solution.py:274
  35.8 29.7 %collective-permute-start.1 = (f32[8,8,128]{2,1,0:T(8,128)S(1)}, f32[8,8,128]{2,1,0:T(8,128)S(1)}, u32[]{:S(2)}, u32[]{:S(2)}) collective-permute-start(f32[8,8,128]{2,1,0:T(8,128)S(1)} %pick.1.kept), channel_id=1, source_target_pairs={{0,16},{16,0},{32,48},{48,32},{64,80},{80,64},{96,112},{112,96},{1... | collective-permute-start | bytes 98312 | tf_op jit(solution)/shard_map/ppermute | solution.py:305
  66.9 10.8 %copy-start.5 = (s32[2,4,1]{1,2,0:T(1,128)S(1)}, s32[2,4,1]{1,2,0:T(1,128)}, u32[]{:S(2)}) copy-start(s32[2,4,1]{1,2,0:T(1,128)} %param.9) | copy-start | bytes 100
  66.9 15.5 %all-to-all-start.1 = ((f32[16,8,8,128]{3,2,1,0:T(8,128)}), f32[16,8,8,128]{3,2,1,0:T(8,128)}, u32[]{:S(2)}, u32[]{:S(2)}) async-start(f32[16,8,8,128]{3,2,1,0:T(8,128)} %copies_of.1), calls=%async_computation.1 | async-start | bytes 1048576 | tf_op jit(solution)/shard_map/all_to_all | solution.py:281
  73.5 1.0 copy-start.2
  75.8 10.0 %collective-permute-start.4 = (f32[16,1024]{1,0:T(8,128)}, f32[16,1024]{1,0:T(8,128)S(1)}, u32[]{:S(2)}, u32[]{:S(2)}) collective-permute-start(f32[16,1024]{1,0:T(8,128)} %get-tuple-element.30), channel_id=1, source_target_pairs={{0,1},{1,2},{2,3},{3,4},{4,5},{5,6},{6,7},{7,8},{8,9},{9,10},{10,1... | collective-permute-start | bytes 196616 | tf_op jit(solution)/shard_map/ppermute | solution.py:274
  77.8 8.0 %copy-start.3 = (f32[8,16,1024]{2,1,0:T(8,128)S(1)}, f32[8,16,1024]{2,1,0:T(8,128)}, u32[]{:S(2)}) copy-start(f32[8,16,1024]{2,1,0:T(8,128)} %field.5) | copy-start | bytes 1572868
  86.7 5.2 %collective-permute-start.5 = (f32[8,1024]{1,0:T(8,128)S(1)}, f32[8,1024]{1,0:T(8,128)S(1)}, u32[]{:S(2)}, u32[]{:S(2)}) collective-permute-start(f32[8,1024]{1,0:T(8,128)S(1)} %get-tuple-element.35), channel_id=1, source_target_pairs={{1,0},{2,1},{3,2},{4,3},{5,4},{6,5},{7,6},{8,7},{9,8},{10,9},{11,1... | collective-permute-start | bytes 98312 | tf_op jit(solution)/shard_map/ppermute | solution.py:274
  92.1 18.7 %collective-permute-start.6 = (f32[16,1024]{1,0:T(8,128)S(1)}, f32[16,1024]{1,0:T(8,128)S(1)}, u32[]{:S(2)}, u32[]{:S(2)}) collective-permute-start(f32[16,1024]{1,0:T(8,128)S(1)} %top_dual.1.after), channel_id=1, source_target_pairs={{0,16},{16,32},{32,48},{48,64},{64,80},{80,96},{96,112},{112,128},... | collective-permute-start | bytes 196616 | tf_op jit(solution)/shard_map/ppermute | solution.py:274
  100.9 5.7 %copy-start.1 = (f32[3,8,16,1024]{3,2,1,0:T(8,128)S(1)}, f32[3,8,16,1024]{3,2,1,0:T(8,128)}, u32[]{:S(2)}) copy-start(f32[3,8,16,1024]{3,2,1,0:T(8,128)} %get-tuple-element.20.dual) | copy-start | bytes 4718596
  100.9 5.7 %collective-permute-start.7 = (f32[8,1024]{1,0:T(8,128)S(1)}, f32[8,1024]{1,0:T(8,128)S(1)}, u32[]{:S(2)}, u32[]{:S(2)}) collective-permute-start(f32[8,1024]{1,0:T(8,128)S(1)} %get-tuple-element.37.after), channel_id=1, source_target_pairs={{0,1},{1,2},{2,3},{3,4},{4,5},{5,6},{6,7},{7,8},{8,9},{9,10},{10,1... | collective-permute-start | bytes 98312 | tf_op jit(solution)/shard_map/ppermute | solution.py:274

commit v5 on v4

--- a/solution.py
+++ b/solution.py
@@ -24,7 +24,7 @@
         out_shape=tuple(jax.ShapeDtypeStruct(shape, jnp.float32) for shape in out_shapes),
         in_specs=in_specs,
         compiler_params=pltpu.CompilerParams(vmem_limit_bytes=16 << 20),
-        cost_estimate=pl.CostEstimate(flops=0, transcendentals=0, bytes_accessed=int(cost_us * 3.0e6)),
+        cost_estimate=pl.CostEstimate(flops=int(cost_us * 1.0e9), transcendentals=0, bytes_accessed=int(cost_us * 3.0e6)),
         name=kernel.__name__,
         **more,
     )
@@ -91,34 +91,23 @@
         copies[place] = piece
 
 
-def end_layers(field, dual, ahead, down, up, layers, duals, sems):
+def first_layer(field, dual, ahead, down, layers, duals, sems):
     copies = [
-        pltpu.make_async_copy(field.at[0:2], layers.at[0:2], sems.at[0]),
-        pltpu.make_async_copy(dual.at[:, 0], duals.at[0], sems.at[1]),
-        pltpu.make_async_copy(field.at[LAYERS - 1], layers.at[2], sems.at[2]),
-        pltpu.make_async_copy(dual.at[:, LAYERS - 1], duals.at[1], sems.at[3]),
+        pltpu.make_async_copy(field.at[0:2], layers, sems.at[0]),
+        pltpu.make_async_copy(dual.at[:, 0], duals, sems.at[1]),
     ]
     for copy in copies:
         copy.start()
     for copy in copies:
         copy.wait()
     here = layers[0]
-    dual_z, dual_x, dual_y = dual_layer(here, layers[1], ahead[0:1, :], duals[0, 0], duals[0, 1], duals[0, 2], False)
+    dual_z, dual_x, dual_y = dual_layer(here, layers[1], ahead[0:1, :], duals[0], duals[1], duals[2], False)
     down[0:16, :] = here
     down[16:32, :] = here + 0.25 * (dual_z + flux(dual_x, dual_y, jnp.zeros((1, LANES), jnp.float32)))
     down[32:40, :] = dual_x[8:16, :]
-    moved_x, moved_y = moved_sides(layers[2], ahead[7:8, :], duals[1, 1], duals[1, 2])
-    up[0:16, :] = duals[1, 0] - 0.25 * layers[2]
-    up[16:32, :] = moved_x * moved_x + moved_y * moved_y
-
-
-def top_of(up, here):
-    moved = up[0:16, :] + 0.25 * here
-    scale = 1.0 / jnp.sqrt(jnp.maximum(moved * moved + up[16:32, :], 1.0))
-    return jnp.where(lax.axis_index("slab") == 0, 0.0, moved * scale)
-
-
-def all_duals(field, dual, ahead, below, up, new_dual, top, side):
+
+
+def all_duals(field, dual, ahead, below, new_dual, top, side):
     slab_end = lax.axis_index("slab") == Z_LAST
     for layer in range(LAYERS):
         last = layer == LAYERS - 1
@@ -135,7 +124,7 @@
         new_dual[1, layer] = dual_x
         new_dual[2, layer] = dual_y
         side[layer : layer + 1, :] = dual_x[15:16, :]
-    top[...] = top_of(up, field[0])
+    top[...] = new_dual[0, LAYERS - 1]
     side[8:16, :] = jnp.zeros((8, LANES), jnp.float32)
     side[8:9, :] = below[39:40, :]
 
@@ -292,30 +281,29 @@
     spread = exchange(pieces)
 
     ahead = passed_along(field[:, 0], "tile", -1)
-    down, up = call(
-        end_layers, [(40, LANES), (32, LANES)], 1, [HBM, HBM, VMEM],
+    (down,) = call(
+        first_layer, [(40, LANES)], 1, [HBM, HBM, VMEM],
         scratch_shapes=[
+            pltpu.VMEM((2, ROWS, LANES), jnp.float32),
             pltpu.VMEM((3, ROWS, LANES), jnp.float32),
-            pltpu.VMEM((2, 3, ROWS, LANES), jnp.float32),
-            pltpu.SemaphoreType.DMA((4,)),
+            pltpu.SemaphoreType.DMA((2,)),
         ],
     )(pltpu.with_memory_space_constraint(field, pltpu.HBM), pltpu.with_memory_space_constraint(dual, pltpu.HBM), ahead)
     (kept,) = call(pick, [(8, 8, 128)], 1, [SMEM, VMEM])(owner, spread)
     kept, _ = lax.optimization_barrier((kept, down))
     across = lax.ppermute(kept, "slab", [(index, index ^ 1) for index in range(32)])
     below = passed_along(down, "slab", -1)
-    above = passed_along(up, "slab", 1)
-    across, below, above = lax.optimization_barrier((across, below, above))
     (copies,) = call(copies_of, [pieces.shape], 1, [SMEM, VMEM, VMEM])(owner, kept, across)
     batches = exchange(copies)
     below, _ = lax.optimization_barrier((below, copies))
-    dual, above, side = call(all_duals, [(3,) + block, (ROWS, LANES), (ROWS, LANES)], 1, [VMEM] * 5)(
-        field, dual, ahead, below, above
+    dual, top, side = call(all_duals, [(3,) + block, (ROWS, LANES), (ROWS, LANES)], 4, [VMEM] * 4)(
+        field, dual, ahead, below
     )
     before = passed_along(side, "tile", 1)
+    above = passed_along(top, "slab", 1)
 
     (tally,) = call(first_votes, [(BINS + 1, LAYERS + 1, ROWS, LANES)], 4, [SMEM, VMEM])(visible, batches)
-    before, tally = lax.optimization_barrier((before, tally))
+    above, before, tally = lax.optimization_barrier((above, before, tally))
     current, extra, side = call(first_update, [block, (LAYERS + 1, ROWS, LANES), (LAYERS, LANES)], 1, [VMEM] * 6)(
         field, dual, above, before, below, tally
     )

time: 112 us -> 106 us (0.946)
  the two profiles are of different devices: /device:TPU:3 before, /device:TPU:101 now
where the time goes in v5:
time: 106 us; the launch traced here: 105 us
  starting transfers between devices  44.9 us (42%)
  waiting for transfers between devices  42.3 us (40%)
  Pallas kernels  14.6 us (14%)
  local copies, waits for them, and re-layouts  2.53 us (2%)
    ppermute x7, waiting for transfers between devices, passed_along(): lax.ppermute(value, axis, [(source, source + steps) for source in range(f...  42.3 us
    ppermute x7, starting transfers between devices, passed_along(): lax.ppermute(value, axis, [(source, source + steps) for source in range(f...  21.3 us
    ppermute x1, starting transfers between devices, per_device(): lax.ppermute(kept, 'slab', [(index, index ^ 1) for index in range(32)])  11.9 us
    all_to_all x2, starting transfers between devices, exchange(): return lax.all_to_all(pieces, 'slab', 0, 0, axis_index_groups=GROUPS)  11.7 us
    pallas_call x1, Pallas kernels, per_device(): call(first_votes, [(BINS + 1, LAYERS + 1, ROWS, LANES)], 4, [SMEM, VMEM])  2.98 us
    pallas_call x1, Pallas kernels, per_device(): call(second_votes, [(BINS + 1,) + block], 3, [SMEM, VMEM, VMEM, ANY])  2.9 us
  transfers between devices with their start and end apart: 10, of which 5 were waited for; matrix products, arithmetic and copies ran while one was open for 1% of the time, Pallas kernels for 12%

profile of v5, /device:TPU:101, one launch (start us, length us, event | category | flops | bytes accessed | tf_op | source)
XLA Modules:
  0.0 105.2 jit_solution(3573848489873519911)
XLA Ops:
  0.6 6.9 %all-to-all-start = ((f32[16,8,8,128]{3,2,1,0:T(8,128)}), f32[16,8,8,128]{3,2,1,0:T(8,128)S(1)}, u32[]{:S(2)}, u32[]{:S(2)}) async-start(f32[16,8,8,128]{3,2,1,0:T(8,128)} %bitcast.6), calls=%async_computation | async-start | bytes 1048576 | tf_op jit(solution)/shard_map/all_to_all | solution.py:270
  7.5 1.0 slice.9
  8.5 0.0 copy-start.3
  8.5 3.1 %collective-permute-start = (f32[8,1024]{1,0:T(8,128)S(1)}, f32[8,1024]{1,0:T(8,128)S(1)}, u32[]{:S(2)}, u32[]{:S(2)}) collective-permute-start(f32[8,1024]{1,0:T(8,128)S(1)} %bitcast.7), channel_id=1, source_target_pairs={{1,0},{2,1},{3,2},{4,3},{5,4},{6,5},{7,6},{8,7},{9,8},{10,9},{11,1... | collective-permute-start | bytes 98312 | tf_op jit(solution)/shard_map/ppermute | solution.py:263
  11.7 4.6 %collective-permute-done.ahead = f32[8,1024]{1,0:T(8,128)S(1)} collective-permute-done((f32[8,1024]{1,0:T(8,128)S(1)}, f32[8,1024]{1,0:T(8,128)S(1)}, u32[]{:S(2)}, u32[]{:S(2)}) %collective-permute-start) | collective-permute-done | bytes 32800 | tf_op jit(solution)/shard_map/ppermute | solution.py:263
  16.3 1.2 %first_layer.1 = f32[40,1024]{1,0:T(8,128)S(1)} custom-call(f32[8,16,1024]{2,1,0:T(8,128)} %field.5, f32[3,8,16,1024]{3,2,1,0:T(8,128)} %dual.3, f32[8,1024]{1,0:T(8,128)S(1)} %collective-permute-done.ahead), custom_call_target="tpu_custom_call" | custom-call | flops 1000000000 | bytes 3000000 | tf_op jit(solution)/shard_map/first_layer/pallas_call | solution.py:284
  17.5 0.0 all-to-all-done.spread
  17.5 0.0 copy-done.3
  17.5 0.6 pick.1.kept
  18.1 0.0 copy-start.4
  18.1 0.0 copy-start.1
  18.1 11.9 %collective-permute-start.2 = (f32[8,8,128]{2,1,0:T(8,128)S(1)}, f32[8,8,128]{2,1,0:T(8,128)S(1)}, u32[]{:S(2)}, u32[]{:S(2)}) collective-permute-start(f32[8,8,128]{2,1,0:T(8,128)S(1)} %pick.1.kept), channel_id=1, source_target_pairs={{0,16},{16,0},{32,48},{48,32},{64,80},{80,64},{96,112},{112,96},{1... | collective-permute-start | bytes 98312 | tf_op jit(solution)/shard_map/ppermute | solution.py:294
  30.0 4.1 %collective-permute-start.1 = (f32[40,1024]{1,0:T(8,128)S(1)}, f32[40,1024]{1,0:T(8,128)S(1)}, u32[]{:S(2)}, u32[]{:S(2)}) collective-permute-start(f32[40,1024]{1,0:T(8,128)S(1)} %first_layer.1), channel_id=1, source_target_pairs={{16,0},{32,16},{48,32},{64,48},{80,64},{96,80},{112,96},{128,112},... | collective-permute-start | bytes 491528 | tf_op jit(solution)/shard_map/ppermute | solution.py:263
  34.1 0.0 collective-permute-done.2.across
  34.1 1.4 %copies_of.1 = f32[16,8,8,128]{3,2,1,0:T(8,128)} custom-call(s32[2]{0:T(128)S(1)} %copy-done.3, f32[8,8,128]{2,1,0:T(8,128)S(1)} %pick.1.kept, f32[8,8,128]{2,1,0:T(8,128)S(1)} %collective-permute-done.2.across), custom_call_target="tpu_custom_call" | custom-call | flops 1000000000 | bytes 3000000 | tf_op jit(solution)/shard_map/copies_of/pallas_call | solution.py:296
  35.5 4.8 %all-to-all-start.1 = ((f32[16,8,8,128]{3,2,1,0:T(8,128)}), f32[16,8,8,128]{3,2,1,0:T(8,128)S(1)}, u32[]{:S(2)}, u32[]{:S(2)}) async-start(f32[16,8,8,128]{3,2,1,0:T(8,128)} %copies_of.1), calls=%async_computation.1 | async-start | bytes 1048576 | tf_op jit(solution)/shard_map/all_to_all | solution.py:270
  40.3 0.0 copy-done.4
  40.3 0.1 copy.9.visible
  40.4 17.4 %collective-permute-done.1.below = f32[40,1024]{1,0:T(8,128)S(1)} collective-permute-done((f32[40,1024]{1,0:T(8,128)S(1)}, f32[40,1024]{1,0:T(8,128)S(1)}, u32[]{:S(2)}, u32[]{:S(2)}) %collective-permute-start.1) | collective-permute-done | bytes 163872 | tf_op jit(solution)/shard_map/ppermute | solution.py:263
  57.8 0.0 copy-done.1
  57.8 0.0 copy-start.2
  57.8 1.4 %copy-done.2 = f32[3,8,16,1024]{3,2,1,0:T(8,128)S(1)} copy-done((f32[3,8,16,1024]{3,2,1,0:T(8,128)S(1)}, f32[3,8,16,1024]{3,2,1,0:T(8,128)}, u32[]{:S(2)}) %copy-start.2) | copy-done | bytes 1572888
  59.2 0.6 all_duals.1
  59.8 1.9 %collective-permute-start.3 = (f32[16,1024]{1,0:T(8,128)S(1)}, f32[16,1024]{1,0:T(8,128)S(1)}, u32[]{:S(2)}, u32[]{:S(2)}) collective-permute-start(f32[16,1024]{1,0:T(8,128)S(1)} %get-tuple-element.20), channel_id=1, source_target_pairs={{0,16},{16,32},{32,48},{48,64},{64,80},{80,96},{96,112},{112,128},... | collective-permute-start | bytes 196616 | tf_op jit(solution)/shard_map/ppermute | solution.py:263
  61.7 5.5 %collective-permute-start.4 = (f32[16,1024]{1,0:T(8,128)S(1)}, f32[16,1024]{1,0:T(8,128)S(1)}, u32[]{:S(2)}, u32[]{:S(2)}) collective-permute-start(f32[16,1024]{1,0:T(8,128)S(1)} %get-tuple-element.21), channel_id=1, source_target_pairs={{0,1},{1,2},{2,3},{3,4},{4,5},{5,6},{6,7},{7,8},{8,9},{9,10},{10,1... | collective-permute-start | bytes 196616 | tf_op jit(solution)/shard_map/ppermute | solution.py:263
  67.2 0.0 all-to-all-done.1.batches
  67.3 3.0 %first_votes.1.tally = f32[9,9,16,1024]{3,2,1,0:T(8,128)S(1)} custom-call(s32[2,4,1]{2,1,0:T(4,128)S(1)} %copy.9.visible, f32[16,8,8,128]{3,2,1,0:T(8,128)S(1)} %all-to-all-done.1.batches), custom_call_target="tpu_custom_call" | custom-call | flops 4000000000 | bytes 12000000 | tf_op jit(solution)/shard_map/first_votes/pallas_call | solution.py:305
  70.2 9.3 %collective-permute-done.3.above = f32[16,1024]{1,0:T(8,128)S(1)} collective-permute-done((f32[16,1024]{1,0:T(8,128)S(1)}, f32[16,1024]{1,0:T(8,128)S(1)}, u32[]{:S(2)}, u32[]{:S(2)}) %collective-permute-start.3) | collective-permute-done | bytes 65568 | tf_op jit(solution)/shard_map/ppermute | solution.py:263
  79.6 0.0 collective-permute-done.4.before
  79.6 0.9 first_update.1
  80.5 2.7 %collective-permute-start.5 = (f32[8,1024]{1,0:T(8,128)S(1)}, f32[8,1024]{1,0:T(8,128)S(1)}, u32[]{:S(2)}, u32[]{:S(2)}) collective-permute-start(f32[8,1024]{1,0:T(8,128)S(1)} %get-tuple-element.27), channel_id=1, source_target_pairs={{1,0},{2,1},{3,2},{4,3},{5,4},{6,5},{7,6},{8,7},{9,8},{10,9},{11,1... | collective-permute-start | bytes 98312 | tf_op jit(solution)/shard_map/ppermute | solution.py:263
  83.3 3.7 %collective-permute-done.5.ahead = f32[8,1024]{1,0:T(8,128)S(1)} collective-permute-done((f32[8,1024]{1,0:T(8,128)S(1)}, f32[8,1024]{1,0:T(8,128)S(1)}, u32[]{:S(2)}, u32[]{:S(2)}) %collective-permute-start.5) | collective-permute-done | bytes 32800 | tf_op jit(solution)/shard_map/ppermute | solution.py:263
  86.9 0.1 top_dual.1.after
  87.1 1.9 %collective-permute-start.6 = (f32[16,1024]{1,0:T(8,128)S(1)}, f32[16,1024]{1,0:T(8,128)S(1)}, u32[]{:S(2)}, u32[]{:S(2)}) collective-permute-start(f32[16,1024]{1,0:T(8,128)S(1)} %top_dual.1.after), channel_id=1, source_target_pairs={{0,16},{16,32},{32,48},{48,64},{64,80},{80,96},{96,112},{112,128},... | collective-permute-start | bytes 196616 | tf_op jit(solution)/shard_map/ppermute | solution.py:263
  89.0 1.8 %second_duals.1 = (f32[3,8,16,1024]{3,2,1,0:T(8,128)}, f32[8,1024]{1,0:T(8,128)S(1)}) custom-call(f32[9,16,1024]{2,1,0:T(8,128)S(1)} %get-tuple-element.26.extra, f32[3,8,16,1024]{3,2,1,0:T(8,128)S(1)} %get-tuple-element.19.dual, f32[8,1024]{1,0:T(8,128)S(1)} %collective-permute-done.5.ahead, f32[16,1024]{1,0:T(8,128)S(1)} %top_dual.1.after), custom_call_target="tpu_custom_call" | custom-call | flops 1000000000 | bytes 3000000 | tf_op jit(solution)/shard_map/second_duals/pallas_call | solution.py:313
  90.8 0.0 copy-start
  90.8 2.0 %collective-permute-start.7 = (f32[8,1024]{1,0:T(8,128)S(1)}, f32[8,1024]{1,0:T(8,128)S(1)}, u32[]{:S(2)}, u32[]{:S(2)}) collective-permute-start(f32[8,1024]{1,0:T(8,128)S(1)} %get-tuple-element.29.after), channel_id=1, source_target_pairs={{0,1},{1,2},{2,3},{3,4},{4,5},{5,6},{6,7},{7,8},{8,9},{9,10},{10,1... | collective-permute-start | bytes 98312 | tf_op jit(solution)/shard_map/ppermute | solution.py:263
  92.8 2.9 %second_votes.1.tally = f32[9,8,16,1024]{3,2,1,0:T(8,128)S(1)} custom-call(s32[2,4,1]{2,1,0:T(4,128)S(1)} %copy.9.visible, f32[16,8,8,128]{3,2,1,0:T(8,128)S(1)} %all-to-all-done.1.batches, f32[9,9,16,1024]{3,2,1,0:T(8,128)S(1)} %first_votes.1.tally, f32[8,1024]{1,0:T(8,128)S(1)} %get-tuple-element.29.after), custom_call_target="tpu_custom_call" | custom-call | flops 3000000000 | bytes 9000000 | tf_op jit(solution)/shard_map/second_votes/pallas_call | solution.py:315
  95.7 0.0 collective-permute-done.7.before
  95.7 0.0 copy-done
  95.7 1.4 %last_layers.1.updated_in = f32[8,16,1024]{2,1,0:T(8,128)} custom-call(f32[8,16,1024]{2,1,0:T(8,128)S(1)} %get-tuple-element.25.current, f32[3,8,16,1024]{3,2,1,0:T(8,128)S(1)} %copy-done, f32[8,1024]{1,0:T(8,128)S(1)} %collective-permute-done.7.before, f32[9,8,16,1024]{3,2,1,0:T(8,128)S(1)} %second_votes.1.tally), custom_call_target="tpu_custom_call" | custom-call | flops 1000000000 | bytes 3000000 | tf_op jit(solution)/shard_map/last_layers/pallas_call | solution.py:316
  97.2 7.3 %collective-permute-done.6.above = f32[16,1024]{1,0:T(8,128)S(1)} collective-permute-done((f32[16,1024]{1,0:T(8,128)S(1)}, f32[16,1024]{1,0:T(8,128)S(1)}, u32[]{:S(2)}, u32[]{:S(2)}) %collective-permute-start.6) | collective-permute-done | bytes 65568 | tf_op jit(solution)/shard_map/ppermute | solution.py:263
  104.4 0.8 last_layer.1
  (3 shorter events, 0.0 us)
Async XLA Ops:
  0.6 16.9 %all-to-all-start = ((f32[16,8,8,128]{3,2,1,0:T(8,128)}), f32[16,8,8,128]{3,2,1,0:T(8,128)S(1)}, u32[]{:S(2)}, u32[]{:S(2)}) async-start(f32[16,8,8,128]{3,2,1,0:T(8,128)} %bitcast.6), calls=%async_computation | async-start | bytes 1048576 | tf_op jit(solution)/shard_map/all_to_all | solution.py:270
  8.5 9.0 %copy-start.3 = (s32[2]{0:T(128)S(1)}, s32[2]{0:T(128)}, u32[]{:S(2)}) copy-start(s32[2]{0:T(128)} %owner.3) | copy-start | bytes 28
  8.5 7.8 %collective-permute-start = (f32[8,1024]{1,0:T(8,128)S(1)}, f32[8,1024]{1,0:T(8,128)S(1)}, u32[]{:S(2)}, u32[]{:S(2)}) collective-permute-start(f32[8,1024]{1,0:T(8,128)S(1)} %bitcast.7), channel_id=1, source_target_pairs={{1,0},{2,1},{3,2},{4,3},{5,4},{6,5},{7,6},{8,7},{9,8},{10,9},{11,1... | collective-permute-start | bytes 98312 | tf_op jit(solution)/shard_map/ppermute | solution.py:263
  18.1 22.2 %copy-start.4 = (s32[2,4,1]{1,2,0:T(1,128)S(1)}, s32[2,4,1]{1,2,0:T(1,128)}, u32[]{:S(2)}) copy-start(s32[2,4,1]{1,2,0:T(1,128)} %param.9) | copy-start | bytes 100
  18.1 39.7 %copy-start.1 = (f32[8,16,1024]{2,1,0:T(8,128)S(1)}, f32[8,16,1024]{2,1,0:T(8,128)}, u32[]{:S(2)}) copy-start(f32[8,16,1024]{2,1,0:T(8,128)} %field.5) | copy-start | bytes 1572868
  18.1 16.0 %collective-permute-start.2 = (f32[8,8,128]{2,1,0:T(8,128)S(1)}, f32[8,8,128]{2,1,0:T(8,128)S(1)}, u32[]{:S(2)}, u32[]{:S(2)}) collective-permute-start(f32[8,8,128]{2,1,0:T(8,128)S(1)} %pick.1.kept), channel_id=1, source_target_pairs={{0,16},{16,0},{32,48},{48,32},{64,80},{80,64},{96,112},{112,96},{1... | collective-permute-start | bytes 98312 | tf_op jit(solution)/shard_map/ppermute | solution.py:294
  30.0 27.8 %collective-permute-start.1 = (f32[40,1024]{1,0:T(8,128)S(1)}, f32[40,1024]{1,0:T(8,128)S(1)}, u32[]{:S(2)}, u32[]{:S(2)}) collective-permute-start(f32[40,1024]{1,0:T(8,128)S(1)} %first_layer.1), channel_id=1, source_target_pairs={{16,0},{32,16},{48,32},{64,48},{80,64},{96,80},{112,96},{128,112},... | collective-permute-start | bytes 491528 | tf_op jit(solution)/shard_map/ppermute | solution.py:263
  35.5 31.7 %all-to-all-start.1 = ((f32[16,8,8,128]{3,2,1,0:T(8,128)}), f32[16,8,8,128]{3,2,1,0:T(8,128)S(1)}, u32[]{:S(2)}, u32[]{:S(2)}) async-start(f32[16,8,8,128]{3,2,1,0:T(8,128)} %copies_of.1), calls=%async_computation.1 | async-start | bytes 1048576 | tf_op jit(solution)/shard_map/all_to_all | solution.py:270
  57.8 1.4 %copy-start.2 = (f32[3,8,16,1024]{3,2,1,0:T(8,128)S(1)}, f32[3,8,16,1024]{3,2,1,0:T(8,128)}, u32[]{:S(2)}) copy-start(f32[3,8,16,1024]{3,2,1,0:T(8,128)} %dual.3) | copy-start | bytes 4718596
  59.8 19.8 %collective-permute-start.3 = (f32[16,1024]{1,0:T(8,128)S(1)}, f32[16,1024]{1,0:T(8,128)S(1)}, u32[]{:S(2)}, u32[]{:S(2)}) collective-permute-start(f32[16,1024]{1,0:T(8,128)S(1)} %get-tuple-element.20), channel_id=1, source_target_pairs={{0,16},{16,32},{32,48},{48,64},{64,80},{80,96},{96,112},{112,128},... | collective-permute-start | bytes 196616 | tf_op jit(solution)/shard_map/ppermute | solution.py:263
  61.7 17.8 %collective-permute-start.4 = (f32[16,1024]{1,0:T(8,128)S(1)}, f32[16,1024]{1,0:T(8,128)S(1)}, u32[]{:S(2)}, u32[]{:S(2)}) collective-permute-start(f32[16,1024]{1,0:T(8,128)S(1)} %get-tuple-element.21), channel_id=1, source_target_pairs={{0,1},{1,2},{2,3},{3,4},{4,5},{5,6},{6,7},{7,8},{8,9},{9,10},{10,1... | collective-permute-start | bytes 196616 | tf_op jit(solution)/shard_map/ppermute | solution.py:263
  80.5 6.5 %collective-permute-start.5 = (f32[8,1024]{1,0:T(8,128)S(1)}, f32[8,1024]{1,0:T(8,128)S(1)}, u32[]{:S(2)}, u32[]{:S(2)}) collective-permute-start(f32[8,1024]{1,0:T(8,128)S(1)} %get-tuple-element.27), channel_id=1, source_target_pairs={{1,0},{2,1},{3,2},{4,3},{5,4},{6,5},{7,6},{8,7},{9,8},{10,9},{11,1... | collective-permute-start | bytes 98312 | tf_op jit(solution)/shard_map/ppermute | solution.py:263
  87.1 17.4 %collective-permute-start.6 = (f32[16,1024]{1,0:T(8,128)S(1)}, f32[16,1024]{1,0:T(8,128)S(1)}, u32[]{:S(2)}, u32[]{:S(2)}) collective-permute-start(f32[16,1024]{1,0:T(8,128)S(1)} %top_dual.1.after), channel_id=1, source_target_pairs={{0,16},{16,32},{32,48},{48,64},{64,80},{80,96},{96,112},{112,128},... | collective-permute-start | bytes 196616 | tf_op jit(solution)/shard_map/ppermute | solution.py:263
  90.8 5.0 %copy-start = (f32[3,8,16,1024]{3,2,1,0:T(8,128)S(1)}, f32[3,8,16,1024]{3,2,1,0:T(8,128)}, u32[]{:S(2)}) copy-start(f32[3,8,16,1024]{3,2,1,0:T(8,128)} %get-tuple-element.16.dual) | copy-start | bytes 4718596
  90.8 5.0 %collective-permute-start.7 = (f32[8,1024]{1,0:T(8,128)S(1)}, f32[8,1024]{1,0:T(8,128)S(1)}, u32[]{:S(2)}, u32[]{:S(2)}) collective-permute-start(f32[8,1024]{1,0:T(8,128)S(1)} %get-tuple-element.29.after), channel_id=1, source_target_pairs={{0,1},{1,2},{2,3},{3,4},{4,5},{5,6},{6,7},{7,8},{8,9},{9,10},{10,1... | collective-permute-start | bytes 98312 | tf_op jit(solution)/shard_map/ppermute | solution.py:263

commit v6 on v5

--- a/solution.py
+++ b/solution.py
@@ -74,11 +74,6 @@
     )
 
 
-def flux(dual_x, dual_y, before_row):
-    before = jnp.where(row_ids() == 0, spread_row(before_row), pltpu.roll(dual_x, 1, 0))
-    return (dual_x - before) + (dual_y - pltpu.roll(dual_y, 1, 1))
-
-
 def pick(owner, spread, kept):
     kept[...] = spread[lax.shift_right_logical(owner[lax.shift_right_logical(lax.axis_index("slab"), 4)], 1)]
 
@@ -91,29 +86,13 @@
         copies[place] = piece
 
 
-def first_layer(field, dual, ahead, down, layers, duals, sems):
-    copies = [
-        pltpu.make_async_copy(field.at[0:2], layers, sems.at[0]),
-        pltpu.make_async_copy(dual.at[:, 0], duals, sems.at[1]),
-    ]
-    for copy in copies:
-        copy.start()
-    for copy in copies:
-        copy.wait()
-    here = layers[0]
-    dual_z, dual_x, dual_y = dual_layer(here, layers[1], ahead[0:1, :], duals[0], duals[1], duals[2], False)
-    down[0:16, :] = here
-    down[16:32, :] = here + 0.25 * (dual_z + flux(dual_x, dual_y, jnp.zeros((1, LANES), jnp.float32)))
-    down[32:40, :] = dual_x[8:16, :]
-
-
-def all_duals(field, dual, ahead, below, new_dual, top, side):
+def all_duals(field, dual, ahead, past, new_dual, top, side):
     slab_end = lax.axis_index("slab") == Z_LAST
     for layer in range(LAYERS):
         last = layer == LAYERS - 1
         dual_z, dual_x, dual_y = dual_layer(
             field[layer],
-            below[0:16, :] if last else field[layer + 1],
+            past[...] if last else field[layer + 1],
             ahead[layer : layer + 1, :],
             dual[0, layer],
             dual[1, layer],
@@ -124,9 +103,47 @@
         new_dual[1, layer] = dual_x
         new_dual[2, layer] = dual_y
         side[layer : layer + 1, :] = dual_x[15:16, :]
-    top[...] = new_dual[0, LAYERS - 1]
-    side[8:16, :] = jnp.zeros((8, LANES), jnp.float32)
-    side[8:9, :] = below[39:40, :]
+        if last:
+            top[...] = dual_z
+
+
+def second_duals(field, dual, ahead, past, after, new_dual, side):
+    slab_end = lax.axis_index("slab") == Z_LAST
+    for layer in range(LAYERS):
+        last = layer == LAYERS - 1
+        dual_z, dual_x, dual_y = dual_layer(
+            field[layer],
+            past[...] if last else field[layer + 1],
+            ahead[layer : layer + 1, :],
+            dual[0, layer],
+            dual[1, layer],
+            dual[2, layer],
+            slab_end if last else False,
+        )
+        new_dual[0, layer] = dual_z
+        new_dual[1, layer] = dual_x
+        new_dual[2, layer] = dual_y
+        side[layer : layer + 1, :] = dual_x[15:16, :]
+
+
+def flux_of(dual, before, layer):
+    row, dual_x, dual_y = spread_row(before[layer : layer + 1, :]), dual[1, layer], dual[2, layer]
+    shifted = jnp.where(row_ids() == 0, row, pltpu.roll(dual_x, 1, 0))
+    return (dual_x - shifted) + (dual_y - pltpu.roll(dual_y, 1, 1))
+
+
+def stepped(field, dual, above, before, layer):
+    prev = above[...] if layer == 0 else dual[0, layer - 1]
+    return field[layer] + 0.25 * ((dual[0, layer] - prev) + flux_of(dual, before, layer))
+
+
+def first_values(field, dual, before, values):
+    values[...] = field[0] + 0.25 * (dual[0, 0] + flux_of(dual, before, 0))
+
+
+def all_values(field, dual, above, before, values):
+    for layer in range(LAYERS):
+        values[layer] = stepped(field, dual, above, before, layer)
 
 
 def ramps(depth, base):
@@ -202,50 +219,23 @@
     return proximal(values, sums, tally[BINS - 1, layer], tally[BINS, layer])
 
 
-def stepped(field, dual, above, before, layer):
-    prev = above[...] if layer == 0 else dual[0, layer - 1]
-    return field[layer] + 0.25 * (
-        (dual[0, layer] - prev) + flux(dual[1, layer], dual[2, layer], before[layer : layer + 1, :])
-    )
-
-
-def first_update(field, dual, above, before, below, tally, updated, extra, side):
+def first_update(field, values, tally, updated, extra, side):
     for layer in range(LAYERS):
-        new = counted(stepped(field, dual, above, before, layer), tally, layer)
+        new = counted(values[layer], tally, layer)
         updated[layer] = new
         new = 2.0 * new - field[layer]
         extra[layer] = new
         side[layer : layer + 1, :] = new[0:1, :]
-    past = jnp.where(row_ids() == 0, spread_row(before[8:9, :]), 0.0)
-    values = below[16:32, :] - 0.25 * (dual[0, LAYERS - 1] + past)
-    extra[LAYERS] = 2.0 * counted(values, tally, LAYERS) - below[0:16, :]
-
-
-def top_dual(extra, dual, ahead, top):
-    layer = LAYERS - 1
+
+
+def past_update(below, values, dual, tally, extra):
+    extra[...] = 2.0 * counted(values[...] - 0.25 * dual[0, 0], tally, 0) - below[...]
+
+
+def top_dual(extra, past, dual, ahead, top):
     slab_end = lax.axis_index("slab") == Z_LAST
-    top[...] = dual_layer(
-        extra[0], extra[1], ahead[layer : layer + 1, :], dual[0, 0], dual[1, 0], dual[2, 0], slab_end
-    )[0]
-
-
-def second_duals(extra, dual, ahead, after, new_dual, side):
-    slab_end = lax.axis_index("slab") == Z_LAST
-    for layer in range(LAYERS):
-        last = layer == LAYERS - 1
-        dual_z, dual_x, dual_y = dual_layer(
-            extra[layer],
-            extra[layer + 1],
-            ahead[layer : layer + 1, :],
-            dual[0, layer],
-            dual[1, layer],
-            dual[2, layer],
-            slab_end if last else False,
-        )
-        new_dual[0, layer] = dual_z
-        new_dual[1, layer] = dual_x
-        new_dual[2, layer] = dual_y
-        side[layer : layer + 1, :] = dual_x[15:16, :]
+    row = ahead[LAYERS - 1 : LAYERS, :]
+    top[...] = dual_layer(extra[0], past[...], row, dual[0, 0], dual[1, 0], dual[2, 0], slab_end)[0]
 
 
 def last_layers(current, dual, before, tally, updated):
@@ -280,37 +270,35 @@
     pieces = depth.reshape(16, 8, 8, 128).transpose(0, 2, 1, 3)
     spread = exchange(pieces)
 
+    below = passed_along(field[0], "slab", -1)
     ahead = passed_along(field[:, 0], "tile", -1)
-    (down,) = call(
-        first_layer, [(40, LANES)], 1, [HBM, HBM, VMEM],
-        scratch_shapes=[
-            pltpu.VMEM((2, ROWS, LANES), jnp.float32),
-            pltpu.VMEM((3, ROWS, LANES), jnp.float32),
-            pltpu.SemaphoreType.DMA((2,)),
-        ],
-    )(pltpu.with_memory_space_constraint(field, pltpu.HBM), pltpu.with_memory_space_constraint(dual, pltpu.HBM), ahead)
     (kept,) = call(pick, [(8, 8, 128)], 1, [SMEM, VMEM])(owner, spread)
-    kept, _ = lax.optimization_barrier((kept, down))
     across = lax.ppermute(kept, "slab", [(index, index ^ 1) for index in range(32)])
-    below = passed_along(down, "slab", -1)
+    below, ahead, _ = lax.optimization_barrier((below, ahead, kept))
+    layer, rows = (ROWS, LANES), (LAYERS, LANES)
+    dual, top, side = call(all_duals, [(3,) + block, layer, rows], 1, [VMEM] * 4)(field, dual, ahead, below)
+    above = passed_along(top, "slab", 1)
+    before = passed_along(side, "tile", 1)
+    across, top, side = lax.optimization_barrier((across, top, side))
     (copies,) = call(copies_of, [pieces.shape], 1, [SMEM, VMEM, VMEM])(owner, kept, across)
     batches = exchange(copies)
-    below, _ = lax.optimization_barrier((below, copies))
-    dual, top, side = call(all_duals, [(3,) + block, (ROWS, LANES), (ROWS, LANES)], 4, [VMEM] * 4)(
-        field, dual, ahead, below
-    )
-    before = passed_along(side, "tile", 1)
+    (values,) = call(first_values, [layer], 1, [VMEM] * 3)(field, dual, before)
+    past_values = passed_along(values, "slab", -1)
+    (values,) = call(all_values, [block], 5, [VMEM] * 4)(field, dual, above, before)
+
+    (tally,) = call(first_votes, [(BINS + 1, LAYERS + 1) + layer], 12, [SMEM, VMEM])(visible, batches)
+    current, extra, side = call(first_update, [block, block, rows], 1, [VMEM] * 3)(field, values, tally)
+    ahead = passed_along(side, "tile", -1)
+    last_tally = pl.BlockSpec((BINS + 1, 1) + layer, lambda step: (0, LAYERS, 0, 0))
+    last_dual = pl.BlockSpec((3, 1) + layer, lambda step: (0, LAYERS - 1, 0, 0))
+    last_block = pl.BlockSpec((1,) + layer, lambda step: (LAYERS - 1, 0, 0))
+    past_values, _ = lax.optimization_barrier((past_values, side))
+    (past,) = call(past_update, [layer], 1, [VMEM, VMEM, last_dual, last_tally], grid=(1,))(
+        below, past_values, dual, tally
+    )
+    (top,) = call(top_dual, [layer], 1, [last_block, VMEM, last_dual, VMEM], grid=(1,))(extra, past, dual, ahead)
     above = passed_along(top, "slab", 1)
-
-    (tally,) = call(first_votes, [(BINS + 1, LAYERS + 1, ROWS, LANES)], 4, [SMEM, VMEM])(visible, batches)
-    above, before, tally = lax.optimization_barrier((above, before, tally))
-    current, extra, side = call(first_update, [block, (LAYERS + 1, ROWS, LANES), (LAYERS, LANES)], 1, [VMEM] * 6)(
-        field, dual, above, before, below, tally
-    )
-    ahead = passed_along(side, "tile", -1)
-    (top,) = call(top_dual, [(ROWS, LANES)], 1, [VMEM] * 3)(extra[7:9], dual[:, 7:8], ahead)
-    above = passed_along(top, "slab", 1)
-    dual, side = call(second_duals, [(3,) + block, (LAYERS, LANES)], 1, [VMEM] * 3 + [ANY])(extra, dual, ahead, top)
+    dual, side = call(second_duals, [(3,) + block, rows], 1, [VMEM] * 4 + [ANY])(extra, dual, ahead, past, top)
     before = passed_along(side, "tile", 1)
     (tally,) = call(second_votes, [(BINS + 1,) + block], 3, [SMEM, VMEM, VMEM, ANY])(visible, batches, tally, side)
     (rest,) = call(last_layers, [block], 1, [VMEM] * 4)(current, dual, before, tally)

time: 106 us -> 99.7 us (0.941)
  the two profiles are of different devices: /device:TPU:101 before, /device:TPU:35 now
where the time goes in v6:
time: 99.7 us; the launch traced here: 99.1 us
  starting transfers between devices  71.3 us (72%)
  Pallas kernels  13.5 us (14%)
  waiting for transfers between devices  10.1 us (10%)
  local copies, waits for them, and re-layouts  3.33 us (3%)
    ppermute x8, starting transfers between devices, passed_along(): lax.ppermute(value, axis, [(source, source + steps) for source in range(f...  52.5 us
    all_to_all x2, starting transfers between devices, exchange(): return lax.all_to_all(pieces, 'slab', 0, 0, axis_index_groups=GROUPS)  16.9 us
    ppermute x8, waiting for transfers between devices, passed_along(): lax.ppermute(value, axis, [(source, source + steps) for source in range(f...  7.07 us
    all_to_all x2, waiting for transfers between devices, exchange(): return lax.all_to_all(pieces, 'slab', 0, 0, axis_index_groups=GROUPS)  3.05 us
    pallas_call x1, Pallas kernels, per_device(): call(first_votes, [(BINS + 1, LAYERS + 1) + layer], 12, [SMEM, VMEM])  2.98 us
    pallas_call x1, Pallas kernels, per_device(): call(second_votes, [(BINS + 1,) + block], 3, [SMEM, VMEM, VMEM, ANY])  2.9 us
  transfers between devices with their start and end apart: 11, of which 3 were waited for; matrix products, arithmetic and copies ran while one was open for 3% of the time, Pallas kernels for 13%

profile of v6, /device:TPU:35, one launch (start us, length us, event | category | flops | bytes accessed | tf_op | source)
XLA Modules:
  0.0 99.1 jit_solution(502811390776147421)
XLA Ops:
  0.6 6.9 %all-to-all-start = ((f32[16,8,8,128]{3,2,1,0:T(8,128)}), f32[16,8,8,128]{3,2,1,0:T(8,128)S(1)}, u32[]{:S(2)}, u32[]{:S(2)}) async-start(f32[16,8,8,128]{3,2,1,0:T(8,128)} %bitcast.8), calls=%async_computation | async-start | bytes 1048576 | tf_op jit(solution)/shard_map/all_to_all | solution.py:260
  7.6 1.0 slice.7
  8.5 3.1 %collective-permute-start.1 = (f32[8,1024]{1,0:T(8,128)S(1)}, f32[8,1024]{1,0:T(8,128)S(1)}, u32[]{:S(2)}, u32[]{:S(2)}) collective-permute-start(f32[8,1024]{1,0:T(8,128)S(1)} %bitcast.9), channel_id=1, source_target_pairs={{1,0},{2,1},{3,2},{4,3},{5,4},{6,5},{7,6},{8,7},{9,8},{10,9},{11,1... | collective-permute-start | bytes 98312 | tf_op jit(solution)/shard_map/ppermute | solution.py:253
  11.7 0.8 slice_bitcast_fusion
  12.5 16.6 %collective-permute-start = (f32[16,1024]{1,0:T(8,128)S(1)}, f32[16,1024]{1,0:T(8,128)S(1)}, u32[]{:S(2)}, u32[]{:S(2)}) collective-permute-start(f32[16,1024]{1,0:T(8,128)S(1)} %slice_bitcast_fusion), channel_id=1, source_target_pairs={{16,0},{32,16},{48,32},{64,48},{80,64},{96,80},{112,96},{128,112},... | collective-permute-start | bytes 196616 | tf_op jit(solution)/shard_map/ppermute | solution.py:253
  29.2 0.8 copy.9.visible
  30.0 0.0 copy-start.1
  30.0 0.0 all-to-all-done.spread
  30.0 0.0 copy-start.3
  30.0 0.7 copy-done.3
  30.7 0.0 copy-start.2
  30.7 0.6 pick.1.kept
  31.3 0.0 copy-start.4
  31.3 1.9 %collective-permute-start.4 = (f32[8,8,128]{2,1,0:T(8,128)S(1)}, f32[8,8,128]{2,1,0:T(8,128)S(1)}, u32[]{:S(2)}, u32[]{:S(2)}) collective-permute-start(f32[8,8,128]{2,1,0:T(8,128)S(1)} %pick.1.kept), channel_id=1, source_target_pairs={{0,16},{16,0},{32,48},{48,32},{64,80},{80,64},{96,112},{112,96},{1... | collective-permute-start | bytes 98312 | tf_op jit(solution)/shard_map/ppermute | solution.py:276
  33.2 0.0 collective-permute-done.1.ahead
  33.2 0.0 collective-permute-done.past.below
  33.2 0.0 copy-done.1
  33.2 0.0 copy-done.2
  33.2 0.6 all_duals.1
  33.8 4.5 %collective-permute-start.3 = (f32[8,1024]{1,0:T(8,128)S(1)}, f32[8,1024]{1,0:T(8,128)S(1)}, u32[]{:S(2)}, u32[]{:S(2)}) collective-permute-start(f32[8,1024]{1,0:T(8,128)S(1)} %get-tuple-element.20), channel_id=1, source_target_pairs={{0,1},{1,2},{2,3},{3,4},{4,5},{5,6},{6,7},{7,8},{8,9},{9,10},{10,1... | collective-permute-start | bytes 98312 | tf_op jit(solution)/shard_map/ppermute | solution.py:253
  38.3 10.7 %collective-permute-start.2 = (f32[16,1024]{1,0:T(8,128)S(1)}, f32[16,1024]{1,0:T(8,128)S(1)}, u32[]{:S(2)}, u32[]{:S(2)}) collective-permute-start(f32[16,1024]{1,0:T(8,128)S(1)} %get-tuple-element.19), channel_id=1, source_target_pairs={{0,16},{16,32},{32,48},{48,64},{64,80},{80,96},{96,112},{112,128},... | collective-permute-start | bytes 196616 | tf_op jit(solution)/shard_map/ppermute | solution.py:253
  49.0 0.0 collective-permute-done.4.across
  49.0 0.0 copy-done.4
  49.1 1.4 %copies_of.1 = f32[16,8,8,128]{3,2,1,0:T(8,128)} custom-call(s32[2]{0:T(128)S(1)} %copy-done.4, f32[8,8,128]{2,1,0:T(8,128)S(1)} %pick.1.kept, f32[8,8,128]{2,1,0:T(8,128)S(1)} %collective-permute-done.4.across), custom_call_target="tpu_custom_call" | custom-call | flops 1000000000 | bytes 3000000 | tf_op jit(solution)/shard_map/copies_of/pallas_call | solution.py:283
  50.5 9.9 %all-to-all-start.1 = ((f32[16,8,8,128]{3,2,1,0:T(8,128)}), f32[16,8,8,128]{3,2,1,0:T(8,128)S(1)}, u32[]{:S(2)}, u32[]{:S(2)}) async-start(f32[16,8,8,128]{3,2,1,0:T(8,128)} %copies_of.1), calls=%async_computation.1 | async-start | bytes 1048576 | tf_op jit(solution)/shard_map/all_to_all | solution.py:260
  60.4 0.0 collective-permute-done.3.before
  60.4 0.1 first_values.1
  60.5 4.0 %collective-permute-start.6 = (f32[16,1024]{1,0:T(8,128)S(1)}, f32[16,1024]{1,0:T(8,128)S(1)}, u32[]{:S(2)}, u32[]{:S(2)}) collective-permute-start(f32[16,1024]{1,0:T(8,128)S(1)} %first_values.1), channel_id=1, source_target_pairs={{16,0},{32,16},{48,32},{64,48},{80,64},{96,80},{112,96},{128,112},... | collective-permute-start | bytes 196616 | tf_op jit(solution)/shard_map/ppermute | solution.py:253
  64.5 0.0 collective-permute-done.2.above
  64.6 0.3 all_values.1.values
  64.9 3.0 %all-to-all-done.1.batches = f32[16,8,8,128]{3,2,1,0:T(8,128)S(1)} async-done(((f32[16,8,8,128]{3,2,1,0:T(8,128)}), f32[16,8,8,128]{3,2,1,0:T(8,128)S(1)}, u32[]{:S(2)}, u32[]{:S(2)}) %all-to-all-start.1) | async-done | bytes 524320 | tf_op jit(solution)/shard_map/all_to_all | solution.py:260
  67.9 3.0 %first_votes.1.tally = f32[9,9,16,1024]{3,2,1,0:T(8,128)S(1)} custom-call(s32[2,4,1]{2,1,0:T(4,128)S(1)} %copy.9.visible, f32[16,8,8,128]{3,2,1,0:T(8,128)S(1)} %all-to-all-done.1.batches), custom_call_target="tpu_custom_call" | custom-call | flops 12000000000 | bytes 36000000 | tf_op jit(solution)/shard_map/first_votes/pallas_call | solution.py:289
  70.9 0.5 first_update.1
  71.4 4.9 %collective-permute-start.5 = (f32[8,1024]{1,0:T(8,128)S(1)}, f32[8,1024]{1,0:T(8,128)S(1)}, u32[]{:S(2)}, u32[]{:S(2)}) collective-permute-start(f32[8,1024]{1,0:T(8,128)S(1)} %get-tuple-element.24), channel_id=1, source_target_pairs={{1,0},{2,1},{3,2},{4,3},{5,4},{6,5},{7,6},{8,7},{9,8},{10,9},{11,1... | collective-permute-start | bytes 98312 | tf_op jit(solution)/shard_map/ppermute | solution.py:253
  76.4 0.0 collective-permute-done.6.values
  76.4 0.1 past_update.1.past
  76.4 0.9 collective-permute-done.5.ahead
  77.4 0.1 top_dual.1.after
  77.5 6.2 %collective-permute-start.7 = (f32[16,1024]{1,0:T(8,128)S(1)}, f32[16,1024]{1,0:T(8,128)S(1)}, u32[]{:S(2)}, u32[]{:S(2)}) collective-permute-start(f32[16,1024]{1,0:T(8,128)S(1)} %top_dual.1.after), channel_id=1, source_target_pairs={{0,16},{16,32},{32,48},{48,64},{64,80},{80,96},{96,112},{112,128},... | collective-permute-start | bytes 196616 | tf_op jit(solution)/shard_map/ppermute | solution.py:253
  83.7 1.8 %second_duals.1 = (f32[3,8,16,1024]{3,2,1,0:T(8,128)}, f32[8,1024]{1,0:T(8,128)S(1)}) custom-call(f32[8,16,1024]{2,1,0:T(8,128)S(1)} %get-tuple-element.23.extra.field, f32[3,8,16,1024]{3,2,1,0:T(8,128)S(1)} %get-tuple-element.18.dual, f32[8,1024]{1,0:T(8,128)S(1)} %collective-permute-done.5.ahead, f32[16,1024]{1,0:T(8,128)S(1)} %past_update.1.past, ...), custom_call_target="tpu_custom_call" | custom-call | flops 1000000000 | bytes 3000000 | tf_op jit(solution)/shard_map/second_duals/pallas_call | solution.py:301
  85.5 0.0 copy-start
  85.5 2.3 %collective-permute-start.8 = (f32[8,1024]{1,0:T(8,128)S(1)}, f32[8,1024]{1,0:T(8,128)S(1)}, u32[]{:S(2)}, u32[]{:S(2)}) collective-permute-start(f32[8,1024]{1,0:T(8,128)S(1)} %get-tuple-element.27.after), channel_id=1, source_target_pairs={{0,1},{1,2},{2,3},{3,4},{4,5},{5,6},{6,7},{7,8},{8,9},{9,10},{10,1... | collective-permute-start | bytes 98312 | tf_op jit(solution)/shard_map/ppermute | solution.py:253
  87.8 2.9 %second_votes.1.tally = f32[9,8,16,1024]{3,2,1,0:T(8,128)S(1)} custom-call(s32[2,4,1]{2,1,0:T(4,128)S(1)} %copy.9.visible, f32[16,8,8,128]{3,2,1,0:T(8,128)S(1)} %all-to-all-done.1.batches, f32[9,9,16,1024]{3,2,1,0:T(8,128)S(1)} %first_votes.1.tally, f32[8,1024]{1,0:T(8,128)S(1)} %get-tuple-element.27.after), custom_call_target="tpu_custom_call" | custom-call | flops 3000000000 | bytes 9000000 | tf_op jit(solution)/shard_map/second_votes/pallas_call | solution.py:303
  90.7 0.0 collective-permute-done.8.before
  90.7 0.0 copy-done
  90.7 1.4 %last_layers.1.updated_in = f32[8,16,1024]{2,1,0:T(8,128)} custom-call(f32[8,16,1024]{2,1,0:T(8,128)S(1)} %get-tuple-element.22.current, f32[3,8,16,1024]{3,2,1,0:T(8,128)S(1)} %copy-done, f32[8,1024]{1,0:T(8,128)S(1)} %collective-permute-done.8.before, f32[9,8,16,1024]{3,2,1,0:T(8,128)S(1)} %second_votes.1.tally), custom_call_target="tpu_custom_call" | custom-call | flops 1000000000 | bytes 3000000 | tf_op jit(solution)/shard_map/last_layers/pallas_call | solution.py:304
  92.2 6.1 %collective-permute-done.7.above = f32[16,1024]{1,0:T(8,128)S(1)} collective-permute-done((f32[16,1024]{1,0:T(8,128)S(1)}, f32[16,1024]{1,0:T(8,128)S(1)}, u32[]{:S(2)}, u32[]{:S(2)}) %collective-permute-start.7) | collective-permute-done | bytes 65568 | tf_op jit(solution)/shard_map/ppermute | solution.py:253
  98.3 0.8 last_layer.1
  (1 shorter events, 0.0 us)
Async XLA Ops:
  0.6 29.3 %all-to-all-start = ((f32[16,8,8,128]{3,2,1,0:T(8,128)}), f32[16,8,8,128]{3,2,1,0:T(8,128)S(1)}, u32[]{:S(2)}, u32[]{:S(2)}) async-start(f32[16,8,8,128]{3,2,1,0:T(8,128)} %bitcast.8), calls=%async_computation | async-start | bytes 1048576 | tf_op jit(solution)/shard_map/all_to_all | solution.py:260
  8.5 24.7 %collective-permute-start.1 = (f32[8,1024]{1,0:T(8,128)S(1)}, f32[8,1024]{1,0:T(8,128)S(1)}, u32[]{:S(2)}, u32[]{:S(2)}) collective-permute-start(f32[8,1024]{1,0:T(8,128)S(1)} %bitcast.9), channel_id=1, source_target_pairs={{1,0},{2,1},{3,2},{4,3},{5,4},{6,5},{7,6},{8,7},{9,8},{10,9},{11,1... | collective-permute-start | bytes 98312 | tf_op jit(solution)/shard_map/ppermute | solution.py:253
  12.5 20.7 %collective-permute-start = (f32[16,1024]{1,0:T(8,128)S(1)}, f32[16,1024]{1,0:T(8,128)S(1)}, u32[]{:S(2)}, u32[]{:S(2)}) collective-permute-start(f32[16,1024]{1,0:T(8,128)S(1)} %slice_bitcast_fusion), channel_id=1, source_target_pairs={{16,0},{32,16},{48,32},{64,48},{80,64},{96,80},{112,96},{128,112},... | collective-permute-start | bytes 196616 | tf_op jit(solution)/shard_map/ppermute | solution.py:253
  30.0 3.3 %copy-start.1 = (f32[8,16,1024]{2,1,0:T(8,128)S(1)}, f32[8,16,1024]{2,1,0:T(8,128)}, u32[]{:S(2)}) copy-start(f32[8,16,1024]{2,1,0:T(8,128)} %field.7) | copy-start | bytes 1572868
  30.0 0.7 copy-start.3
  30.7 2.5 %copy-start.2 = (f32[3,8,16,1024]{3,2,1,0:T(8,128)S(1)}, f32[3,8,16,1024]{3,2,1,0:T(8,128)}, u32[]{:S(2)}) copy-start(f32[3,8,16,1024]{3,2,1,0:T(8,128)} %dual.1) | copy-start | bytes 4718596
  31.3 17.8 %copy-start.4 = (s32[2]{0:T(128)S(1)}, s32[2]{0:T(128)}, u32[]{:S(2)}) copy-start(s32[2]{0:T(128)} %owner.3) | copy-start | bytes 28
  31.3 17.8 %collective-permute-start.4 = (f32[8,8,128]{2,1,0:T(8,128)S(1)}, f32[8,8,128]{2,1,0:T(8,128)S(1)}, u32[]{:S(2)}, u32[]{:S(2)}) collective-permute-start(f32[8,8,128]{2,1,0:T(8,128)S(1)} %pick.1.kept), channel_id=1, source_target_pairs={{0,16},{16,0},{32,48},{48,32},{64,80},{80,64},{96,112},{112,96},{1... | collective-permute-start | bytes 98312 | tf_op jit(solution)/shard_map/ppermute | solution.py:276
  33.8 26.6 %collective-permute-start.3 = (f32[8,1024]{1,0:T(8,128)S(1)}, f32[8,1024]{1,0:T(8,128)S(1)}, u32[]{:S(2)}, u32[]{:S(2)}) collective-permute-start(f32[8,1024]{1,0:T(8,128)S(1)} %get-tuple-element.20), channel_id=1, source_target_pairs={{0,1},{1,2},{2,3},{3,4},{4,5},{5,6},{6,7},{7,8},{8,9},{9,10},{10,1... | collective-permute-start | bytes 98312 | tf_op jit(solution)/shard_map/ppermute | solution.py:253
  38.3 26.2 %collective-permute-start.2 = (f32[16,1024]{1,0:T(8,128)S(1)}, f32[16,1024]{1,0:T(8,128)S(1)}, u32[]{:S(2)}, u32[]{:S(2)}) collective-permute-start(f32[16,1024]{1,0:T(8,128)S(1)} %get-tuple-element.19), channel_id=1, source_target_pairs={{0,16},{16,32},{32,48},{48,64},{64,80},{80,96},{96,112},{112,128},... | collective-permute-start | bytes 196616 | tf_op jit(solution)/shard_map/ppermute | solution.py:253
  50.5 17.5 %all-to-all-start.1 = ((f32[16,8,8,128]{3,2,1,0:T(8,128)}), f32[16,8,8,128]{3,2,1,0:T(8,128)S(1)}, u32[]{:S(2)}, u32[]{:S(2)}) async-start(f32[16,8,8,128]{3,2,1,0:T(8,128)} %copies_of.1), calls=%async_computation.1 | async-start | bytes 1048576 | tf_op jit(solution)/shard_map/all_to_all | solution.py:260
  60.5 15.8 %collective-permute-start.6 = (f32[16,1024]{1,0:T(8,128)S(1)}, f32[16,1024]{1,0:T(8,128)S(1)}, u32[]{:S(2)}, u32[]{:S(2)}) collective-permute-start(f32[16,1024]{1,0:T(8,128)S(1)} %first_values.1), channel_id=1, source_target_pairs={{16,0},{32,16},{48,32},{64,48},{80,64},{96,80},{112,96},{128,112},... | collective-permute-start | bytes 196616 | tf_op jit(solution)/shard_map/ppermute | solution.py:253
  71.4 5.9 %collective-permute-start.5 = (f32[8,1024]{1,0:T(8,128)S(1)}, f32[8,1024]{1,0:T(8,128)S(1)}, u32[]{:S(2)}, u32[]{:S(2)}) collective-permute-start(f32[8,1024]{1,0:T(8,128)S(1)} %get-tuple-element.24), channel_id=1, source_target_pairs={{1,0},{2,1},{3,2},{4,3},{5,4},{6,5},{7,6},{8,7},{9,8},{10,9},{11,1... | collective-permute-start | bytes 98312 | tf_op jit(solution)/shard_map/ppermute | solution.py:253
  77.5 20.8 %collective-permute-start.7 = (f32[16,1024]{1,0:T(8,128)S(1)}, f32[16,1024]{1,0:T(8,128)S(1)}, u32[]{:S(2)}, u32[]{:S(2)}) collective-permute-start(f32[16,1024]{1,0:T(8,128)S(1)} %top_dual.1.after), channel_id=1, source_target_pairs={{0,16},{16,32},{32,48},{48,64},{64,80},{80,96},{96,112},{112,128},... | collective-permute-start | bytes 196616 | tf_op jit(solution)/shard_map/ppermute | solution.py:253
  85.5 5.2 %copy-start = (f32[3,8,16,1024]{3,2,1,0:T(8,128)S(1)}, f32[3,8,16,1024]{3,2,1,0:T(8,128)}, u32[]{:S(2)}) copy-start(f32[3,8,16,1024]{3,2,1,0:T(8,128)} %get-tuple-element.15.dual) | copy-start | bytes 4718596
  85.5 5.2 %collective-permute-start.8 = (f32[8,1024]{1,0:T(8,128)S(1)}, f32[8,1024]{1,0:T(8,128)S(1)}, u32[]{:S(2)}, u32[]{:S(2)}) collective-permute-start(f32[8,1024]{1,0:T(8,128)S(1)} %get-tuple-element.27.after), channel_id=1, source_target_pairs={{0,1},{1,2},{2,3},{3,4},{4,5},{5,6},{6,7},{7,8},{8,9},{9,10},{10,1... | collective-permute-start | bytes 98312 | tf_op jit(solution)/shard_map/ppermute | solution.py:253

commit v7 on v6

--- a/solution.py
+++ b/solution.py
@@ -78,12 +78,15 @@
     kept[...] = spread[lax.shift_right_logical(owner[lax.shift_right_logical(lax.axis_index("slab"), 4)], 1)]
 
 
-def copies_of(owner, kept, across, copies):
+def copies_of(owner, kept, across, copies, piece, sems):
     slab = lax.axis_index("slab")
     here = (owner[lax.shift_right_logical(slab, 4)] & 1) == (slab & 1)
-    piece = jnp.where(here, kept[...], across[...])
-    for place in range(16):
-        copies[place] = piece
+    piece[...] = jnp.where(here, kept[...], across[...])
+    moves = [pltpu.make_async_copy(piece, copies.at[place], sems.at[place]) for place in range(16)]
+    for move in moves:
+        move.start()
+    for move in moves:
+        move.wait()
 
 
 def all_duals(field, dual, ahead, past, new_dual, top, side):
@@ -184,7 +187,7 @@
 
 def first_votes(visible, batches, tally):
     base = slab_base()
-    caps = [STEP * visible[0, view, 0].astype(jnp.float32) for view in range(VIEWS)]
+    caps = [STEP * visible[0, 0, view].astype(jnp.float32) for view in range(VIEWS)]
 
     def body(index, carry):
         half, column, rows, lanes = block_of(index)
@@ -200,7 +203,7 @@
 
 def second_votes(visible, batches, tally, after, new_tally):
     base = slab_base()
-    caps = [STEP * visible[1, view, 0].astype(jnp.float32) for view in range(VIEWS)]
+    caps = [STEP * visible[1, 0, view].astype(jnp.float32) for view in range(VIEWS)]
 
     def body(index, carry):
         half, column, rows, lanes = block_of(index)
@@ -262,6 +265,8 @@
 
 def per_device(field, dual, depth, owner, visible):
     block = (LAYERS, ROWS, LANES)
+    owner = pltpu.with_memory_space_constraint(owner, pltpu.HBM)
+    visible = visible.transpose(0, 2, 1)
 
     first_one = pl.BlockSpec((1, ROWS, LANES), lambda step: (0, 0, 0))
     first_one_dual = pl.BlockSpec((3, 1, ROWS, LANES), lambda step: (0, 0, 0, 0))
@@ -271,16 +276,20 @@
     spread = exchange(pieces)
 
     below = passed_along(field[0], "slab", -1)
-    ahead = passed_along(field[:, 0], "tile", -1)
     (kept,) = call(pick, [(8, 8, 128)], 1, [SMEM, VMEM])(owner, spread)
+    first_rows, _ = lax.optimization_barrier((field[:, 0], kept))
+    ahead = passed_along(first_rows, "tile", -1)
     across = lax.ppermute(kept, "slab", [(index, index ^ 1) for index in range(32)])
-    below, ahead, _ = lax.optimization_barrier((below, ahead, kept))
+    across, below = lax.optimization_barrier((across, below))
+    (copies,) = call(
+        copies_of, [pieces.shape], 1, [SMEM, VMEM, VMEM], out_specs=(ANY,),
+        scratch_shapes=[pltpu.VMEM((8, 8, 128), jnp.float32), pltpu.SemaphoreType.DMA((16,))],
+    )(owner, kept, across)
+    ahead, _ = lax.optimization_barrier((ahead, copies))
     layer, rows = (ROWS, LANES), (LAYERS, LANES)
     dual, top, side = call(all_duals, [(3,) + block, layer, rows], 1, [VMEM] * 4)(field, dual, ahead, below)
     above = passed_along(top, "slab", 1)
     before = passed_along(side, "tile", 1)
-    across, top, side = lax.optimization_barrier((across, top, side))
-    (copies,) = call(copies_of, [pieces.shape], 1, [SMEM, VMEM, VMEM])(owner, kept, across)
     batches = exchange(copies)
     (values,) = call(first_values, [layer], 1, [VMEM] * 3)(field, dual, before)
     past_values = passed_along(values, "slab", -1)

time: 99.7 us -> 102 us (1.023)
  the two profiles are of different devices: /device:TPU:35 before, /device:TPU:37 now
where the time goes in v7:
time: 102 us
  starting transfers between devices  69 us (68%)
  waiting for transfers between devices  17.1 us (17%)
  Pallas kernels  13.7 us (13%)
    ppermute x8, starting transfers between devices, passed_along(): lax.ppermute(value, axis, [(source, source + steps) for source in range(f...  52.6 us
    ppermute x8, waiting for transfers between devices, passed_along(): lax.ppermute(value, axis, [(source, source + steps) for source in range(f...  13.3 us
    all_to_all x2, starting transfers between devices, exchange(): return lax.all_to_all(pieces, 'slab', 0, 0, axis_index_groups=GROUPS)  11.2 us
    ppermute x1, starting transfers between devices, per_device(): lax.ppermute(kept, 'slab', [(index, index ^ 1) for index in range(32)])  5.21 us
    ppermute x1, waiting for transfers between devices, per_device(): lax.ppermute(kept, 'slab', [(index, index ^ 1) for index in range(32)])  3.8 us
    pallas_call x1, Pallas kernels, per_device(): call(first_votes, [(BINS + 1, LAYERS + 1) + layer], 12, [SMEM, VMEM])  2.93 us
    pallas_call x1, Pallas kernels, per_device(): call(second_votes, [(BINS + 1,) + block], 3, [SMEM, VMEM, VMEM, ANY])  2.85 us
  transfers between devices with their start and end apart: 11, of which 4 were waited for; matrix products, arithmetic and copies ran while one was open for 1% of the time, Pallas kernels for 12%

profile of v7, /device:TPU:37, one launch (start us, length us, event | category | flops | bytes accessed | tf_op | source)
XLA Modules:
  0.0 101.5 jit_solution(16722703662192983942)
XLA Ops:
  0.6 6.9 %all-to-all-start = ((f32[16,8,8,128]{3,2,1,0:T(8,128)}), f32[16,8,8,128]{3,2,1,0:T(8,128)S(1)}, u32[]{:S(2)}, u32[]{:S(2)}) async-start(f32[16,8,8,128]{3,2,1,0:T(8,128)} %bitcast.13), calls=%async_computation | async-start | bytes 1048576 | tf_op jit(solution)/shard_map/all_to_all | solution.py:263
  7.5 0.8 slice_bitcast_fusion
  8.4 0.0 copy-start.1
  8.4 16.8 %collective-permute-start.2 = (f32[16,1024]{1,0:T(8,128)S(1)}, f32[16,1024]{1,0:T(8,128)S(1)}, u32[]{:S(2)}, u32[]{:S(2)}) collective-permute-start(f32[16,1024]{1,0:T(8,128)S(1)} %slice_bitcast_fusion), channel_id=1, source_target_pairs={{16,0},{32,16},{48,32},{64,48},{80,64},{96,80},{112,96},{128,112},... | collective-permute-start | bytes 196616 | tf_op jit(solution)/shard_map/ppermute | solution.py:256
  25.2 0.0 all-to-all-done.spread
  25.2 0.7 pick.1.kept
  25.9 5.2 %collective-permute-start.1 = (f32[8,8,128]{2,1,0:T(8,128)S(1)}, f32[8,8,128]{2,1,0:T(8,128)S(1)}, u32[]{:S(2)}, u32[]{:S(2)}) collective-permute-start(f32[8,8,128]{2,1,0:T(8,128)S(1)} %pick.1.kept), channel_id=1, source_target_pairs={{0,16},{16,0},{32,48},{48,32},{64,80},{80,64},{96,112},{112,96},{1... | collective-permute-start | bytes 98312 | tf_op jit(solution)/shard_map/ppermute | solution.py:282
  31.1 0.0 copy-done.1
  31.1 0.0 copy-start.2
  31.1 4.4 %collective-permute-start = (f32[8,1024]{1,0:T(8,128)S(1)}, f32[8,1024]{1,0:T(8,128)S(1)}, u32[]{:S(2)}, u32[]{:S(2)}) collective-permute-start(f32[8,1024]{1,0:T(8,128)S(1)} %bitcast.14), channel_id=1, source_target_pairs={{1,0},{2,1},{3,2},{4,3},{5,4},{6,5},{7,6},{8,7},{9,8},{10,9},{11,1... | collective-permute-start | bytes 98312 | tf_op jit(solution)/shard_map/ppermute | solution.py:256
  35.5 0.0 collective-permute-done.2.past.below
  35.5 3.8 %collective-permute-done.1.across = f32[8,8,128]{2,1,0:T(8,128)S(1)} collective-permute-done((f32[8,8,128]{2,1,0:T(8,128)S(1)}, f32[8,8,128]{2,1,0:T(8,128)S(1)}, u32[]{:S(2)}, u32[]{:S(2)}) %collective-permute-start.1) | collective-permute-done | bytes 32800 | tf_op jit(solution)/shard_map/ppermute | solution.py:282
  39.3 1.6 %copies_of.1 = f32[16,8,8,128]{3,2,1,0:T(8,128)} custom-call(s32[2]{0:T(128)} %owner.3, f32[8,8,128]{2,1,0:T(8,128)S(1)} %pick.1.kept, f32[8,8,128]{2,1,0:T(8,128)S(1)} %collective-permute-done.1.across), custom_call_target="tpu_custom_call" | custom-call | flops 1000000000 | bytes 3000000 | tf_op jit(solution)/shard_map/copies_of/pallas_call | solution.py:284
  40.9 0.0 collective-permute-done.ahead
  41.0 0.0 copy-done.2
  41.0 0.6 all_duals.1
  41.6 6.1 %collective-permute-start.4 = (f32[8,1024]{1,0:T(8,128)S(1)}, f32[8,1024]{1,0:T(8,128)S(1)}, u32[]{:S(2)}, u32[]{:S(2)}) collective-permute-start(f32[8,1024]{1,0:T(8,128)S(1)} %get-tuple-element.23), channel_id=1, source_target_pairs={{0,1},{1,2},{2,3},{3,4},{4,5},{5,6},{6,7},{7,8},{8,9},{9,10},{10,1... | collective-permute-start | bytes 98312 | tf_op jit(solution)/shard_map/ppermute | solution.py:256
  47.7 4.3 %all-to-all-start.1 = ((f32[16,8,8,128]{3,2,1,0:T(8,128)}), f32[16,8,8,128]{3,2,1,0:T(8,128)S(1)}, u32[]{:S(2)}, u32[]{:S(2)}) async-start(f32[16,8,8,128]{3,2,1,0:T(8,128)} %copies_of.1), calls=%async_computation.1 | async-start | bytes 1048576 | tf_op jit(solution)/shard_map/all_to_all | solution.py:263
  51.9 6.4 %collective-permute-start.3 = (f32[16,1024]{1,0:T(8,128)S(1)}, f32[16,1024]{1,0:T(8,128)S(1)}, u32[]{:S(2)}, u32[]{:S(2)}) collective-permute-start(f32[16,1024]{1,0:T(8,128)S(1)} %get-tuple-element.22), channel_id=1, source_target_pairs={{0,16},{16,32},{32,48},{48,64},{64,80},{80,96},{96,112},{112,128},... | collective-permute-start | bytes 196616 | tf_op jit(solution)/shard_map/ppermute | solution.py:256
  58.3 0.0 collective-permute-done.4.before
  58.3 0.1 first_values.1
  58.4 0.0 copy-start.3
  58.4 10.6 %collective-permute-start.6 = (f32[16,1024]{1,0:T(8,128)S(1)}, f32[16,1024]{1,0:T(8,128)S(1)}, u32[]{:S(2)}, u32[]{:S(2)}) collective-permute-start(f32[16,1024]{1,0:T(8,128)S(1)} %first_values.1), channel_id=1, source_target_pairs={{16,0},{32,16},{48,32},{64,48},{80,64},{96,80},{112,96},{128,112},... | collective-permute-start | bytes 196616 | tf_op jit(solution)/shard_map/ppermute | solution.py:256
  69.1 3.1 %collective-permute-done.3.above = f32[16,1024]{1,0:T(8,128)S(1)} collective-permute-done((f32[16,1024]{1,0:T(8,128)S(1)}, f32[16,1024]{1,0:T(8,128)S(1)}, u32[]{:S(2)}, u32[]{:S(2)}) %collective-permute-start.3) | collective-permute-done | bytes 65568 | tf_op jit(solution)/shard_map/ppermute | solution.py:256
  72.2 0.3 all_values.1.values
  72.5 0.0 all-to-all-done.1.batches
  72.5 0.0 copy-done.3
  72.5 2.9 %first_votes.1.tally = f32[9,9,16,1024]{3,2,1,0:T(8,128)S(1)} custom-call(s32[2,1,4]{2,1,0:T(1,128)S(1)} %bitcast.11, f32[16,8,8,128]{3,2,1,0:T(8,128)S(1)} %all-to-all-done.1.batches), custom_call_target="tpu_custom_call" | custom-call | flops 12000000000 | bytes 36000000 | tf_op jit(solution)/shard_map/first_votes/pallas_call | solution.py:298
  75.4 0.5 first_update.1
  76.0 2.5 %collective-permute-start.5 = (f32[8,1024]{1,0:T(8,128)S(1)}, f32[8,1024]{1,0:T(8,128)S(1)}, u32[]{:S(2)}, u32[]{:S(2)}) collective-permute-start(f32[8,1024]{1,0:T(8,128)S(1)} %get-tuple-element.26), channel_id=1, source_target_pairs={{1,0},{2,1},{3,2},{4,3},{5,4},{6,5},{7,6},{8,7},{9,8},{10,9},{11,1... | collective-permute-start | bytes 98312 | tf_op jit(solution)/shard_map/ppermute | solution.py:256
  78.5 0.0 collective-permute-done.6.values
  78.5 0.1 past_update.1.past
  78.6 4.0 %collective-permute-done.5.ahead = f32[8,1024]{1,0:T(8,128)S(1)} collective-permute-done((f32[8,1024]{1,0:T(8,128)S(1)}, f32[8,1024]{1,0:T(8,128)S(1)}, u32[]{:S(2)}, u32[]{:S(2)}) %collective-permute-start.5) | collective-permute-done | bytes 32800 | tf_op jit(solution)/shard_map/ppermute | solution.py:256
  82.5 0.1 top_dual.1.after
  82.6 2.9 %collective-permute-start.7 = (f32[16,1024]{1,0:T(8,128)S(1)}, f32[16,1024]{1,0:T(8,128)S(1)}, u32[]{:S(2)}, u32[]{:S(2)}) collective-permute-start(f32[16,1024]{1,0:T(8,128)S(1)} %top_dual.1.after), channel_id=1, source_target_pairs={{0,16},{16,32},{32,48},{48,64},{64,80},{80,96},{96,112},{112,128},... | collective-permute-start | bytes 196616 | tf_op jit(solution)/shard_map/ppermute | solution.py:256
  85.6 1.7 %second_duals.1 = (f32[3,8,16,1024]{3,2,1,0:T(8,128)}, f32[8,1024]{1,0:T(8,128)S(1)}) custom-call(f32[8,16,1024]{2,1,0:T(8,128)S(1)} %get-tuple-element.25.extra.field, f32[3,8,16,1024]{3,2,1,0:T(8,128)S(1)} %get-tuple-element.21.dual, f32[8,1024]{1,0:T(8,128)S(1)} %collective-permute-done.5.ahead, f32[16,1024]{1,0:T(8,128)S(1)} %past_update.1.past, ...), custom_call_target="tpu_custom_call" | custom-call | flops 1000000000 | bytes 3000000 | tf_op jit(solution)/shard_map/second_duals/pallas_call | solution.py:310
  87.3 0.0 copy-start
  87.3 3.0 %collective-permute-start.8 = (f32[8,1024]{1,0:T(8,128)S(1)}, f32[8,1024]{1,0:T(8,128)S(1)}, u32[]{:S(2)}, u32[]{:S(2)}) collective-permute-start(f32[8,1024]{1,0:T(8,128)S(1)} %get-tuple-element.29.after), channel_id=1, source_target_pairs={{0,1},{1,2},{2,3},{3,4},{4,5},{5,6},{6,7},{7,8},{8,9},{9,10},{10,1... | collective-permute-start | bytes 98312 | tf_op jit(solution)/shard_map/ppermute | solution.py:256
  90.3 2.9 %second_votes.1.tally = f32[9,8,16,1024]{3,2,1,0:T(8,128)S(1)} custom-call(s32[2,1,4]{2,1,0:T(1,128)S(1)} %bitcast.12, f32[16,8,8,128]{3,2,1,0:T(8,128)S(1)} %all-to-all-done.1.batches, f32[9,9,16,1024]{3,2,1,0:T(8,128)S(1)} %first_votes.1.tally, f32[8,1024]{1,0:T(8,128)S(1)} %get-tuple-element.29.after), custom_call_target="tpu_custom_call" | custom-call | flops 3000000000 | bytes 9000000 | tf_op jit(solution)/shard_map/second_votes/pallas_call | solution.py:312
  93.1 0.0 collective-permute-done.8.before
  93.1 0.0 copy-done
  93.1 1.4 %last_layers.1.updated_in = f32[8,16,1024]{2,1,0:T(8,128)} custom-call(f32[8,16,1024]{2,1,0:T(8,128)S(1)} %get-tuple-element.24.current, f32[3,8,16,1024]{3,2,1,0:T(8,128)S(1)} %copy-done, f32[8,1024]{1,0:T(8,128)S(1)} %collective-permute-done.8.before, f32[9,8,16,1024]{3,2,1,0:T(8,128)S(1)} %second_votes.1.tally), custom_call_target="tpu_custom_call" | custom-call | flops 1000000000 | bytes 3000000 | tf_op jit(solution)/shard_map/last_layers/pallas_call | solution.py:313
  94.6 6.2 %collective-permute-done.7.above = f32[16,1024]{1,0:T(8,128)S(1)} collective-permute-done((f32[16,1024]{1,0:T(8,128)S(1)}, f32[16,1024]{1,0:T(8,128)S(1)}, u32[]{:S(2)}, u32[]{:S(2)}) %collective-permute-start.7) | collective-permute-done | bytes 65568 | tf_op jit(solution)/shard_map/ppermute | solution.py:256
  100.8 0.8 last_layer.1
  (2 shorter events, 0.0 us)
Async XLA Ops:
  0.6 24.5 %all-to-all-start = ((f32[16,8,8,128]{3,2,1,0:T(8,128)}), f32[16,8,8,128]{3,2,1,0:T(8,128)S(1)}, u32[]{:S(2)}, u32[]{:S(2)}) async-start(f32[16,8,8,128]{3,2,1,0:T(8,128)} %bitcast.13), calls=%async_computation | async-start | bytes 1048576 | tf_op jit(solution)/shard_map/all_to_all | solution.py:263
  8.4 22.7 %copy-start.1 = (f32[8,16,1024]{2,1,0:T(8,128)S(1)}, f32[8,16,1024]{2,1,0:T(8,128)}, u32[]{:S(2)}) copy-start(f32[8,16,1024]{2,1,0:T(8,128)} %field.7) | copy-start | bytes 1572868
  8.4 27.2 %collective-permute-start.2 = (f32[16,1024]{1,0:T(8,128)S(1)}, f32[16,1024]{1,0:T(8,128)S(1)}, u32[]{:S(2)}, u32[]{:S(2)}) collective-permute-start(f32[16,1024]{1,0:T(8,128)S(1)} %slice_bitcast_fusion), channel_id=1, source_target_pairs={{16,0},{32,16},{48,32},{64,48},{80,64},{96,80},{112,96},{128,112},... | collective-permute-start | bytes 196616 | tf_op jit(solution)/shard_map/ppermute | solution.py:256
  25.9 13.5 %collective-permute-start.1 = (f32[8,8,128]{2,1,0:T(8,128)S(1)}, f32[8,8,128]{2,1,0:T(8,128)S(1)}, u32[]{:S(2)}, u32[]{:S(2)}) collective-permute-start(f32[8,8,128]{2,1,0:T(8,128)S(1)} %pick.1.kept), channel_id=1, source_target_pairs={{0,16},{16,0},{32,48},{48,32},{64,80},{80,64},{96,112},{112,96},{1... | collective-permute-start | bytes 98312 | tf_op jit(solution)/shard_map/ppermute | solution.py:282
  31.1 9.8 %copy-start.2 = (f32[3,8,16,1024]{3,2,1,0:T(8,128)S(1)}, f32[3,8,16,1024]{3,2,1,0:T(8,128)}, u32[]{:S(2)}) copy-start(f32[3,8,16,1024]{3,2,1,0:T(8,128)} %dual.1) | copy-start | bytes 4718596
  31.1 9.8 %collective-permute-start = (f32[8,1024]{1,0:T(8,128)S(1)}, f32[8,1024]{1,0:T(8,128)S(1)}, u32[]{:S(2)}, u32[]{:S(2)}) collective-permute-start(f32[8,1024]{1,0:T(8,128)S(1)} %bitcast.14), channel_id=1, source_target_pairs={{1,0},{2,1},{3,2},{4,3},{5,4},{6,5},{7,6},{8,7},{9,8},{10,9},{11,1... | collective-permute-start | bytes 98312 | tf_op jit(solution)/shard_map/ppermute | solution.py:256
  41.6 16.8 %collective-permute-start.4 = (f32[8,1024]{1,0:T(8,128)S(1)}, f32[8,1024]{1,0:T(8,128)S(1)}, u32[]{:S(2)}, u32[]{:S(2)}) collective-permute-start(f32[8,1024]{1,0:T(8,128)S(1)} %get-tuple-element.23), channel_id=1, source_target_pairs={{0,1},{1,2},{2,3},{3,4},{4,5},{5,6},{6,7},{7,8},{8,9},{9,10},{10,1... | collective-permute-start | bytes 98312 | tf_op jit(solution)/shard_map/ppermute | solution.py:256
  47.7 24.8 %all-to-all-start.1 = ((f32[16,8,8,128]{3,2,1,0:T(8,128)}), f32[16,8,8,128]{3,2,1,0:T(8,128)S(1)}, u32[]{:S(2)}, u32[]{:S(2)}) async-start(f32[16,8,8,128]{3,2,1,0:T(8,128)} %copies_of.1), calls=%async_computation.1 | async-start | bytes 1048576 | tf_op jit(solution)/shard_map/all_to_all | solution.py:263
  51.9 20.3 %collective-permute-start.3 = (f32[16,1024]{1,0:T(8,128)S(1)}, f32[16,1024]{1,0:T(8,128)S(1)}, u32[]{:S(2)}, u32[]{:S(2)}) collective-permute-start(f32[16,1024]{1,0:T(8,128)S(1)} %get-tuple-element.22), channel_id=1, source_target_pairs={{0,16},{16,32},{32,48},{48,64},{64,80},{80,96},{96,112},{112,128},... | collective-permute-start | bytes 196616 | tf_op jit(solution)/shard_map/ppermute | solution.py:256
  58.4 14.1 %copy-start.3 = (s32[2,4,1]{1,2,0:T(1,128)S(1)}, s32[2,4,1]{1,2,0:T(1,128)}, u32[]{:S(2)}) copy-start(s32[2,4,1]{1,2,0:T(1,128)} %param.9) | copy-start | bytes 100
  58.4 20.0 %collective-permute-start.6 = (f32[16,1024]{1,0:T(8,128)S(1)}, f32[16,1024]{1,0:T(8,128)S(1)}, u32[]{:S(2)}, u32[]{:S(2)}) collective-permute-start(f32[16,1024]{1,0:T(8,128)S(1)} %first_values.1), channel_id=1, source_target_pairs={{16,0},{32,16},{48,32},{64,48},{80,64},{96,80},{112,96},{128,112},... | collective-permute-start | bytes 196616 | tf_op jit(solution)/shard_map/ppermute | solution.py:256
  76.0 6.6 %collective-permute-start.5 = (f32[8,1024]{1,0:T(8,128)S(1)}, f32[8,1024]{1,0:T(8,128)S(1)}, u32[]{:S(2)}, u32[]{:S(2)}) collective-permute-start(f32[8,1024]{1,0:T(8,128)S(1)} %get-tuple-element.26), channel_id=1, source_target_pairs={{1,0},{2,1},{3,2},{4,3},{5,4},{6,5},{7,6},{8,7},{9,8},{10,9},{11,1... | collective-permute-start | bytes 98312 | tf_op jit(solution)/shard_map/ppermute | solution.py:256
  82.6 18.1 %collective-permute-start.7 = (f32[16,1024]{1,0:T(8,128)S(1)}, f32[16,1024]{1,0:T(8,128)S(1)}, u32[]{:S(2)}, u32[]{:S(2)}) collective-permute-start(f32[16,1024]{1,0:T(8,128)S(1)} %top_dual.1.after), channel_id=1, source_target_pairs={{0,16},{16,32},{32,48},{48,64},{64,80},{80,96},{96,112},{112,128},... | collective-permute-start | bytes 196616 | tf_op jit(solution)/shard_map/ppermute | solution.py:256
  87.3 5.8 %copy-start = (f32[3,8,16,1024]{3,2,1,0:T(8,128)S(1)}, f32[3,8,16,1024]{3,2,1,0:T(8,128)}, u32[]{:S(2)}) copy-start(f32[3,8,16,1024]{3,2,1,0:T(8,128)} %get-tuple-element.16.dual) | copy-start | bytes 4718596
  87.3 5.8 %collective-permute-start.8 = (f32[8,1024]{1,0:T(8,128)S(1)}, f32[8,1024]{1,0:T(8,128)S(1)}, u32[]{:S(2)}, u32[]{:S(2)}) collective-permute-start(f32[8,1024]{1,0:T(8,128)S(1)} %get-tuple-element.29.after), channel_id=1, source_target_pairs={{0,1},{1,2},{2,3},{3,4},{4,5},{5,6},{6,7},{7,8},{8,9},{9,10},{10,1... | collective-permute-start | bytes 98312 | tf_op jit(solution)/shard_map/ppermute | solution.py:256

commit v8 on v7

--- a/solution.py
+++ b/solution.py
@@ -89,17 +89,33 @@
         move.wait()
 
 
-def all_duals(field, dual, ahead, past, new_dual, top, side):
+def staged(field, first_layer, first_rows, field_here, sems):
+    moves = [
+        pltpu.make_async_copy(field.at[:, 0], first_rows, sems.at[0]),
+        pltpu.make_async_copy(field.at[0], first_layer, sems.at[1]),
+        pltpu.make_async_copy(field, field_here, sems.at[2]),
+    ]
+    for move in moves:
+        move.start()
+    for move in moves:
+        move.wait()
+
+
+def all_duals(field, given, ahead, past, new_dual, top, side, dual, sems):
+    moves = [pltpu.make_async_copy(given.at[:, layer], dual.at[layer], sems.at[layer]) for layer in range(LAYERS)]
+    for move in moves:
+        move.start()
     slab_end = lax.axis_index("slab") == Z_LAST
     for layer in range(LAYERS):
         last = layer == LAYERS - 1
+        moves[layer].wait()
         dual_z, dual_x, dual_y = dual_layer(
             field[layer],
             past[...] if last else field[layer + 1],
             ahead[layer : layer + 1, :],
-            dual[0, layer],
-            dual[1, layer],
-            dual[2, layer],
+            dual[layer, 0],
+            dual[layer, 1],
+            dual[layer, 2],
             slab_end if last else False,
         )
         new_dual[0, layer] = dual_z
@@ -232,13 +248,14 @@
 
 
 def past_update(below, values, dual, tally, extra):
-    extra[...] = 2.0 * counted(values[...] - 0.25 * dual[0, 0], tally, 0) - below[...]
+    extra[...] = 2.0 * counted(values[...] - 0.25 * dual[0, LAYERS - 1], tally, LAYERS) - below[...]
 
 
 def top_dual(extra, past, dual, ahead, top):
+    last = LAYERS - 1
     slab_end = lax.axis_index("slab") == Z_LAST
-    row = ahead[LAYERS - 1 : LAYERS, :]
-    top[...] = dual_layer(extra[0], past[...], row, dual[0, 0], dual[1, 0], dual[2, 0], slab_end)[0]
+    row = ahead[last:LAYERS, :]
+    top[...] = dual_layer(extra[last], past[...], row, dual[0, last], dual[1, last], dual[2, last], slab_end)[0]
 
 
 def last_layers(current, dual, before, tally, updated):
@@ -246,8 +263,11 @@
         updated[layer] = counted(stepped(current, dual, None, before, layer), tally, layer)
 
 
-def last_layer(current, dual, above, before, tally, updated_in, updated):
-    updated[0] = counted(stepped(current, dual, above, before, 0), tally, 0)
+def last_layer(current, dual, above, before, tally, updated_in, updated, layer, sem):
+    layer[...] = counted(stepped(current, dual, above, before, 0), tally, 0)
+    move = pltpu.make_async_copy(layer, updated.at[0], sem)
+    move.start()
+    move.wait()
 
 
 def passed_along(value, axis, steps):
@@ -268,28 +288,29 @@
     owner = pltpu.with_memory_space_constraint(owner, pltpu.HBM)
     visible = visible.transpose(0, 2, 1)
 
-    first_one = pl.BlockSpec((1, ROWS, LANES), lambda step: (0, 0, 0))
-    first_one_dual = pl.BlockSpec((3, 1, ROWS, LANES), lambda step: (0, 0, 0, 0))
-    tally_one = pl.BlockSpec((BINS + 1, 1, ROWS, LANES), lambda step: (0, 0, 0, 0))
-
     pieces = depth.reshape(16, 8, 8, 128).transpose(0, 2, 1, 3)
     spread = exchange(pieces)
 
-    below = passed_along(field[0], "slab", -1)
+    first_layer, first_rows, field = call(
+        staged, [(ROWS, LANES), (LAYERS, LANES), block], 1, [HBM], scratch_shapes=[pltpu.SemaphoreType.DMA((3,))]
+    )(pltpu.with_memory_space_constraint(field, pltpu.HBM))
+    below = passed_along(first_layer, "slab", -1)
+    ahead = passed_along(first_rows, "tile", -1)
     (kept,) = call(pick, [(8, 8, 128)], 1, [SMEM, VMEM])(owner, spread)
-    first_rows, _ = lax.optimization_barrier((field[:, 0], kept))
-    ahead = passed_along(first_rows, "tile", -1)
     across = lax.ppermute(kept, "slab", [(index, index ^ 1) for index in range(32)])
-    across, below = lax.optimization_barrier((across, below))
+    below, ahead, _ = lax.optimization_barrier((below, ahead, kept))
+    layer, rows = (ROWS, LANES), (LAYERS, LANES)
+    dual, top, side = call(
+        all_duals, [(3,) + block, layer, rows], 1, [VMEM, HBM, VMEM, VMEM],
+        scratch_shapes=[pltpu.VMEM((LAYERS, 3, ROWS, LANES), jnp.float32), pltpu.SemaphoreType.DMA((LAYERS,))],
+    )(field, pltpu.with_memory_space_constraint(dual, pltpu.HBM), ahead, below)
+    above = passed_along(top, "slab", 1)
+    before = passed_along(side, "tile", 1)
+    across, top, side = lax.optimization_barrier((across, top, side))
     (copies,) = call(
         copies_of, [pieces.shape], 1, [SMEM, VMEM, VMEM], out_specs=(ANY,),
         scratch_shapes=[pltpu.VMEM((8, 8, 128), jnp.float32), pltpu.SemaphoreType.DMA((16,))],
     )(owner, kept, across)
-    ahead, _ = lax.optimization_barrier((ahead, copies))
-    layer, rows = (ROWS, LANES), (LAYERS, LANES)
-    dual, top, side = call(all_duals, [(3,) + block, layer, rows], 1, [VMEM] * 4)(field, dual, ahead, below)
-    above = passed_along(top, "slab", 1)
-    before = passed_along(side, "tile", 1)
     batches = exchange(copies)
     (values,) = call(first_values, [layer], 1, [VMEM] * 3)(field, dual, before)
     past_values = passed_along(values, "slab", -1)
@@ -298,14 +319,9 @@
     (tally,) = call(first_votes, [(BINS + 1, LAYERS + 1) + layer], 12, [SMEM, VMEM])(visible, batches)
     current, extra, side = call(first_update, [block, block, rows], 1, [VMEM] * 3)(field, values, tally)
     ahead = passed_along(side, "tile", -1)
-    last_tally = pl.BlockSpec((BINS + 1, 1) + layer, lambda step: (0, LAYERS, 0, 0))
-    last_dual = pl.BlockSpec((3, 1) + layer, lambda step: (0, LAYERS - 1, 0, 0))
-    last_block = pl.BlockSpec((1,) + layer, lambda step: (LAYERS - 1, 0, 0))
     past_values, _ = lax.optimization_barrier((past_values, side))
-    (past,) = call(past_update, [layer], 1, [VMEM, VMEM, last_dual, last_tally], grid=(1,))(
-        below, past_values, dual, tally
-    )
-    (top,) = call(top_dual, [layer], 1, [last_block, VMEM, last_dual, VMEM], grid=(1,))(extra, past, dual, ahead)
+    (past,) = call(past_update, [layer], 1, [VMEM] * 4)(below, past_values, dual, tally)
+    (top,) = call(top_dual, [layer], 1, [VMEM] * 4)(extra, past, dual, ahead)
     above = passed_along(top, "slab", 1)
     dual, side = call(second_duals, [(3,) + block, rows], 1, [VMEM] * 4 + [ANY])(extra, dual, ahead, past, top)
     before = passed_along(side, "tile", 1)
@@ -313,8 +329,8 @@
     (rest,) = call(last_layers, [block], 1, [VMEM] * 4)(current, dual, before, tally)
     above, rest = lax.optimization_barrier((above, rest))
     (current,) = call(
-        last_layer, [block], 1, [first_one, first_one_dual, VMEM, VMEM, tally_one, ANY], grid=(1,),
-        out_specs=(first_one,), input_output_aliases={5: 0},
+        last_layer, [block], 1, [VMEM] * 5 + [ANY], out_specs=(ANY,), input_output_aliases={5: 0},
+        scratch_shapes=[pltpu.VMEM((ROWS, LANES), jnp.float32), pltpu.SemaphoreType.DMA],
     )(current, dual, above, before, tally, rest)
     return (current, dual)
 

time: 102 us -> 101 us (level)
  the two profiles are of different devices: /device:TPU:37 before, /device:TPU:38 now
where the time goes in v8:
time: 101 us; the launch traced here: 100 us
  starting transfers between devices  69.5 us (69%)
  Pallas kernels  16.3 us (16%)
  waiting for transfers between devices  13.6 us (13%)
    ppermute x8, starting transfers between devices, passed_along(): lax.ppermute(value, axis, [(source, source + steps) for source in range(f...  47.4 us
    all_to_all x2, starting transfers between devices, exchange(): return lax.all_to_all(pieces, 'slab', 0, 0, axis_index_groups=GROUPS)  18.1 us
    ppermute x8, waiting for transfers between devices, passed_along(): lax.ppermute(value, axis, [(source, source + steps) for source in range(f...  10 us
    ppermute x1, starting transfers between devices, per_device(): lax.ppermute(kept, 'slab', [(index, index ^ 1) for index in range(32)])  3.91 us
    all_to_all x2, waiting for transfers between devices, exchange(): return lax.all_to_all(pieces, 'slab', 0, 0, axis_index_groups=GROUPS)  3.56 us
    pallas_call x1, Pallas kernels, per_device(): call(first_votes, [(BINS + 1, LAYERS + 1) + layer], 12, [SMEM, VMEM])  2.93 us
    pallas_call x1, Pallas kernels, per_device(): call(second_votes, [(BINS + 1,) + block], 3, [SMEM, VMEM, VMEM, ANY])  2.85 us
    pallas_call x1, Pallas kernels, per_device(): call(all_duals, [(3,) + block, layer, rows], 1, [VMEM, HBM, VMEM, VMEM],...  2.02 us
  transfers between devices with their start and end apart: 11, of which 5 were waited for; matrix products, arithmetic and copies ran while one was open for 0% of the time, Pallas kernels for 15%

profile of v8, /device:TPU:38, one launch (start us, length us, event | category | flops | bytes accessed | tf_op | source)
XLA Modules:
  0.0 100.2 jit_solution(13985048096533562491)
XLA Ops:
  0.6 7.4 %all-to-all-start = ((f32[16,8,8,128]{3,2,1,0:T(8,128)}), f32[16,8,8,128]{3,2,1,0:T(8,128)S(1)}, u32[]{:S(2)}, u32[]{:S(2)}) async-start(f32[16,8,8,128]{3,2,1,0:T(8,128)} %bitcast.8), calls=%async_computation | async-start | bytes 1048576 | tf_op jit(solution)/shard_map/all_to_all | solution.py:283
  8.1 1.2 %staged.1 = (f32[16,1024]{1,0:T(8,128)S(1)}, f32[8,1024]{1,0:T(8,128)S(1)}, f32[8,16,1024]{2,1,0:T(8,128)S(1)}) custom-call(f32[8,16,1024]{2,1,0:T(8,128)} %field.1), custom_call_target="tpu_custom_call" | custom-call | flops 1000000000 | bytes 3000000 | tf_op jit(solution)/shard_map/staged/pallas_call | solution.py:294
  9.3 1.9 %collective-permute-start.1 = (f32[8,1024]{1,0:T(8,128)S(1)}, f32[8,1024]{1,0:T(8,128)S(1)}, u32[]{:S(2)}, u32[]{:S(2)}) collective-permute-start(f32[8,1024]{1,0:T(8,128)S(1)} %get-tuple-element.21), channel_id=1, source_target_pairs={{1,0},{2,1},{3,2},{4,3},{5,4},{6,5},{7,6},{8,7},{9,8},{10,9},{11,1... | collective-permute-start | bytes 98312 | tf_op jit(solution)/shard_map/ppermute | solution.py:276
  11.2 17.2 %collective-permute-start = (f32[16,1024]{1,0:T(8,128)S(1)}, f32[16,1024]{1,0:T(8,128)S(1)}, u32[]{:S(2)}, u32[]{:S(2)}) collective-permute-start(f32[16,1024]{1,0:T(8,128)S(1)} %get-tuple-element.20), channel_id=1, source_target_pairs={{16,0},{32,16},{48,32},{64,48},{80,64},{96,80},{112,96},{128,112},... | collective-permute-start | bytes 196616 | tf_op jit(solution)/shard_map/ppermute | solution.py:276
  28.4 0.0 all-to-all-done.spread
  28.4 0.7 pick.1.kept
  29.1 3.9 %collective-permute-start.4 = (f32[8,8,128]{2,1,0:T(8,128)S(1)}, f32[8,8,128]{2,1,0:T(8,128)S(1)}, u32[]{:S(2)}, u32[]{:S(2)}) collective-permute-start(f32[8,8,128]{2,1,0:T(8,128)S(1)} %pick.1.kept), channel_id=1, source_target_pairs={{0,16},{16,0},{32,48},{48,32},{64,80},{80,64},{96,112},{112,96},{1... | collective-permute-start | bytes 98312 | tf_op jit(solution)/shard_map/ppermute | solution.py:300
  33.0 0.0 collective-permute-done.1.ahead
  33.1 2.9 %collective-permute-done.past.below = f32[16,1024]{1,0:T(8,128)S(1)} collective-permute-done((f32[16,1024]{1,0:T(8,128)S(1)}, f32[16,1024]{1,0:T(8,128)S(1)}, u32[]{:S(2)}, u32[]{:S(2)}) %collective-permute-start) | collective-permute-done | bytes 65568 | tf_op jit(solution)/shard_map/ppermute | solution.py:276
  35.9 2.0 %all_duals.1 = (f32[3,8,16,1024]{3,2,1,0:T(8,128)S(1)}, f32[16,1024]{1,0:T(8,128)S(1)}, f32[8,1024]{1,0:T(8,128)S(1)}) custom-call(f32[8,16,1024]{2,1,0:T(8,128)S(1)} %get-tuple-element.19.field, f32[3,8,16,1024]{3,2,1,0:T(8,128)} %given.1, f32[8,1024]{1,0:T(8,128)S(1)} %collective-permute-done.1.ahead, f32[16,1024]{1,0:T(8,128)S(1)} %collective-permute-done.past.below), custom_call_target="tpu_custom_call" | custom-call | flops 1000000000 | bytes 3000000 | tf_op jit(solution)/shard_map/all_duals/pallas_call | solution.py:303
  38.0 1.9 %collective-permute-start.3 = (f32[8,1024]{1,0:T(8,128)S(1)}, f32[8,1024]{1,0:T(8,128)S(1)}, u32[]{:S(2)}, u32[]{:S(2)}) collective-permute-start(f32[8,1024]{1,0:T(8,128)S(1)} %get-tuple-element.26), channel_id=1, source_target_pairs={{0,1},{1,2},{2,3},{3,4},{4,5},{5,6},{6,7},{7,8},{8,9},{9,10},{10,1... | collective-permute-start | bytes 98312 | tf_op jit(solution)/shard_map/ppermute | solution.py:276
  39.9 10.8 %collective-permute-start.2 = (f32[16,1024]{1,0:T(8,128)S(1)}, f32[16,1024]{1,0:T(8,128)S(1)}, u32[]{:S(2)}, u32[]{:S(2)}) collective-permute-start(f32[16,1024]{1,0:T(8,128)S(1)} %get-tuple-element.25), channel_id=1, source_target_pairs={{0,16},{16,32},{32,48},{48,64},{64,80},{80,96},{96,112},{112,128},... | collective-permute-start | bytes 196616 | tf_op jit(solution)/shard_map/ppermute | solution.py:276
  50.7 0.0 collective-permute-done.4.across
  50.7 1.6 %copies_of.1 = f32[16,8,8,128]{3,2,1,0:T(8,128)} custom-call(s32[2]{0:T(128)} %owner.3, f32[8,8,128]{2,1,0:T(8,128)S(1)} %pick.1.kept, f32[8,8,128]{2,1,0:T(8,128)S(1)} %collective-permute-done.4.across), custom_call_target="tpu_custom_call" | custom-call | flops 1000000000 | bytes 3000000 | tf_op jit(solution)/shard_map/copies_of/pallas_call | solution.py:310
  52.3 10.7 %all-to-all-start.1 = ((f32[16,8,8,128]{3,2,1,0:T(8,128)}), f32[16,8,8,128]{3,2,1,0:T(8,128)S(1)}, u32[]{:S(2)}, u32[]{:S(2)}) async-start(f32[16,8,8,128]{3,2,1,0:T(8,128)} %copies_of.1), calls=%async_computation.1 | async-start | bytes 1048576 | tf_op jit(solution)/shard_map/all_to_all | solution.py:283
  63.0 0.0 collective-permute-done.3.before
  63.0 0.1 first_values.1
  63.1 0.0 copy-start.1
  63.1 4.3 %collective-permute-start.6 = (f32[16,1024]{1,0:T(8,128)S(1)}, f32[16,1024]{1,0:T(8,128)S(1)}, u32[]{:S(2)}, u32[]{:S(2)}) collective-permute-start(f32[16,1024]{1,0:T(8,128)S(1)} %first_values.1), channel_id=1, source_target_pairs={{16,0},{32,16},{48,32},{64,48},{80,64},{96,80},{112,96},{128,112},... | collective-permute-start | bytes 196616 | tf_op jit(solution)/shard_map/ppermute | solution.py:276
  67.4 0.0 collective-permute-done.2.above
  67.4 0.3 all_values.1.values
  67.7 3.6 %all-to-all-done.1.batches = f32[16,8,8,128]{3,2,1,0:T(8,128)S(1)} async-done(((f32[16,8,8,128]{3,2,1,0:T(8,128)}), f32[16,8,8,128]{3,2,1,0:T(8,128)S(1)}, u32[]{:S(2)}, u32[]{:S(2)}) %all-to-all-start.1) | async-done | bytes 524320 | tf_op jit(solution)/shard_map/all_to_all | solution.py:283
  71.3 0.0 copy-done.1
  71.3 2.9 %first_votes.1.tally = f32[9,9,16,1024]{3,2,1,0:T(8,128)S(1)} custom-call(s32[2,1,4]{2,1,0:T(1,128)S(1)} %bitcast.6, f32[16,8,8,128]{3,2,1,0:T(8,128)S(1)} %all-to-all-done.1.batches), custom_call_target="tpu_custom_call" | custom-call | flops 12000000000 | bytes 36000000 | tf_op jit(solution)/shard_map/first_votes/pallas_call | solution.py:319
  74.2 0.5 first_update.1
  74.7 1.9 %collective-permute-start.5 = (f32[8,1024]{1,0:T(8,128)S(1)}, f32[8,1024]{1,0:T(8,128)S(1)}, u32[]{:S(2)}, u32[]{:S(2)}) collective-permute-start(f32[8,1024]{1,0:T(8,128)S(1)} %get-tuple-element.30), channel_id=1, source_target_pairs={{1,0},{2,1},{3,2},{4,3},{5,4},{6,5},{7,6},{8,7},{9,8},{10,9},{11,1... | collective-permute-start | bytes 98312 | tf_op jit(solution)/shard_map/ppermute | solution.py:276
  76.7 1.5 %collective-permute-done.6.values = f32[16,1024]{1,0:T(8,128)S(1)} collective-permute-done((f32[16,1024]{1,0:T(8,128)S(1)}, f32[16,1024]{1,0:T(8,128)S(1)}, u32[]{:S(2)}, u32[]{:S(2)}) %collective-permute-start.6) | collective-permute-done | bytes 65568 | tf_op jit(solution)/shard_map/ppermute | solution.py:276
  78.1 0.1 past_update.1.past
  78.2 0.0 collective-permute-done.5.ahead
  78.2 0.1 top_dual.1.after
  78.4 7.3 %collective-permute-start.7 = (f32[16,1024]{1,0:T(8,128)S(1)}, f32[16,1024]{1,0:T(8,128)S(1)}, u32[]{:S(2)}, u32[]{:S(2)}) collective-permute-start(f32[16,1024]{1,0:T(8,128)S(1)} %top_dual.1.after), channel_id=1, source_target_pairs={{0,16},{16,32},{32,48},{48,64},{64,80},{80,96},{96,112},{112,128},... | collective-permute-start | bytes 196616 | tf_op jit(solution)/shard_map/ppermute | solution.py:276
  85.7 1.7 %second_duals.1 = (f32[3,8,16,1024]{3,2,1,0:T(8,128)}, f32[8,1024]{1,0:T(8,128)S(1)}) custom-call(f32[8,16,1024]{2,1,0:T(8,128)S(1)} %get-tuple-element.29.extra.field, f32[3,8,16,1024]{3,2,1,0:T(8,128)S(1)} %get-tuple-element.24.dual, f32[8,1024]{1,0:T(8,128)S(1)} %collective-permute-done.5.ahead, f32[16,1024]{1,0:T(8,128)S(1)} %past_update.1.past, ...), custom_call_target="tpu_custom_call" | custom-call | flops 1000000000 | bytes 3000000 | tf_op jit(solution)/shard_map/second_duals/pallas_call | solution.py:326
  87.4 0.0 copy-start
  87.4 2.0 %collective-permute-start.8 = (f32[8,1024]{1,0:T(8,128)S(1)}, f32[8,1024]{1,0:T(8,128)S(1)}, u32[]{:S(2)}, u32[]{:S(2)}) collective-permute-start(f32[8,1024]{1,0:T(8,128)S(1)} %get-tuple-element.33.after), channel_id=1, source_target_pairs={{0,1},{1,2},{2,3},{3,4},{4,5},{5,6},{6,7},{7,8},{8,9},{9,10},{10,1... | collective-permute-start | bytes 98312 | tf_op jit(solution)/shard_map/ppermute | solution.py:276
  89.4 2.9 %second_votes.1.tally = f32[9,8,16,1024]{3,2,1,0:T(8,128)S(1)} custom-call(s32[2,1,4]{2,1,0:T(1,128)S(1)} %bitcast.7, f32[16,8,8,128]{3,2,1,0:T(8,128)S(1)} %all-to-all-done.1.batches, f32[9,9,16,1024]{3,2,1,0:T(8,128)S(1)} %first_votes.1.tally, f32[8,1024]{1,0:T(8,128)S(1)} %get-tuple-element.33.after), custom_call_target="tpu_custom_call" | custom-call | flops 3000000000 | bytes 9000000 | tf_op jit(solution)/shard_map/second_votes/pallas_call | solution.py:328
  92.3 0.5 collective-permute-done.8.before
  92.8 0.0 copy-done
  92.8 1.4 %last_layers.1.updated_in = f32[8,16,1024]{2,1,0:T(8,128)} custom-call(f32[8,16,1024]{2,1,0:T(8,128)S(1)} %get-tuple-element.28.current, f32[3,8,16,1024]{3,2,1,0:T(8,128)S(1)} %copy-done, f32[8,1024]{1,0:T(8,128)S(1)} %collective-permute-done.8.before, f32[9,8,16,1024]{3,2,1,0:T(8,128)S(1)} %second_votes.1.tally), custom_call_target="tpu_custom_call" | custom-call | flops 1000000000 | bytes 3000000 | tf_op jit(solution)/shard_map/last_layers/pallas_call | solution.py:329
  94.2 5.2 %collective-permute-done.7.above = f32[16,1024]{1,0:T(8,128)S(1)} collective-permute-done((f32[16,1024]{1,0:T(8,128)S(1)}, f32[16,1024]{1,0:T(8,128)S(1)}, u32[]{:S(2)}, u32[]{:S(2)}) %collective-permute-start.7) | collective-permute-done | bytes 65568 | tf_op jit(solution)/shard_map/ppermute | solution.py:276
  99.4 0.8 last_layer.1
Async XLA Ops:
  0.6 27.8 %all-to-all-start = ((f32[16,8,8,128]{3,2,1,0:T(8,128)}), f32[16,8,8,128]{3,2,1,0:T(8,128)S(1)}, u32[]{:S(2)}, u32[]{:S(2)}) async-start(f32[16,8,8,128]{3,2,1,0:T(8,128)} %bitcast.8), calls=%async_computation | async-start | bytes 1048576 | tf_op jit(solution)/shard_map/all_to_all | solution.py:283
  9.3 23.8 %collective-permute-start.1 = (f32[8,1024]{1,0:T(8,128)S(1)}, f32[8,1024]{1,0:T(8,128)S(1)}, u32[]{:S(2)}, u32[]{:S(2)}) collective-permute-start(f32[8,1024]{1,0:T(8,128)S(1)} %get-tuple-element.21), channel_id=1, source_target_pairs={{1,0},{2,1},{3,2},{4,3},{5,4},{6,5},{7,6},{8,7},{9,8},{10,9},{11,1... | collective-permute-start | bytes 98312 | tf_op jit(solution)/shard_map/ppermute | solution.py:276
  11.2 24.7 %collective-permute-start = (f32[16,1024]{1,0:T(8,128)S(1)}, f32[16,1024]{1,0:T(8,128)S(1)}, u32[]{:S(2)}, u32[]{:S(2)}) collective-permute-start(f32[16,1024]{1,0:T(8,128)S(1)} %get-tuple-element.20), channel_id=1, source_target_pairs={{16,0},{32,16},{48,32},{64,48},{80,64},{96,80},{112,96},{128,112},... | collective-permute-start | bytes 196616 | tf_op jit(solution)/shard_map/ppermute | solution.py:276
  29.1 21.6 %collective-permute-start.4 = (f32[8,8,128]{2,1,0:T(8,128)S(1)}, f32[8,8,128]{2,1,0:T(8,128)S(1)}, u32[]{:S(2)}, u32[]{:S(2)}) collective-permute-start(f32[8,8,128]{2,1,0:T(8,128)S(1)} %pick.1.kept), channel_id=1, source_target_pairs={{0,16},{16,0},{32,48},{48,32},{64,80},{80,64},{96,112},{112,96},{1... | collective-permute-start | bytes 98312 | tf_op jit(solution)/shard_map/ppermute | solution.py:300
  38.0 25.0 %collective-permute-start.3 = (f32[8,1024]{1,0:T(8,128)S(1)}, f32[8,1024]{1,0:T(8,128)S(1)}, u32[]{:S(2)}, u32[]{:S(2)}) collective-permute-start(f32[8,1024]{1,0:T(8,128)S(1)} %get-tuple-element.26), channel_id=1, source_target_pairs={{0,1},{1,2},{2,3},{3,4},{4,5},{5,6},{6,7},{7,8},{8,9},{9,10},{10,1... | collective-permute-start | bytes 98312 | tf_op jit(solution)/shard_map/ppermute | solution.py:276
  39.9 27.5 %collective-permute-start.2 = (f32[16,1024]{1,0:T(8,128)S(1)}, f32[16,1024]{1,0:T(8,128)S(1)}, u32[]{:S(2)}, u32[]{:S(2)}) collective-permute-start(f32[16,1024]{1,0:T(8,128)S(1)} %get-tuple-element.25), channel_id=1, source_target_pairs={{0,16},{16,32},{32,48},{48,64},{64,80},{80,96},{96,112},{112,128},... | collective-permute-start | bytes 196616 | tf_op jit(solution)/shard_map/ppermute | solution.py:276
  52.3 19.0 %all-to-all-start.1 = ((f32[16,8,8,128]{3,2,1,0:T(8,128)}), f32[16,8,8,128]{3,2,1,0:T(8,128)S(1)}, u32[]{:S(2)}, u32[]{:S(2)}) async-start(f32[16,8,8,128]{3,2,1,0:T(8,128)} %copies_of.1), calls=%async_computation.1 | async-start | bytes 1048576 | tf_op jit(solution)/shard_map/all_to_all | solution.py:283
  63.1 8.2 %copy-start.1 = (s32[2,4,1]{1,2,0:T(1,128)S(1)}, s32[2,4,1]{1,2,0:T(1,128)}, u32[]{:S(2)}) copy-start(s32[2,4,1]{1,2,0:T(1,128)} %param.9) | copy-start | bytes 100
  63.1 15.0 %collective-permute-start.6 = (f32[16,1024]{1,0:T(8,128)S(1)}, f32[16,1024]{1,0:T(8,128)S(1)}, u32[]{:S(2)}, u32[]{:S(2)}) collective-permute-start(f32[16,1024]{1,0:T(8,128)S(1)} %first_values.1), channel_id=1, source_target_pairs={{16,0},{32,16},{48,32},{64,48},{80,64},{96,80},{112,96},{128,112},... | collective-permute-start | bytes 196616 | tf_op jit(solution)/shard_map/ppermute | solution.py:276
  74.7 3.5 %collective-permute-start.5 = (f32[8,1024]{1,0:T(8,128)S(1)}, f32[8,1024]{1,0:T(8,128)S(1)}, u32[]{:S(2)}, u32[]{:S(2)}) collective-permute-start(f32[8,1024]{1,0:T(8,128)S(1)} %get-tuple-element.30), channel_id=1, source_target_pairs={{1,0},{2,1},{3,2},{4,3},{5,4},{6,5},{7,6},{8,7},{9,8},{10,9},{11,1... | collective-permute-start | bytes 98312 | tf_op jit(solution)/shard_map/ppermute | solution.py:276
  78.4 21.0 %collective-permute-start.7 = (f32[16,1024]{1,0:T(8,128)S(1)}, f32[16,1024]{1,0:T(8,128)S(1)}, u32[]{:S(2)}, u32[]{:S(2)}) collective-permute-start(f32[16,1024]{1,0:T(8,128)S(1)} %top_dual.1.after), channel_id=1, source_target_pairs={{0,16},{16,32},{32,48},{48,64},{64,80},{80,96},{96,112},{112,128},... | collective-permute-start | bytes 196616 | tf_op jit(solution)/shard_map/ppermute | solution.py:276
  87.4 5.4 %copy-start = (f32[3,8,16,1024]{3,2,1,0:T(8,128)S(1)}, f32[3,8,16,1024]{3,2,1,0:T(8,128)}, u32[]{:S(2)}) copy-start(f32[3,8,16,1024]{3,2,1,0:T(8,128)} %get-tuple-element.18.dual) | copy-start | bytes 4718596
  87.4 5.4 %collective-permute-start.8 = (f32[8,1024]{1,0:T(8,128)S(1)}, f32[8,1024]{1,0:T(8,128)S(1)}, u32[]{:S(2)}, u32[]{:S(2)}) collective-permute-start(f32[8,1024]{1,0:T(8,128)S(1)} %get-tuple-element.33.after), channel_id=1, source_target_pairs={{0,1},{1,2},{2,3},{3,4},{4,5},{5,6},{6,7},{7,8},{8,9},{9,10},{10,1... | collective-permute-start | bytes 98312 | tf_op jit(solution)/shard_map/ppermute | solution.py:276

commit v9 on v8

--- a/solution.py
+++ b/solution.py
@@ -78,15 +78,12 @@
     kept[...] = spread[lax.shift_right_logical(owner[lax.shift_right_logical(lax.axis_index("slab"), 4)], 1)]
 
 
-def copies_of(owner, kept, across, copies, piece, sems):
+def copies_of(owner, kept, across, copies):
     slab = lax.axis_index("slab")
     here = (owner[lax.shift_right_logical(slab, 4)] & 1) == (slab & 1)
-    piece[...] = jnp.where(here, kept[...], across[...])
-    moves = [pltpu.make_async_copy(piece, copies.at[place], sems.at[place]) for place in range(16)]
-    for move in moves:
-        move.start()
-    for move in moves:
-        move.wait()
+    piece = jnp.where(here, kept[...], across[...])
+    for place in range(16):
+        copies[place] = piece
 
 
 def staged(field, first_layer, first_rows, field_here, sems):
@@ -101,21 +98,21 @@
         move.wait()
 
 
-def all_duals(field, given, ahead, past, new_dual, top, side, dual, sems):
-    moves = [pltpu.make_async_copy(given.at[:, layer], dual.at[layer], sems.at[layer]) for layer in range(LAYERS)]
-    for move in moves:
-        move.start()
+def relay(given, same):
+    same[...] = given[...]
+
+
+def all_duals(field, dual, ahead, past, new_dual, top, side):
     slab_end = lax.axis_index("slab") == Z_LAST
     for layer in range(LAYERS):
         last = layer == LAYERS - 1
-        moves[layer].wait()
         dual_z, dual_x, dual_y = dual_layer(
             field[layer],
             past[...] if last else field[layer + 1],
             ahead[layer : layer + 1, :],
-            dual[layer, 0],
-            dual[layer, 1],
-            dual[layer, 2],
+            dual[0, layer],
+            dual[1, layer],
+            dual[2, layer],
             slab_end if last else False,
         )
         new_dual[0, layer] = dual_z
@@ -295,22 +292,18 @@
         staged, [(ROWS, LANES), (LAYERS, LANES), block], 1, [HBM], scratch_shapes=[pltpu.SemaphoreType.DMA((3,))]
     )(pltpu.with_memory_space_constraint(field, pltpu.HBM))
     below = passed_along(first_layer, "slab", -1)
+    (kept,) = call(pick, [(8, 8, 128)], 1, [SMEM, VMEM])(owner, spread)
+    first_rows, _ = lax.optimization_barrier((first_rows, spread))
     ahead = passed_along(first_rows, "tile", -1)
-    (kept,) = call(pick, [(8, 8, 128)], 1, [SMEM, VMEM])(owner, spread)
     across = lax.ppermute(kept, "slab", [(index, index ^ 1) for index in range(32)])
-    below, ahead, _ = lax.optimization_barrier((below, ahead, kept))
+    below, _ = lax.optimization_barrier((below, kept))
+    (below,) = call(relay, [(ROWS, LANES)], 2, [VMEM])(below)
     layer, rows = (ROWS, LANES), (LAYERS, LANES)
-    dual, top, side = call(
-        all_duals, [(3,) + block, layer, rows], 1, [VMEM, HBM, VMEM, VMEM],
-        scratch_shapes=[pltpu.VMEM((LAYERS, 3, ROWS, LANES), jnp.float32), pltpu.SemaphoreType.DMA((LAYERS,))],
-    )(field, pltpu.with_memory_space_constraint(dual, pltpu.HBM), ahead, below)
+    dual, top, side = call(all_duals, [(3,) + block, layer, rows], 1, [VMEM] * 4)(field, dual, ahead, below)
     above = passed_along(top, "slab", 1)
     before = passed_along(side, "tile", 1)
     across, top, side = lax.optimization_barrier((across, top, side))
-    (copies,) = call(
-        copies_of, [pieces.shape], 1, [SMEM, VMEM, VMEM], out_specs=(ANY,),
-        scratch_shapes=[pltpu.VMEM((8, 8, 128), jnp.float32), pltpu.SemaphoreType.DMA((16,))],
-    )(owner, kept, across)
+    (copies,) = call(copies_of, [pieces.shape], 1, [SMEM, VMEM, VMEM])(owner, kept, across)
     batches = exchange(copies)
     (values,) = call(first_values, [layer], 1, [VMEM] * 3)(field, dual, before)
     past_values = passed_along(values, "slab", -1)

time: 101 us -> 98.4 us (0.974)
  waiting for transfers between devices: 13.6 us -> 7.93 us
  starting transfers between devices: 69.5 us -> 74.2 us
  Pallas kernels: 16.3 us -> 14.8 us
    ppermute x8, starting transfers between devices: 47.4 us -> 55.1 us  [passed_along(): lax.ppermute(value, axis, [(source, source + steps) for source in range(f...]
    all_to_all x2, starting transfers between devices: 18.1 us -> 13.3 us  [exchange(): return lax.all_to_all(pieces, 'slab', 0, 0, axis_index_groups=GROUPS)]
    all_to_all x2, waiting for transfers between devices: 3.56 us -> 0.01 us  [exchange(): return lax.all_to_all(pieces, 'slab', 0, 0, axis_index_groups=GROUPS)]
    ppermute x8, waiting for transfers between devices: 10 us -> 7.93 us  [passed_along(): lax.ppermute(value, axis, [(source, source + steps) for source in range(f...]
    ppermute x1, starting transfers between devices: 3.91 us -> 5.84 us  [per_device(): lax.ppermute(kept, 'slab', [(index, index ^ 1) for index in range(32)])]
    pallas_call x2 -> x3, Pallas kernels: 3.62 us -> 2.11 us  [the longest x1 1.53 us: per_device(): call(copies_of, [pieces.shape], 1, [SMEM, VMEM, VMEM])(owner, kept, across)]
  transfers between devices with their start and end apart: 11 -> 11, of which waited for: 5 -> 5; matrix products, arithmetic and copies ran while one was open for 0% -> 0% of each run, Pallas kernels for 15% -> 14%
where the time goes in v9:
time: 98.4 us; the launch traced here: 97.8 us
  starting transfers between devices  74.2 us (75%)
  Pallas kernels  14.8 us (15%)
  waiting for transfers between devices  7.93 us (8%)
    ppermute x8, starting transfers between devices, passed_along(): lax.ppermute(value, axis, [(source, source + steps) for source in range(f...  55.1 us
    all_to_all x2, starting transfers between devices, exchange(): return lax.all_to_all(pieces, 'slab', 0, 0, axis_index_groups=GROUPS)  13.3 us
    ppermute x8, waiting for transfers between devices, passed_along(): lax.ppermute(value, axis, [(source, source + steps) for source in range(f...  7.93 us
    ppermute x1, starting transfers between devices, per_device(): lax.ppermute(kept, 'slab', [(index, index ^ 1) for index in range(32)])  5.84 us
    pallas_call x1, Pallas kernels, per_device(): call(first_votes, [(BINS + 1, LAYERS + 1) + layer], 12, [SMEM, VMEM])  2.93 us
    pallas_call x1, Pallas kernels, per_device(): call(second_votes, [(BINS + 1,) + block], 3, [SMEM, VMEM, VMEM, ANY])  2.85 us
  transfers between devices with their start and end apart: 11, of which 5 were waited for; matrix products, arithmetic and copies ran while one was open for 0% of the time, Pallas kernels for 14%

profile of v9, /device:TPU:38, one launch (start us, length us, event | category | flops | bytes accessed | tf_op | source)
XLA Modules:
  0.0 97.8 jit_solution(4455315725454069263)
XLA Ops:
  0.6 7.4 %all-to-all-start = ((f32[16,8,8,128]{3,2,1,0:T(8,128)}), f32[16,8,8,128]{3,2,1,0:T(8,128)S(1)}, u32[]{:S(2)}, u32[]{:S(2)}) async-start(f32[16,8,8,128]{3,2,1,0:T(8,128)} %bitcast.8), calls=%async_computation | async-start | bytes 1048576 | tf_op jit(solution)/shard_map/all_to_all | solution.py:280
  8.1 1.2 %staged.1 = (f32[16,1024]{1,0:T(8,128)S(1)}, f32[8,1024]{1,0:T(8,128)S(1)}, f32[8,16,1024]{2,1,0:T(8,128)S(1)}) custom-call(f32[8,16,1024]{2,1,0:T(8,128)} %field.1), custom_call_target="tpu_custom_call" | custom-call | flops 1000000000 | bytes 3000000 | tf_op jit(solution)/shard_map/staged/pallas_call | solution.py:291
  9.3 17.2 %collective-permute-start.1 = (f32[16,1024]{1,0:T(8,128)S(1)}, f32[16,1024]{1,0:T(8,128)S(1)}, u32[]{:S(2)}, u32[]{:S(2)}) collective-permute-start(f32[16,1024]{1,0:T(8,128)S(1)} %get-tuple-element.22), channel_id=1, source_target_pairs={{16,0},{32,16},{48,32},{64,48},{80,64},{96,80},{112,96},{128,112},... | collective-permute-start | bytes 196616 | tf_op jit(solution)/shard_map/ppermute | solution.py:273
  26.5 0.0 all-to-all-done.spread
  26.5 0.7 pick.1.kept
  27.2 5.8 %collective-permute-start.4 = (f32[8,8,128]{2,1,0:T(8,128)S(1)}, f32[8,8,128]{2,1,0:T(8,128)S(1)}, u32[]{:S(2)}, u32[]{:S(2)}) collective-permute-start(f32[8,8,128]{2,1,0:T(8,128)S(1)} %pick.1.kept), channel_id=1, source_target_pairs={{0,16},{16,0},{32,48},{48,32},{64,80},{80,64},{96,112},{112,96},{1... | collective-permute-start | bytes 98312 | tf_op jit(solution)/shard_map/ppermute | solution.py:298
  33.0 0.0 copy-start.1
  33.1 2.1 %collective-permute-start = (f32[8,1024]{1,0:T(8,128)S(1)}, f32[8,1024]{1,0:T(8,128)S(1)}, u32[]{:S(2)}, u32[]{:S(2)}) collective-permute-start(f32[8,1024]{1,0:T(8,128)S(1)} %get-tuple-element.21), channel_id=1, source_target_pairs={{1,0},{2,1},{3,2},{4,3},{5,4},{6,5},{7,6},{8,7},{9,8},{10,9},{11,1... | collective-permute-start | bytes 98312 | tf_op jit(solution)/shard_map/ppermute | solution.py:273
  35.1 0.0 collective-permute-done.1.given
  35.1 1.6 %collective-permute-done.ahead = f32[8,1024]{1,0:T(8,128)S(1)} collective-permute-done((f32[8,1024]{1,0:T(8,128)S(1)}, f32[8,1024]{1,0:T(8,128)S(1)}, u32[]{:S(2)}, u32[]{:S(2)}) %collective-permute-start) | collective-permute-done | bytes 32800 | tf_op jit(solution)/shard_map/ppermute | solution.py:273
  36.7 0.0 copy-done.1
  36.7 0.6 all_duals.1
  37.3 3.7 %collective-permute-start.3 = (f32[8,1024]{1,0:T(8,128)S(1)}, f32[8,1024]{1,0:T(8,128)S(1)}, u32[]{:S(2)}, u32[]{:S(2)}) collective-permute-start(f32[8,1024]{1,0:T(8,128)S(1)} %get-tuple-element.26), channel_id=1, source_target_pairs={{0,1},{1,2},{2,3},{3,4},{4,5},{5,6},{6,7},{7,8},{8,9},{9,10},{10,1... | collective-permute-start | bytes 98312 | tf_op jit(solution)/shard_map/ppermute | solution.py:273
  41.0 8.4 %collective-permute-start.2 = (f32[16,1024]{1,0:T(8,128)S(1)}, f32[16,1024]{1,0:T(8,128)S(1)}, u32[]{:S(2)}, u32[]{:S(2)}) collective-permute-start(f32[16,1024]{1,0:T(8,128)S(1)} %get-tuple-element.25), channel_id=1, source_target_pairs={{0,16},{16,32},{32,48},{48,64},{64,80},{80,96},{96,112},{112,128},... | collective-permute-start | bytes 196616 | tf_op jit(solution)/shard_map/ppermute | solution.py:273
  49.3 0.0 collective-permute-done.4.across
  49.4 1.5 %copies_of.1 = f32[16,8,8,128]{3,2,1,0:T(8,128)} custom-call(s32[2]{0:T(128)} %owner.3, f32[8,8,128]{2,1,0:T(8,128)S(1)} %pick.1.kept, f32[8,8,128]{2,1,0:T(8,128)S(1)} %collective-permute-done.4.across), custom_call_target="tpu_custom_call" | custom-call | flops 1000000000 | bytes 3000000 | tf_op jit(solution)/shard_map/copies_of/pallas_call | solution.py:306
  50.9 5.8 %all-to-all-start.1 = ((f32[16,8,8,128]{3,2,1,0:T(8,128)}), f32[16,8,8,128]{3,2,1,0:T(8,128)S(1)}, u32[]{:S(2)}, u32[]{:S(2)}) async-start(f32[16,8,8,128]{3,2,1,0:T(8,128)} %copies_of.1), calls=%async_computation.1 | async-start | bytes 1048576 | tf_op jit(solution)/shard_map/all_to_all | solution.py:280
  56.7 0.0 collective-permute-done.3.before
  56.7 0.1 first_values.1
  56.8 0.0 copy-start.2
  56.8 10.3 %collective-permute-start.6 = (f32[16,1024]{1,0:T(8,128)S(1)}, f32[16,1024]{1,0:T(8,128)S(1)}, u32[]{:S(2)}, u32[]{:S(2)}) collective-permute-start(f32[16,1024]{1,0:T(8,128)S(1)} %first_values.1), channel_id=1, source_target_pairs={{16,0},{32,16},{48,32},{64,48},{80,64},{96,80},{112,96},{128,112},... | collective-permute-start | bytes 196616 | tf_op jit(solution)/shard_map/ppermute | solution.py:273
  67.1 0.0 collective-permute-done.2.above
  67.1 0.3 all_values.1.values
  67.4 0.0 all-to-all-done.1.batches
  67.4 0.0 copy-done.2
  67.4 2.9 %first_votes.1.tally = f32[9,9,16,1024]{3,2,1,0:T(8,128)S(1)} custom-call(s32[2,1,4]{2,1,0:T(1,128)S(1)} %bitcast.6, f32[16,8,8,128]{3,2,1,0:T(8,128)S(1)} %all-to-all-done.1.batches), custom_call_target="tpu_custom_call" | custom-call | flops 12000000000 | bytes 36000000 | tf_op jit(solution)/shard_map/first_votes/pallas_call | solution.py:312
  70.4 0.5 first_update.1
  70.9 2.0 %collective-permute-start.5 = (f32[8,1024]{1,0:T(8,128)S(1)}, f32[8,1024]{1,0:T(8,128)S(1)}, u32[]{:S(2)}, u32[]{:S(2)}) collective-permute-start(f32[8,1024]{1,0:T(8,128)S(1)} %get-tuple-element.30), channel_id=1, source_target_pairs={{1,0},{2,1},{3,2},{4,3},{5,4},{6,5},{7,6},{8,7},{9,8},{10,9},{11,1... | collective-permute-start | bytes 98312 | tf_op jit(solution)/shard_map/ppermute | solution.py:273
  72.9 1.4 %collective-permute-done.6.values = f32[16,1024]{1,0:T(8,128)S(1)} collective-permute-done((f32[16,1024]{1,0:T(8,128)S(1)}, f32[16,1024]{1,0:T(8,128)S(1)}, u32[]{:S(2)}, u32[]{:S(2)}) %collective-permute-start.6) | collective-permute-done | bytes 65568 | tf_op jit(solution)/shard_map/ppermute | solution.py:273
  74.2 0.1 past_update.1.past
  74.3 0.1 collective-permute-done.5.ahead
  74.4 0.1 top_dual.1.after
  74.6 9.5 %collective-permute-start.7 = (f32[16,1024]{1,0:T(8,128)S(1)}, f32[16,1024]{1,0:T(8,128)S(1)}, u32[]{:S(2)}, u32[]{:S(2)}) collective-permute-start(f32[16,1024]{1,0:T(8,128)S(1)} %top_dual.1.after), channel_id=1, source_target_pairs={{0,16},{16,32},{32,48},{48,64},{64,80},{80,96},{96,112},{112,128},... | collective-permute-start | bytes 196616 | tf_op jit(solution)/shard_map/ppermute | solution.py:273
  84.0 1.7 %second_duals.1 = (f32[3,8,16,1024]{3,2,1,0:T(8,128)}, f32[8,1024]{1,0:T(8,128)S(1)}) custom-call(f32[8,16,1024]{2,1,0:T(8,128)S(1)} %get-tuple-element.29.extra.field, f32[3,8,16,1024]{3,2,1,0:T(8,128)S(1)} %get-tuple-element.24.dual, f32[8,1024]{1,0:T(8,128)S(1)} %collective-permute-done.5.ahead, f32[16,1024]{1,0:T(8,128)S(1)} %past_update.1.past, ...), custom_call_target="tpu_custom_call" | custom-call | flops 1000000000 | bytes 3000000 | tf_op jit(solution)/shard_map/second_duals/pallas_call | solution.py:319
  85.8 0.0 copy-start
  85.8 2.0 %collective-permute-start.8 = (f32[8,1024]{1,0:T(8,128)S(1)}, f32[8,1024]{1,0:T(8,128)S(1)}, u32[]{:S(2)}, u32[]{:S(2)}) collective-permute-start(f32[8,1024]{1,0:T(8,128)S(1)} %get-tuple-element.33.after), channel_id=1, source_target_pairs={{0,1},{1,2},{2,3},{3,4},{4,5},{5,6},{6,7},{7,8},{8,9},{9,10},{10,1... | collective-permute-start | bytes 98312 | tf_op jit(solution)/shard_map/ppermute | solution.py:273
  87.8 2.9 %second_votes.1.tally = f32[9,8,16,1024]{3,2,1,0:T(8,128)S(1)} custom-call(s32[2,1,4]{2,1,0:T(1,128)S(1)} %bitcast.7, f32[16,8,8,128]{3,2,1,0:T(8,128)S(1)} %all-to-all-done.1.batches, f32[9,9,16,1024]{3,2,1,0:T(8,128)S(1)} %first_votes.1.tally, f32[8,1024]{1,0:T(8,128)S(1)} %get-tuple-element.33.after), custom_call_target="tpu_custom_call" | custom-call | flops 3000000000 | bytes 9000000 | tf_op jit(solution)/shard_map/second_votes/pallas_call | solution.py:321
  90.7 0.4 collective-permute-done.8.before
  91.1 0.0 copy-done
  91.1 1.4 %last_layers.1.updated_in = f32[8,16,1024]{2,1,0:T(8,128)} custom-call(f32[8,16,1024]{2,1,0:T(8,128)S(1)} %get-tuple-element.28.current, f32[3,8,16,1024]{3,2,1,0:T(8,128)S(1)} %copy-done, f32[8,1024]{1,0:T(8,128)S(1)} %collective-permute-done.8.before, f32[9,8,16,1024]{3,2,1,0:T(8,128)S(1)} %second_votes.1.tally), custom_call_target="tpu_custom_call" | custom-call | flops 1000000000 | bytes 3000000 | tf_op jit(solution)/shard_map/last_layers/pallas_call | solution.py:322
  92.6 4.4 %collective-permute-done.7.above = f32[16,1024]{1,0:T(8,128)S(1)} collective-permute-done((f32[16,1024]{1,0:T(8,128)S(1)}, f32[16,1024]{1,0:T(8,128)S(1)}, u32[]{:S(2)}, u32[]{:S(2)}) %collective-permute-start.7) | collective-permute-done | bytes 65568 | tf_op jit(solution)/shard_map/ppermute | solution.py:273
  97.0 0.8 last_layer.1
  (1 shorter events, 0.0 us)
Async XLA Ops:
  0.6 25.9 %all-to-all-start = ((f32[16,8,8,128]{3,2,1,0:T(8,128)}), f32[16,8,8,128]{3,2,1,0:T(8,128)S(1)}, u32[]{:S(2)}, u32[]{:S(2)}) async-start(f32[16,8,8,128]{3,2,1,0:T(8,128)} %bitcast.8), calls=%async_computation | async-start | bytes 1048576 | tf_op jit(solution)/shard_map/all_to_all | solution.py:280
  9.3 25.9 %collective-permute-start.1 = (f32[16,1024]{1,0:T(8,128)S(1)}, f32[16,1024]{1,0:T(8,128)S(1)}, u32[]{:S(2)}, u32[]{:S(2)}) collective-permute-start(f32[16,1024]{1,0:T(8,128)S(1)} %get-tuple-element.22), channel_id=1, source_target_pairs={{16,0},{32,16},{48,32},{64,48},{80,64},{96,80},{112,96},{128,112},... | collective-permute-start | bytes 196616 | tf_op jit(solution)/shard_map/ppermute | solution.py:273
  27.2 22.2 %collective-permute-start.4 = (f32[8,8,128]{2,1,0:T(8,128)S(1)}, f32[8,8,128]{2,1,0:T(8,128)S(1)}, u32[]{:S(2)}, u32[]{:S(2)}) collective-permute-start(f32[8,8,128]{2,1,0:T(8,128)S(1)} %pick.1.kept), channel_id=1, source_target_pairs={{0,16},{16,0},{32,48},{48,32},{64,80},{80,64},{96,112},{112,96},{1... | collective-permute-start | bytes 98312 | tf_op jit(solution)/shard_map/ppermute | solution.py:298
  33.0 3.7 %copy-start.1 = (f32[3,8,16,1024]{3,2,1,0:T(8,128)S(1)}, f32[3,8,16,1024]{3,2,1,0:T(8,128)}, u32[]{:S(2)}) copy-start(f32[3,8,16,1024]{3,2,1,0:T(8,128)} %dual.1) | copy-start | bytes 4718596
  33.1 3.6 %collective-permute-start = (f32[8,1024]{1,0:T(8,128)S(1)}, f32[8,1024]{1,0:T(8,128)S(1)}, u32[]{:S(2)}, u32[]{:S(2)}) collective-permute-start(f32[8,1024]{1,0:T(8,128)S(1)} %get-tuple-element.21), channel_id=1, source_target_pairs={{1,0},{2,1},{3,2},{4,3},{5,4},{6,5},{7,6},{8,7},{9,8},{10,9},{11,1... | collective-permute-start | bytes 98312 | tf_op jit(solution)/shard_map/ppermute | solution.py:273
  37.3 19.4 %collective-permute-start.3 = (f32[8,1024]{1,0:T(8,128)S(1)}, f32[8,1024]{1,0:T(8,128)S(1)}, u32[]{:S(2)}, u32[]{:S(2)}) collective-permute-start(f32[8,1024]{1,0:T(8,128)S(1)} %get-tuple-element.26), channel_id=1, source_target_pairs={{0,1},{1,2},{2,3},{3,4},{4,5},{5,6},{6,7},{7,8},{8,9},{9,10},{10,1... | collective-permute-start | bytes 98312 | tf_op jit(solution)/shard_map/ppermute | solution.py:273
  41.0 26.2 %collective-permute-start.2 = (f32[16,1024]{1,0:T(8,128)S(1)}, f32[16,1024]{1,0:T(8,128)S(1)}, u32[]{:S(2)}, u32[]{:S(2)}) collective-permute-start(f32[16,1024]{1,0:T(8,128)S(1)} %get-tuple-element.25), channel_id=1, source_target_pairs={{0,16},{16,32},{32,48},{48,64},{64,80},{80,96},{96,112},{112,128},... | collective-permute-start | bytes 196616 | tf_op jit(solution)/shard_map/ppermute | solution.py:273
  50.9 16.5 %all-to-all-start.1 = ((f32[16,8,8,128]{3,2,1,0:T(8,128)}), f32[16,8,8,128]{3,2,1,0:T(8,128)S(1)}, u32[]{:S(2)}, u32[]{:S(2)}) async-start(f32[16,8,8,128]{3,2,1,0:T(8,128)} %copies_of.1), calls=%async_computation.1 | async-start | bytes 1048576 | tf_op jit(solution)/shard_map/all_to_all | solution.py:280
  56.8 10.6 %copy-start.2 = (s32[2,4,1]{1,2,0:T(1,128)S(1)}, s32[2,4,1]{1,2,0:T(1,128)}, u32[]{:S(2)}) copy-start(s32[2,4,1]{1,2,0:T(1,128)} %param.9) | copy-start | bytes 100
  56.8 17.4 %collective-permute-start.6 = (f32[16,1024]{1,0:T(8,128)S(1)}, f32[16,1024]{1,0:T(8,128)S(1)}, u32[]{:S(2)}, u32[]{:S(2)}) collective-permute-start(f32[16,1024]{1,0:T(8,128)S(1)} %first_values.1), channel_id=1, source_target_pairs={{16,0},{32,16},{48,32},{64,48},{80,64},{96,80},{112,96},{128,112},... | collective-permute-start | bytes 196616 | tf_op jit(solution)/shard_map/ppermute | solution.py:273
  70.9 3.5 %collective-permute-start.5 = (f32[8,1024]{1,0:T(8,128)S(1)}, f32[8,1024]{1,0:T(8,128)S(1)}, u32[]{:S(2)}, u32[]{:S(2)}) collective-permute-start(f32[8,1024]{1,0:T(8,128)S(1)} %get-tuple-element.30), channel_id=1, source_target_pairs={{1,0},{2,1},{3,2},{4,3},{5,4},{6,5},{7,6},{8,7},{9,8},{10,9},{11,1... | collective-permute-start | bytes 98312 | tf_op jit(solution)/shard_map/ppermute | solution.py:273
  74.6 22.4 %collective-permute-start.7 = (f32[16,1024]{1,0:T(8,128)S(1)}, f32[16,1024]{1,0:T(8,128)S(1)}, u32[]{:S(2)}, u32[]{:S(2)}) collective-permute-start(f32[16,1024]{1,0:T(8,128)S(1)} %top_dual.1.after), channel_id=1, source_target_pairs={{0,16},{16,32},{32,48},{48,64},{64,80},{80,96},{96,112},{112,128},... | collective-permute-start | bytes 196616 | tf_op jit(solution)/shard_map/ppermute | solution.py:273
  85.8 5.4 %copy-start = (f32[3,8,16,1024]{3,2,1,0:T(8,128)S(1)}, f32[3,8,16,1024]{3,2,1,0:T(8,128)}, u32[]{:S(2)}) copy-start(f32[3,8,16,1024]{3,2,1,0:T(8,128)} %get-tuple-element.18.dual) | copy-start | bytes 4718596
  85.8 5.4 %collective-permute-start.8 = (f32[8,1024]{1,0:T(8,128)S(1)}, f32[8,1024]{1,0:T(8,128)S(1)}, u32[]{:S(2)}, u32[]{:S(2)}) collective-permute-start(f32[8,1024]{1,0:T(8,128)S(1)} %get-tuple-element.33.after), channel_id=1, source_target_pairs={{0,1},{1,2},{2,3},{3,4},{4,5},{5,6},{6,7},{7,8},{8,9},{9,10},{10,1... | collective-permute-start | bytes 98312 | tf_op jit(solution)/shard_map/ppermute | solution.py:273

commit v10 on v9

--- a/solution.py
+++ b/solution.py
@@ -123,13 +123,13 @@
             top[...] = dual_z
 
 
-def second_duals(field, dual, ahead, past, after, new_dual, side):
+def second_duals(low, high, dual, ahead, past, after, new_dual, side):
     slab_end = lax.axis_index("slab") == Z_LAST
     for layer in range(LAYERS):
         last = layer == LAYERS - 1
         dual_z, dual_x, dual_y = dual_layer(
-            field[layer],
-            past[...] if last else field[layer + 1],
+            joined(low, high, layer),
+            past[...] if last else joined(low, high, layer + 1),
             ahead[layer : layer + 1, :],
             dual[0, layer],
             dual[1, layer],
@@ -148,9 +148,9 @@
     return (dual_x - shifted) + (dual_y - pltpu.roll(dual_y, 1, 1))
 
 
-def stepped(field, dual, above, before, layer):
+def stepped(here, dual, above, before, layer):
     prev = above[...] if layer == 0 else dual[0, layer - 1]
-    return field[layer] + 0.25 * ((dual[0, layer] - prev) + flux_of(dual, before, layer))
+    return here + 0.25 * ((dual[0, layer] - prev) + flux_of(dual, before, layer))
 
 
 def first_values(field, dual, before, values):
@@ -159,7 +159,7 @@
 
 def all_values(field, dual, above, before, values):
     for layer in range(LAYERS):
-        values[layer] = stepped(field, dual, above, before, layer)
+        values[layer] = stepped(field[layer], dual, above, before, layer)
 
 
 def ramps(depth, base):
@@ -198,36 +198,49 @@
     return (lax.axis_index("slab") * LAYERS).astype(jnp.float32)
 
 
-def first_votes(visible, batches, tally):
+def half_votes(half, visible, batches, tally):
     base = slab_base()
     caps = [STEP * visible[0, 0, view].astype(jnp.float32) for view in range(VIEWS)]
 
-    def body(index, carry):
-        half, column, rows, lanes = block_of(index)
+    def body(column, carry):
+        lanes = pl.ds(pl.multiple_of(column * 128, 128), 128)
         views = [ramps(batches[2 * view + half, column], base) for view in range(VIEWS)]
         for layer in range(LAYERS + 1):
             sums, places, weights = votes(views, caps, float(layer))
             for slot, total in enumerate(sums + [places, weights]):
-                tally[slot, layer, rows, lanes] = total
+                tally[slot, layer, :, lanes] = total
         return carry
 
-    lax.fori_loop(0, 16, body, 0)
-
-
-def second_votes(visible, batches, tally, after, new_tally):
+    lax.fori_loop(0, 8, body, 0)
+
+
+def low_votes(visible, batches, tally):
+    half_votes(0, visible, batches, tally)
+
+
+def high_votes(visible, batches, after, tally):
+    half_votes(1, visible, batches, tally)
+
+
+def joined(low, high, layer):
+    return jnp.concatenate([low[layer], high[layer]], 0)
+
+
+def second_votes(visible, batches, low, high, after, new_tally):
     base = slab_base()
     caps = [STEP * visible[1, 0, view].astype(jnp.float32) for view in range(VIEWS)]
-
-    def body(index, carry):
-        half, column, rows, lanes = block_of(index)
-        views = [ramps(batches[2 * (VIEWS + view) + half, column], base) for view in range(VIEWS)]
-        for layer in range(LAYERS):
-            sums, places, weights = votes(views, caps, float(layer))
-            for slot, total in enumerate(sums + [places, weights]):
-                new_tally[slot, layer, rows, lanes] = tally[slot, layer, rows, lanes] + total
-        return carry
-
-    lax.fori_loop(0, 16, body, 0)
+    for half, tally in ((0, low), (1, high)):
+
+        def body(column, carry, half=half, tally=tally):
+            lanes = pl.ds(pl.multiple_of(column * 128, 128), 128)
+            views = [ramps(batches[2 * (VIEWS + view) + half, column], base) for view in range(VIEWS)]
+            for layer in range(LAYERS):
+                sums, places, weights = votes(views, caps, float(layer))
+                for slot, total in enumerate(sums + [places, weights]):
+                    new_tally[slot, layer, half * 8 : half * 8 + 8, lanes] = tally[slot, layer, :, lanes] + total
+            return carry
+
+        lax.fori_loop(0, 8, body, 0)
 
 
 def counted(values, tally, layer):
@@ -235,33 +248,43 @@
     return proximal(values, sums, tally[BINS - 1, layer], tally[BINS, layer])
 
 
-def first_update(field, values, tally, updated, extra, side):
-    for layer in range(LAYERS):
-        new = counted(values[layer], tally, layer)
+def low_update(field, values, tally, updated, extra, side):
+    for layer in range(LAYERS):
+        new = counted(values[layer, 0:8, :], tally, layer)
         updated[layer] = new
-        new = 2.0 * new - field[layer]
+        new = 2.0 * new - field[layer, 0:8, :]
         extra[layer] = new
         side[layer : layer + 1, :] = new[0:1, :]
 
 
-def past_update(below, values, dual, tally, extra):
-    extra[...] = 2.0 * counted(values[...] - 0.25 * dual[0, LAYERS - 1], tally, LAYERS) - below[...]
-
-
-def top_dual(extra, past, dual, ahead, top):
+def high_update(field, values, tally, updated, extra):
+    for layer in range(LAYERS):
+        new = counted(values[layer, 8:16, :], tally, layer)
+        updated[layer] = new
+        extra[layer] = 2.0 * new - field[layer, 8:16, :]
+
+
+def past_update(below, values, dual, low, high, extra):
+    for half, tally in ((0, low), (1, high)):
+        rows = slice(half * 8, half * 8 + 8)
+        steps = values[rows, :] - 0.25 * dual[0, LAYERS - 1, rows, :]
+        extra[rows, :] = 2.0 * counted(steps, tally, LAYERS) - below[rows, :]
+
+
+def top_dual(low, high, past, dual, ahead, top):
     last = LAYERS - 1
     slab_end = lax.axis_index("slab") == Z_LAST
-    row = ahead[last:LAYERS, :]
-    top[...] = dual_layer(extra[last], past[...], row, dual[0, last], dual[1, last], dual[2, last], slab_end)[0]
-
-
-def last_layers(current, dual, before, tally, updated):
+    here, row = joined(low, high, last), ahead[last:LAYERS, :]
+    top[...] = dual_layer(here, past[...], row, dual[0, last], dual[1, last], dual[2, last], slab_end)[0]
+
+
+def last_layers(low, high, dual, before, tally, updated):
     for layer in range(1, LAYERS):
-        updated[layer] = counted(stepped(current, dual, None, before, layer), tally, layer)
-
-
-def last_layer(current, dual, above, before, tally, updated_in, updated, layer, sem):
-    layer[...] = counted(stepped(current, dual, above, before, 0), tally, 0)
+        updated[layer] = counted(stepped(joined(low, high, layer), dual, None, before, layer), tally, layer)
+
+
+def last_layer(low, high, dual, above, before, tally, updated_in, updated, layer, sem):
+    layer[...] = counted(stepped(joined(low, high, 0), dual, above, before, 0), tally, 0)
     move = pltpu.make_async_copy(layer, updated.at[0], sem)
     move.start()
     move.wait()
@@ -309,22 +332,29 @@
     past_values = passed_along(values, "slab", -1)
     (values,) = call(all_values, [block], 5, [VMEM] * 4)(field, dual, above, before)
 
-    (tally,) = call(first_votes, [(BINS + 1, LAYERS + 1) + layer], 12, [SMEM, VMEM])(visible, batches)
-    current, extra, side = call(first_update, [block, block, rows], 1, [VMEM] * 3)(field, values, tally)
+    half, count = (LAYERS, 8, LANES), (BINS + 1, LAYERS + 1, 8, LANES)
+    (low_tally,) = call(low_votes, [count], 12, [SMEM, VMEM])(visible, batches)
+    low, low_extra, side = call(low_update, [half, half, rows], 1, [VMEM] * 3)(field, values, low_tally)
     ahead = passed_along(side, "tile", -1)
-    past_values, _ = lax.optimization_barrier((past_values, side))
-    (past,) = call(past_update, [layer], 1, [VMEM] * 4)(below, past_values, dual, tally)
-    (top,) = call(top_dual, [layer], 1, [VMEM] * 4)(extra, past, dual, ahead)
+    (high_tally,) = call(high_votes, [count], 12, [SMEM, VMEM, ANY])(visible, batches, side)
+    high, high_extra = call(high_update, [half, half], 1, [VMEM] * 3)(field, values, high_tally)
+    past_values, _ = lax.optimization_barrier((past_values, high))
+    (past,) = call(past_update, [layer], 1, [VMEM] * 5)(below, past_values, dual, low_tally, high_tally)
+    (top,) = call(top_dual, [layer], 1, [VMEM] * 5)(low_extra, high_extra, past, dual, ahead)
     above = passed_along(top, "slab", 1)
-    dual, side = call(second_duals, [(3,) + block, rows], 1, [VMEM] * 4 + [ANY])(extra, dual, ahead, past, top)
+    dual, side = call(second_duals, [(3,) + block, rows], 1, [VMEM] * 5 + [ANY])(
+        low_extra, high_extra, dual, ahead, past, top
+    )
     before = passed_along(side, "tile", 1)
-    (tally,) = call(second_votes, [(BINS + 1,) + block], 3, [SMEM, VMEM, VMEM, ANY])(visible, batches, tally, side)
-    (rest,) = call(last_layers, [block], 1, [VMEM] * 4)(current, dual, before, tally)
+    (tally,) = call(second_votes, [(BINS + 1,) + block], 3, [SMEM] + [VMEM] * 3 + [ANY])(
+        visible, batches, low_tally, high_tally, side
+    )
+    (rest,) = call(last_layers, [block], 1, [VMEM] * 5)(low, high, dual, before, tally)
     above, rest = lax.optimization_barrier((above, rest))
     (current,) = call(
-        last_layer, [block], 1, [VMEM] * 5 + [ANY], out_specs=(ANY,), input_output_aliases={5: 0},
+        last_layer, [block], 1, [VMEM] * 6 + [ANY], out_specs=(ANY,), input_output_aliases={6: 0},
         scratch_shapes=[pltpu.VMEM((ROWS, LANES), jnp.float32), pltpu.SemaphoreType.DMA],
-    )(current, dual, above, before, tally, rest)
+    )(low, high, dual, above, before, tally, rest)
     return (current, dual)
 
 

time: 98.4 us -> 97.7 us (level)
  waiting for transfers between devices: 7.93 us -> 6.9 us
    ppermute x8, waiting for transfers between devices: 7.93 us -> 6.89 us  [passed_along(): lax.ppermute(value, axis, [(source, source + steps) for source in range(f...]
    pallas_call x8 -> x10, Pallas kernels: 10.4 us -> 10.8 us  [the longest x1 2.75 us: per_device(): call(second_votes, [(BINS + 1,) + block], 3, [SMEM] + [VMEM] * 3 + [ANY])]
  transfers between devices with their start and end apart: 11 -> 11, of which waited for: 5 -> 4; matrix products, arithmetic and copies ran while one was open for 0% -> 0% of each run, Pallas kernels for 14% -> 15%
where the time goes in v10:
time: 97.7 us; the launch traced here: 97.1 us
  starting transfers between devices  74.2 us (76%)
  Pallas kernels  15.1 us (15%)
  waiting for transfers between devices  6.9 us (7%)
    ppermute x8, starting transfers between devices, passed_along(): lax.ppermute(value, axis, [(source, source + steps) for source in range(f...  55.1 us
    all_to_all x2, starting transfers between devices, exchange(): return lax.all_to_all(pieces, 'slab', 0, 0, axis_index_groups=GROUPS)  13.3 us
    ppermute x8, waiting for transfers between devices, passed_along(): lax.ppermute(value, axis, [(source, source + steps) for source in range(f...  6.89 us
    ppermute x1, starting transfers between devices, per_device(): lax.ppermute(kept, 'slab', [(index, index ^ 1) for index in range(32)])  5.84 us
    pallas_call x1, Pallas kernels, per_device(): call(second_votes, [(BINS + 1,) + block], 3, [SMEM] + [VMEM] * 3 + [ANY])  2.75 us
  transfers between devices with their start and end apart: 11, of which 4 were waited for; matrix products, arithmetic and copies ran while one was open for 0% of the time, Pallas kernels for 15%

profile of v10, /device:TPU:38, one launch (start us, length us, event | category | flops | bytes accessed | tf_op | source)
XLA Modules:
  0.0 97.1 jit_solution(9675941392637194232)
XLA Ops:
  0.6 7.4 %all-to-all-start = ((f32[16,8,8,128]{3,2,1,0:T(8,128)}), f32[16,8,8,128]{3,2,1,0:T(8,128)S(1)}, u32[]{:S(2)}, u32[]{:S(2)}) async-start(f32[16,8,8,128]{3,2,1,0:T(8,128)} %bitcast.9), calls=%async_computation | async-start | bytes 1048576 | tf_op jit(solution)/shard_map/all_to_all | solution.py:303
  8.1 1.2 %staged.1 = (f32[16,1024]{1,0:T(8,128)S(1)}, f32[8,1024]{1,0:T(8,128)S(1)}, f32[8,16,1024]{2,1,0:T(8,128)S(1)}) custom-call(f32[8,16,1024]{2,1,0:T(8,128)} %field.1), custom_call_target="tpu_custom_call" | custom-call | flops 1000000000 | bytes 3000000 | tf_op jit(solution)/shard_map/staged/pallas_call | solution.py:314
  9.3 17.2 %collective-permute-start.1 = (f32[16,1024]{1,0:T(8,128)S(1)}, f32[16,1024]{1,0:T(8,128)S(1)}, u32[]{:S(2)}, u32[]{:S(2)}) collective-permute-start(f32[16,1024]{1,0:T(8,128)S(1)} %get-tuple-element.24), channel_id=1, source_target_pairs={{16,0},{32,16},{48,32},{64,48},{80,64},{96,80},{112,96},{128,112},... | collective-permute-start | bytes 196616 | tf_op jit(solution)/shard_map/ppermute | solution.py:296
  26.5 0.0 all-to-all-done.spread
  26.5 0.7 pick.1.kept
  27.2 5.8 %collective-permute-start.4 = (f32[8,8,128]{2,1,0:T(8,128)S(1)}, f32[8,8,128]{2,1,0:T(8,128)S(1)}, u32[]{:S(2)}, u32[]{:S(2)}) collective-permute-start(f32[8,8,128]{2,1,0:T(8,128)S(1)} %pick.1.kept), channel_id=1, source_target_pairs={{0,16},{16,0},{32,48},{48,32},{64,80},{80,64},{96,112},{112,96},{1... | collective-permute-start | bytes 98312 | tf_op jit(solution)/shard_map/ppermute | solution.py:321
  33.0 0.0 copy-start.1
  33.1 2.1 %collective-permute-start = (f32[8,1024]{1,0:T(8,128)S(1)}, f32[8,1024]{1,0:T(8,128)S(1)}, u32[]{:S(2)}, u32[]{:S(2)}) collective-permute-start(f32[8,1024]{1,0:T(8,128)S(1)} %get-tuple-element.23), channel_id=1, source_target_pairs={{1,0},{2,1},{3,2},{4,3},{5,4},{6,5},{7,6},{8,7},{9,8},{10,9},{11,1... | collective-permute-start | bytes 98312 | tf_op jit(solution)/shard_map/ppermute | solution.py:296
  35.1 0.0 collective-permute-done.1.given
  35.1 1.6 %collective-permute-done.ahead = f32[8,1024]{1,0:T(8,128)S(1)} collective-permute-done((f32[8,1024]{1,0:T(8,128)S(1)}, f32[8,1024]{1,0:T(8,128)S(1)}, u32[]{:S(2)}, u32[]{:S(2)}) %collective-permute-start) | collective-permute-done | bytes 32800 | tf_op jit(solution)/shard_map/ppermute | solution.py:296
  36.7 0.0 copy-done.1
  36.7 0.6 all_duals.1
  37.3 3.7 %collective-permute-start.3 = (f32[8,1024]{1,0:T(8,128)S(1)}, f32[8,1024]{1,0:T(8,128)S(1)}, u32[]{:S(2)}, u32[]{:S(2)}) collective-permute-start(f32[8,1024]{1,0:T(8,128)S(1)} %get-tuple-element.28), channel_id=1, source_target_pairs={{0,1},{1,2},{2,3},{3,4},{4,5},{5,6},{6,7},{7,8},{8,9},{9,10},{10,1... | collective-permute-start | bytes 98312 | tf_op jit(solution)/shard_map/ppermute | solution.py:296
  41.0 8.4 %collective-permute-start.2 = (f32[16,1024]{1,0:T(8,128)S(1)}, f32[16,1024]{1,0:T(8,128)S(1)}, u32[]{:S(2)}, u32[]{:S(2)}) collective-permute-start(f32[16,1024]{1,0:T(8,128)S(1)} %get-tuple-element.27), channel_id=1, source_target_pairs={{0,16},{16,32},{32,48},{48,64},{64,80},{80,96},{96,112},{112,128},... | collective-permute-start | bytes 196616 | tf_op jit(solution)/shard_map/ppermute | solution.py:296
  49.3 0.0 collective-permute-done.4.across
  49.4 1.5 %copies_of.1 = f32[16,8,8,128]{3,2,1,0:T(8,128)} custom-call(s32[2]{0:T(128)} %owner.3, f32[8,8,128]{2,1,0:T(8,128)S(1)} %pick.1.kept, f32[8,8,128]{2,1,0:T(8,128)S(1)} %collective-permute-done.4.across), custom_call_target="tpu_custom_call" | custom-call | flops 1000000000 | bytes 3000000 | tf_op jit(solution)/shard_map/copies_of/pallas_call | solution.py:329
  50.9 5.8 %all-to-all-start.1 = ((f32[16,8,8,128]{3,2,1,0:T(8,128)}), f32[16,8,8,128]{3,2,1,0:T(8,128)S(1)}, u32[]{:S(2)}, u32[]{:S(2)}) async-start(f32[16,8,8,128]{3,2,1,0:T(8,128)} %copies_of.1), calls=%async_computation.1 | async-start | bytes 1048576 | tf_op jit(solution)/shard_map/all_to_all | solution.py:303
  56.7 0.0 collective-permute-done.3.before
  56.7 0.1 first_values.1
  56.8 0.0 copy-start.2
  56.8 10.3 %collective-permute-start.6 = (f32[16,1024]{1,0:T(8,128)S(1)}, f32[16,1024]{1,0:T(8,128)S(1)}, u32[]{:S(2)}, u32[]{:S(2)}) collective-permute-start(f32[16,1024]{1,0:T(8,128)S(1)} %first_values.1), channel_id=1, source_target_pairs={{16,0},{32,16},{48,32},{64,48},{80,64},{96,80},{112,96},{128,112},... | collective-permute-start | bytes 196616 | tf_op jit(solution)/shard_map/ppermute | solution.py:296
  67.1 0.0 collective-permute-done.2.above
  67.1 0.3 all_values.1.values
  67.4 0.0 all-to-all-done.1.batches
  67.4 0.0 copy-done.2
  67.4 1.7 %low_votes.1.tally.low = f32[9,9,8,1024]{3,2,1,0:T(8,128)S(1)} custom-call(s32[2,1,4]{2,1,0:T(1,128)S(1)} %bitcast.6, f32[16,8,8,128]{3,2,1,0:T(8,128)S(1)} %all-to-all-done.1.batches), custom_call_target="tpu_custom_call" | custom-call | flops 12000000000 | bytes 36000000 | tf_op jit(solution)/shard_map/low_votes/pallas_call | solution.py:336
  69.1 0.3 low_update.1
  69.4 2.0 %collective-permute-start.5 = (f32[8,1024]{1,0:T(8,128)S(1)}, f32[8,1024]{1,0:T(8,128)S(1)}, u32[]{:S(2)}, u32[]{:S(2)}) collective-permute-start(f32[8,1024]{1,0:T(8,128)S(1)} %get-tuple-element.31.after), channel_id=1, source_target_pairs={{1,0},{2,1},{3,2},{4,3},{5,4},{6,5},{7,6},{8,7},{9,8},{10,9},{11,1... | collective-permute-start | bytes 98312 | tf_op jit(solution)/shard_map/ppermute | solution.py:296
  71.4 1.7 %high_votes.1.tally.high = f32[9,9,8,1024]{3,2,1,0:T(8,128)S(1)} custom-call(s32[2,1,4]{2,1,0:T(1,128)S(1)} %bitcast.7, f32[16,8,8,128]{3,2,1,0:T(8,128)S(1)} %all-to-all-done.1.batches, f32[8,1024]{1,0:T(8,128)S(1)} %get-tuple-element.31.after), custom_call_target="tpu_custom_call" | custom-call | flops 12000000000 | bytes 36000000 | tf_op jit(solution)/shard_map/high_votes/pallas_call | solution.py:339
  73.1 0.3 high_update.1
  73.3 1.0 %collective-permute-done.6.values = f32[16,1024]{1,0:T(8,128)S(1)} collective-permute-done((f32[16,1024]{1,0:T(8,128)S(1)}, f32[16,1024]{1,0:T(8,128)S(1)}, u32[]{:S(2)}, u32[]{:S(2)}) %collective-permute-start.6) | collective-permute-done | bytes 65568 | tf_op jit(solution)/shard_map/ppermute | solution.py:296
  74.4 0.1 past_update.1.past
  74.4 0.0 collective-permute-done.5.ahead
  74.4 0.1 top_dual.1.after
  74.6 9.4 %collective-permute-start.7 = (f32[16,1024]{1,0:T(8,128)S(1)}, f32[16,1024]{1,0:T(8,128)S(1)}, u32[]{:S(2)}, u32[]{:S(2)}) collective-permute-start(f32[16,1024]{1,0:T(8,128)S(1)} %top_dual.1.after), channel_id=1, source_target_pairs={{0,16},{16,32},{32,48},{48,64},{64,80},{80,96},{96,112},{112,128},... | collective-permute-start | bytes 196616 | tf_op jit(solution)/shard_map/ppermute | solution.py:296
  84.0 1.7 %second_duals.1 = (f32[3,8,16,1024]{3,2,1,0:T(8,128)}, f32[8,1024]{1,0:T(8,128)S(1)}) custom-call(f32[8,8,1024]{2,1,0:T(8,128)S(1)} %get-tuple-element.33.low, f32[8,8,1024]{2,1,0:T(8,128)S(1)} %get-tuple-element.34.high, f32[3,8,16,1024]{3,2,1,0:T(8,128)S(1)} %get-tuple-element.26.dual, f32[8,1024]{1,0:T(8,128)S(1)} %collective-permute-done.5.ahead, ...), custom_call_target="tpu_custom_call" | custom-call | flops 1000000000 | bytes 3000000 | tf_op jit(solution)/shard_map/second_duals/pallas_call | solution.py:345
  85.8 0.0 copy-start
  85.8 2.0 %collective-permute-start.8 = (f32[8,1024]{1,0:T(8,128)S(1)}, f32[8,1024]{1,0:T(8,128)S(1)}, u32[]{:S(2)}, u32[]{:S(2)}) collective-permute-start(f32[8,1024]{1,0:T(8,128)S(1)} %get-tuple-element.37.after), channel_id=1, source_target_pairs={{0,1},{1,2},{2,3},{3,4},{4,5},{5,6},{6,7},{7,8},{8,9},{9,10},{10,1... | collective-permute-start | bytes 98312 | tf_op jit(solution)/shard_map/ppermute | solution.py:296
  87.8 2.7 %second_votes.1.tally = f32[9,8,16,1024]{3,2,1,0:T(8,128)S(1)} custom-call(s32[2,1,4]{2,1,0:T(1,128)S(1)} %bitcast.8, f32[16,8,8,128]{3,2,1,0:T(8,128)S(1)} %all-to-all-done.1.batches, f32[9,9,8,1024]{3,2,1,0:T(8,128)S(1)} %low_votes.1.tally.low, f32[9,9,8,1024]{3,2,1,0:T(8,128)S(1)} %high_votes.1.tally.high, f32[8,1024]{1,0:T(8,128)S(1)} %get-tuple-element.37.after), custom_call_target="tpu_custom_call" | custom-call | flops 3000000000 | bytes 9000000 | tf_op jit(solution)/shard_map/second_votes/pallas_call | solution.py:349
  90.6 1.2 %collective-permute-done.8.before = f32[8,1024]{1,0:T(8,128)S(1)} collective-permute-done((f32[8,1024]{1,0:T(8,128)S(1)}, f32[8,1024]{1,0:T(8,128)S(1)}, u32[]{:S(2)}, u32[]{:S(2)}) %collective-permute-start.8) | collective-permute-done | bytes 32800 | tf_op jit(solution)/shard_map/ppermute | solution.py:296
  91.7 0.0 copy-done
  91.7 1.4 %last_layers.1.updated_in = f32[8,16,1024]{2,1,0:T(8,128)} custom-call(f32[8,8,1024]{2,1,0:T(8,128)S(1)} %get-tuple-element.30.low, f32[8,8,1024]{2,1,0:T(8,128)S(1)} %get-tuple-element.32.high, f32[3,8,16,1024]{3,2,1,0:T(8,128)S(1)} %copy-done, f32[8,1024]{1,0:T(8,128)S(1)} %collective-permute-done.8.before, f32[9,8,16,1024]{3,2,1,0:T(8,128)S(1)} %second_votes.1.tally), custom_call_target="tpu_custom_call" | custom-call | flops 1000000000 | bytes 3000000 | tf_op jit(solution)/shard_map/last_layers/pallas_call | solution.py:352
  93.1 3.2 %collective-permute-done.7.above = f32[16,1024]{1,0:T(8,128)S(1)} collective-permute-done((f32[16,1024]{1,0:T(8,128)S(1)}, f32[16,1024]{1,0:T(8,128)S(1)}, u32[]{:S(2)}, u32[]{:S(2)}) %collective-permute-start.7) | collective-permute-done | bytes 65568 | tf_op jit(solution)/shard_map/ppermute | solution.py:296
  96.3 0.8 last_layer.1
  (1 shorter events, 0.0 us)
Async XLA Ops:
  0.6 25.9 %all-to-all-start = ((f32[16,8,8,128]{3,2,1,0:T(8,128)}), f32[16,8,8,128]{3,2,1,0:T(8,128)S(1)}, u32[]{:S(2)}, u32[]{:S(2)}) async-start(f32[16,8,8,128]{3,2,1,0:T(8,128)} %bitcast.9), calls=%async_computation | async-start | bytes 1048576 | tf_op jit(solution)/shard_map/all_to_all | solution.py:303
  9.3 25.9 %collective-permute-start.1 = (f32[16,1024]{1,0:T(8,128)S(1)}, f32[16,1024]{1,0:T(8,128)S(1)}, u32[]{:S(2)}, u32[]{:S(2)}) collective-permute-start(f32[16,1024]{1,0:T(8,128)S(1)} %get-tuple-element.24), channel_id=1, source_target_pairs={{16,0},{32,16},{48,32},{64,48},{80,64},{96,80},{112,96},{128,112},... | collective-permute-start | bytes 196616 | tf_op jit(solution)/shard_map/ppermute | solution.py:296
  27.2 22.2 %collective-permute-start.4 = (f32[8,8,128]{2,1,0:T(8,128)S(1)}, f32[8,8,128]{2,1,0:T(8,128)S(1)}, u32[]{:S(2)}, u32[]{:S(2)}) collective-permute-start(f32[8,8,128]{2,1,0:T(8,128)S(1)} %pick.1.kept), channel_id=1, source_target_pairs={{0,16},{16,0},{32,48},{48,32},{64,80},{80,64},{96,112},{112,96},{1... | collective-permute-start | bytes 98312 | tf_op jit(solution)/shard_map/ppermute | solution.py:321
  33.0 3.7 %copy-start.1 = (f32[3,8,16,1024]{3,2,1,0:T(8,128)S(1)}, f32[3,8,16,1024]{3,2,1,0:T(8,128)}, u32[]{:S(2)}) copy-start(f32[3,8,16,1024]{3,2,1,0:T(8,128)} %dual.1) | copy-start | bytes 4718596
  33.1 3.6 %collective-permute-start = (f32[8,1024]{1,0:T(8,128)S(1)}, f32[8,1024]{1,0:T(8,128)S(1)}, u32[]{:S(2)}, u32[]{:S(2)}) collective-permute-start(f32[8,1024]{1,0:T(8,128)S(1)} %get-tuple-element.23), channel_id=1, source_target_pairs={{1,0},{2,1},{3,2},{4,3},{5,4},{6,5},{7,6},{8,7},{9,8},{10,9},{11,1... | collective-permute-start | bytes 98312 | tf_op jit(solution)/shard_map/ppermute | solution.py:296
  37.3 19.4 %collective-permute-start.3 = (f32[8,1024]{1,0:T(8,128)S(1)}, f32[8,1024]{1,0:T(8,128)S(1)}, u32[]{:S(2)}, u32[]{:S(2)}) collective-permute-start(f32[8,1024]{1,0:T(8,128)S(1)} %get-tuple-element.28), channel_id=1, source_target_pairs={{0,1},{1,2},{2,3},{3,4},{4,5},{5,6},{6,7},{7,8},{8,9},{9,10},{10,1... | collective-permute-start | bytes 98312 | tf_op jit(solution)/shard_map/ppermute | solution.py:296
  41.0 26.2 %collective-permute-start.2 = (f32[16,1024]{1,0:T(8,128)S(1)}, f32[16,1024]{1,0:T(8,128)S(1)}, u32[]{:S(2)}, u32[]{:S(2)}) collective-permute-start(f32[16,1024]{1,0:T(8,128)S(1)} %get-tuple-element.27), channel_id=1, source_target_pairs={{0,16},{16,32},{32,48},{48,64},{64,80},{80,96},{96,112},{112,128},... | collective-permute-start | bytes 196616 | tf_op jit(solution)/shard_map/ppermute | solution.py:296
  50.9 16.5 %all-to-all-start.1 = ((f32[16,8,8,128]{3,2,1,0:T(8,128)}), f32[16,8,8,128]{3,2,1,0:T(8,128)S(1)}, u32[]{:S(2)}, u32[]{:S(2)}) async-start(f32[16,8,8,128]{3,2,1,0:T(8,128)} %copies_of.1), calls=%async_computation.1 | async-start | bytes 1048576 | tf_op jit(solution)/shard_map/all_to_all | solution.py:303
  56.8 10.6 %copy-start.2 = (s32[2,4,1]{1,2,0:T(1,128)S(1)}, s32[2,4,1]{1,2,0:T(1,128)}, u32[]{:S(2)}) copy-start(s32[2,4,1]{1,2,0:T(1,128)} %param.9) | copy-start | bytes 100
  56.8 17.5 %collective-permute-start.6 = (f32[16,1024]{1,0:T(8,128)S(1)}, f32[16,1024]{1,0:T(8,128)S(1)}, u32[]{:S(2)}, u32[]{:S(2)}) collective-permute-start(f32[16,1024]{1,0:T(8,128)S(1)} %first_values.1), channel_id=1, source_target_pairs={{16,0},{32,16},{48,32},{64,48},{80,64},{96,80},{112,96},{128,112},... | collective-permute-start | bytes 196616 | tf_op jit(solution)/shard_map/ppermute | solution.py:296
  69.4 5.0 %collective-permute-start.5 = (f32[8,1024]{1,0:T(8,128)S(1)}, f32[8,1024]{1,0:T(8,128)S(1)}, u32[]{:S(2)}, u32[]{:S(2)}) collective-permute-start(f32[8,1024]{1,0:T(8,128)S(1)} %get-tuple-element.31.after), channel_id=1, source_target_pairs={{1,0},{2,1},{3,2},{4,3},{5,4},{6,5},{7,6},{8,7},{9,8},{10,9},{11,1... | collective-permute-start | bytes 98312 | tf_op jit(solution)/shard_map/ppermute | solution.py:296
  74.6 21.7 %collective-permute-start.7 = (f32[16,1024]{1,0:T(8,128)S(1)}, f32[16,1024]{1,0:T(8,128)S(1)}, u32[]{:S(2)}, u32[]{:S(2)}) collective-permute-start(f32[16,1024]{1,0:T(8,128)S(1)} %top_dual.1.after), channel_id=1, source_target_pairs={{0,16},{16,32},{32,48},{48,64},{64,80},{80,96},{96,112},{112,128},... | collective-permute-start | bytes 196616 | tf_op jit(solution)/shard_map/ppermute | solution.py:296
  85.8 6.0 %copy-start = (f32[3,8,16,1024]{3,2,1,0:T(8,128)S(1)}, f32[3,8,16,1024]{3,2,1,0:T(8,128)}, u32[]{:S(2)}) copy-start(f32[3,8,16,1024]{3,2,1,0:T(8,128)} %get-tuple-element.20.dual) | copy-start | bytes 4718596
  85.8 6.0 %collective-permute-start.8 = (f32[8,1024]{1,0:T(8,128)S(1)}, f32[8,1024]{1,0:T(8,128)S(1)}, u32[]{:S(2)}, u32[]{:S(2)}) collective-permute-start(f32[8,1024]{1,0:T(8,128)S(1)} %get-tuple-element.37.after), channel_id=1, source_target_pairs={{0,1},{1,2},{2,3},{3,4},{4,5},{5,6},{6,7},{7,8},{8,9},{9,10},{10,1... | collective-permute-start | bytes 98312 | tf_op jit(solution)/shard_map/ppermute | solution.py:296

commit v11 on v10

--- a/solution.py
+++ b/solution.py
@@ -78,15 +78,13 @@
     kept[...] = spread[lax.shift_right_logical(owner[lax.shift_right_logical(lax.axis_index("slab"), 4)], 1)]
 
 
-def copies_of(owner, kept, across, copies):
-    slab = lax.axis_index("slab")
-    here = (owner[lax.shift_right_logical(slab, 4)] & 1) == (slab & 1)
-    piece = jnp.where(here, kept[...], across[...])
+def copies_of(mine, kept, across, copies):
+    piece = jnp.where(mine[...] > 0.5, kept[...], across[...])
     for place in range(16):
         copies[place] = piece
 
 
-def staged(field, first_layer, first_rows, field_here, sems):
+def staged(owner, visible, field, first_layer, first_rows, field_here, caps, mine, sems):
     moves = [
         pltpu.make_async_copy(field.at[:, 0], first_rows, sems.at[0]),
         pltpu.make_async_copy(field.at[0], first_layer, sems.at[1]),
@@ -94,6 +92,12 @@
     ]
     for move in moves:
         move.start()
+    for view in range(ITERS * VIEWS):
+        cap = STEP * visible[view // VIEWS, 0, view % VIEWS].astype(jnp.float32)
+        caps[view] = jnp.full((8, 128), cap, jnp.float32)
+    slab = lax.axis_index("slab")
+    here = (owner[lax.shift_right_logical(slab, 4)] & 1) == (slab & 1)
+    mine[...] = jnp.full((8, 128), jnp.where(here, 1.0, 0.0), jnp.float32)
     for move in moves:
         move.wait()
 
@@ -198,9 +202,9 @@
     return (lax.axis_index("slab") * LAYERS).astype(jnp.float32)
 
 
-def half_votes(half, visible, batches, tally):
+def half_votes(half, caps_of, batches, tally):
     base = slab_base()
-    caps = [STEP * visible[0, 0, view].astype(jnp.float32) for view in range(VIEWS)]
+    caps = [caps_of[view] for view in range(VIEWS)]
 
     def body(column, carry):
         lanes = pl.ds(pl.multiple_of(column * 128, 128), 128)
@@ -214,21 +218,21 @@
     lax.fori_loop(0, 8, body, 0)
 
 
-def low_votes(visible, batches, tally):
-    half_votes(0, visible, batches, tally)
-
-
-def high_votes(visible, batches, after, tally):
-    half_votes(1, visible, batches, tally)
+def low_votes(caps, batches, tally):
+    half_votes(0, caps, batches, tally)
+
+
+def high_votes(caps, batches, after, tally):
+    half_votes(1, caps, batches, tally)
 
 
 def joined(low, high, layer):
     return jnp.concatenate([low[layer], high[layer]], 0)
 
 
-def second_votes(visible, batches, low, high, after, new_tally):
+def second_votes(caps_of, batches, low, high, after, new_tally):
     base = slab_base()
-    caps = [STEP * visible[1, 0, view].astype(jnp.float32) for view in range(VIEWS)]
+    caps = [caps_of[VIEWS + view] for view in range(VIEWS)]
     for half, tally in ((0, low), (1, high)):
 
         def body(column, carry, half=half, tally=tally):
@@ -306,14 +310,15 @@
 def per_device(field, dual, depth, owner, visible):
     block = (LAYERS, ROWS, LANES)
     owner = pltpu.with_memory_space_constraint(owner, pltpu.HBM)
-    visible = visible.transpose(0, 2, 1)
+    visible = pltpu.with_memory_space_constraint(visible.transpose(0, 2, 1), pltpu.HBM)
 
     pieces = depth.reshape(16, 8, 8, 128).transpose(0, 2, 1, 3)
     spread = exchange(pieces)
 
-    first_layer, first_rows, field = call(
-        staged, [(ROWS, LANES), (LAYERS, LANES), block], 1, [HBM], scratch_shapes=[pltpu.SemaphoreType.DMA((3,))]
-    )(pltpu.with_memory_space_constraint(field, pltpu.HBM))
+    first_layer, first_rows, field, caps, mine = call(
+        staged, [(ROWS, LANES), (LAYERS, LANES), block, (ITERS * VIEWS, 8, 128), (8, 128)], 1, [SMEM, SMEM, HBM],
+        scratch_shapes=[pltpu.SemaphoreType.DMA((3,))],
+    )(owner, visible, pltpu.with_memory_space_constraint(field, pltpu.HBM))
     below = passed_along(first_layer, "slab", -1)
     (kept,) = call(pick, [(8, 8, 128)], 1, [SMEM, VMEM])(owner, spread)
     first_rows, _ = lax.optimization_barrier((first_rows, spread))
@@ -326,17 +331,17 @@
     above = passed_along(top, "slab", 1)
     before = passed_along(side, "tile", 1)
     across, top, side = lax.optimization_barrier((across, top, side))
-    (copies,) = call(copies_of, [pieces.shape], 1, [SMEM, VMEM, VMEM])(owner, kept, across)
+    (copies,) = call(copies_of, [pieces.shape], 1, [VMEM] * 3)(mine, kept, across)
     batches = exchange(copies)
     (values,) = call(first_values, [layer], 1, [VMEM] * 3)(field, dual, before)
     past_values = passed_along(values, "slab", -1)
     (values,) = call(all_values, [block], 5, [VMEM] * 4)(field, dual, above, before)
 
     half, count = (LAYERS, 8, LANES), (BINS + 1, LAYERS + 1, 8, LANES)
-    (low_tally,) = call(low_votes, [count], 12, [SMEM, VMEM])(visible, batches)
+    (low_tally,) = call(low_votes, [count], 12, [VMEM, VMEM])(caps, batches)
     low, low_extra, side = call(low_update, [half, half, rows], 1, [VMEM] * 3)(field, values, low_tally)
     ahead = passed_along(side, "tile", -1)
-    (high_tally,) = call(high_votes, [count], 12, [SMEM, VMEM, ANY])(visible, batches, side)
+    (high_tally,) = call(high_votes, [count], 12, [VMEM, VMEM, ANY])(caps, batches, side)
     high, high_extra = call(high_update, [half, half], 1, [VMEM] * 3)(field, values, high_tally)
     past_values, _ = lax.optimization_barrier((past_values, high))
     (past,) = call(past_update, [layer], 1, [VMEM] * 5)(below, past_values, dual, low_tally, high_tally)
@@ -346,8 +351,8 @@
         low_extra, high_extra, dual, ahead, past, top
     )
     before = passed_along(side, "tile", 1)
-    (tally,) = call(second_votes, [(BINS + 1,) + block], 3, [SMEM] + [VMEM] * 3 + [ANY])(
-        visible, batches, low_tally, high_tally, side
+    (tally,) = call(second_votes, [(BINS + 1,) + block], 3, [VMEM] * 4 + [ANY])(
+        caps, batches, low_tally, high_tally, side
     )
     (rest,) = call(last_layers, [block], 1, [VMEM] * 5)(low, high, dual, before, tally)
     above, rest = lax.optimization_barrier((above, rest))

time: 97.7 us -> 96.4 us (0.987)
  Pallas kernels: 15.1 us -> 13.5 us
  waiting for transfers between devices: 6.9 us -> 8.23 us
  starting transfers between devices: 74.2 us -> 73.2 us
    pallas_call x5, Pallas kernels: 8.83 us -> 7.21 us  [the longest x1 2.2 us: per_device(): call(second_votes, [(BINS + 1,) + block], 3, [VMEM] * 4 + [ANY])]
    ppermute x8, waiting for transfers between devices: 6.89 us -> 8.23 us  [passed_along(): lax.ppermute(value, axis, [(source, source + steps) for source in range(f...]
  transfers between devices with their start and end apart: 11 -> 11, of which waited for: 4 -> 4; matrix products, arithmetic and copies ran while one was open for 0% -> 0% of each run, Pallas kernels for 15% -> 13%
where the time goes in v11:
time: 96.4 us; the launch traced here: 95.8 us
  starting transfers between devices  73.2 us (76%)
  Pallas kernels  13.5 us (14%)
  waiting for transfers between devices  8.23 us (9%)
    ppermute x8, starting transfers between devices, passed_along(): lax.ppermute(value, axis, [(source, source + steps) for source in range(f...  54.7 us
    all_to_all x2, starting transfers between devices, exchange(): return lax.all_to_all(pieces, 'slab', 0, 0, axis_index_groups=GROUPS)  13.4 us
    ppermute x8, waiting for transfers between devices, passed_along(): lax.ppermute(value, axis, [(source, source + steps) for source in range(f...  8.23 us
    ppermute x1, starting transfers between devices, per_device(): lax.ppermute(kept, 'slab', [(index, index ^ 1) for index in range(32)])  5.14 us
    pallas_call x1, Pallas kernels, per_device(): call(second_votes, [(BINS + 1,) + block], 3, [VMEM] * 4 + [ANY])  2.2 us
  transfers between devices with their start and end apart: 11, of which 4 were waited for; matrix products, arithmetic and copies ran while one was open for 0% of the time, Pallas kernels for 13%

profile of v11, /device:TPU:38, one launch (start us, length us, event | category | flops | bytes accessed | tf_op | source)
XLA Modules:
  0.0 95.8 jit_solution(1899871448272683155)
XLA Ops:
  0.6 7.4 %all-to-all-start = ((f32[16,8,8,128]{3,2,1,0:T(8,128)}), f32[16,8,8,128]{3,2,1,0:T(8,128)S(1)}, u32[]{:S(2)}, u32[]{:S(2)}) async-start(f32[16,8,8,128]{3,2,1,0:T(8,128)} %bitcast.6), calls=%async_computation | async-start | bytes 1048576 | tf_op jit(solution)/shard_map/all_to_all | solution.py:307
  8.1 1.9 %staged.1 = (f32[16,1024]{1,0:T(8,128)S(1)}, f32[8,1024]{1,0:T(8,128)S(1)}, f32[8,16,1024]{2,1,0:T(8,128)S(1)}, f32[8,8,128]{2,1,0:T(8,128)S(1)}, f32[8,128]{1,0:T(8,128)S(1)}) custom-call(s32[2]{0:T(128)} %owner.3, s32[2,1,4]{2,1,0:T(1,128)} %bitcast.7, f32[8,16,1024]{2,1,0:T(8,128)} %field.1), custom_call_target="tpu_custom_call" | custom-call | flops 1000000000 | bytes 3000000 | tf_op jit(solution)/shard_map/staged/pallas_call | solution.py:318
  10.0 17.2 %collective-permute-start.1 = (f32[16,1024]{1,0:T(8,128)S(1)}, f32[16,1024]{1,0:T(8,128)S(1)}, u32[]{:S(2)}, u32[]{:S(2)}) collective-permute-start(f32[16,1024]{1,0:T(8,128)S(1)} %get-tuple-element.26), channel_id=1, source_target_pairs={{16,0},{32,16},{48,32},{64,48},{80,64},{96,80},{112,96},{128,112},... | collective-permute-start | bytes 196616 | tf_op jit(solution)/shard_map/ppermute | solution.py:300
  27.2 0.0 all-to-all-done.spread
  27.2 0.7 pick.1.kept
  27.9 5.1 %collective-permute-start.4 = (f32[8,8,128]{2,1,0:T(8,128)S(1)}, f32[8,8,128]{2,1,0:T(8,128)S(1)}, u32[]{:S(2)}, u32[]{:S(2)}) collective-permute-start(f32[8,8,128]{2,1,0:T(8,128)S(1)} %pick.1.kept), channel_id=1, source_target_pairs={{0,16},{16,0},{32,48},{48,32},{64,80},{80,64},{96,112},{112,96},{1... | collective-permute-start | bytes 98312 | tf_op jit(solution)/shard_map/ppermute | solution.py:326
  33.0 0.0 copy-start.1
  33.1 2.1 %collective-permute-start = (f32[8,1024]{1,0:T(8,128)S(1)}, f32[8,1024]{1,0:T(8,128)S(1)}, u32[]{:S(2)}, u32[]{:S(2)}) collective-permute-start(f32[8,1024]{1,0:T(8,128)S(1)} %get-tuple-element.25), channel_id=1, source_target_pairs={{1,0},{2,1},{3,2},{4,3},{5,4},{6,5},{7,6},{8,7},{9,8},{10,9},{11,1... | collective-permute-start | bytes 98312 | tf_op jit(solution)/shard_map/ppermute | solution.py:300
  35.1 0.0 collective-permute-done.1.given
  35.1 1.6 %collective-permute-done.ahead = f32[8,1024]{1,0:T(8,128)S(1)} collective-permute-done((f32[8,1024]{1,0:T(8,128)S(1)}, f32[8,1024]{1,0:T(8,128)S(1)}, u32[]{:S(2)}, u32[]{:S(2)}) %collective-permute-start) | collective-permute-done | bytes 32800 | tf_op jit(solution)/shard_map/ppermute | solution.py:300
  36.7 0.0 copy-done.1
  36.7 0.6 all_duals.1
  37.3 3.7 %collective-permute-start.3 = (f32[8,1024]{1,0:T(8,128)S(1)}, f32[8,1024]{1,0:T(8,128)S(1)}, u32[]{:S(2)}, u32[]{:S(2)}) collective-permute-start(f32[8,1024]{1,0:T(8,128)S(1)} %get-tuple-element.30), channel_id=1, source_target_pairs={{0,1},{1,2},{2,3},{3,4},{4,5},{5,6},{6,7},{7,8},{8,9},{9,10},{10,1... | collective-permute-start | bytes 98312 | tf_op jit(solution)/shard_map/ppermute | solution.py:300
  41.0 9.6 %collective-permute-start.2 = (f32[16,1024]{1,0:T(8,128)S(1)}, f32[16,1024]{1,0:T(8,128)S(1)}, u32[]{:S(2)}, u32[]{:S(2)}) collective-permute-start(f32[16,1024]{1,0:T(8,128)S(1)} %get-tuple-element.29), channel_id=1, source_target_pairs={{0,16},{16,32},{32,48},{48,64},{64,80},{80,96},{96,112},{112,128},... | collective-permute-start | bytes 196616 | tf_op jit(solution)/shard_map/ppermute | solution.py:300
  50.5 0.0 collective-permute-done.4.across
  50.5 0.8 copies_of.1
  51.4 5.9 %all-to-all-start.1 = ((f32[16,8,8,128]{3,2,1,0:T(8,128)}), f32[16,8,8,128]{3,2,1,0:T(8,128)S(1)}, u32[]{:S(2)}, u32[]{:S(2)}) async-start(f32[16,8,8,128]{3,2,1,0:T(8,128)} %copies_of.1), calls=%async_computation.1 | async-start | bytes 1048576 | tf_op jit(solution)/shard_map/all_to_all | solution.py:307
  57.3 0.0 collective-permute-done.3.before
  57.3 0.1 first_values.1
  57.4 9.0 %collective-permute-start.6 = (f32[16,1024]{1,0:T(8,128)S(1)}, f32[16,1024]{1,0:T(8,128)S(1)}, u32[]{:S(2)}, u32[]{:S(2)}) collective-permute-start(f32[16,1024]{1,0:T(8,128)S(1)} %first_values.1), channel_id=1, source_target_pairs={{16,0},{32,16},{48,32},{64,48},{80,64},{96,80},{112,96},{128,112},... | collective-permute-start | bytes 196616 | tf_op jit(solution)/shard_map/ppermute | solution.py:300
  66.4 0.0 collective-permute-done.2.above
  66.5 0.3 all_values.1.values
  66.7 0.0 all-to-all-done.1.batches
  66.7 1.1 %low_votes.1.tally.low = f32[9,9,8,1024]{3,2,1,0:T(8,128)S(1)} custom-call(f32[8,8,128]{2,1,0:T(8,128)S(1)} %get-tuple-element.31.caps.caps_of, f32[16,8,8,128]{3,2,1,0:T(8,128)S(1)} %all-to-all-done.1.batches), custom_call_target="tpu_custom_call" | custom-call | flops 12000000000 | bytes 36000000 | tf_op jit(solution)/shard_map/low_votes/pallas_call | solution.py:341
  67.9 0.3 low_update.1
  68.2 2.5 %collective-permute-start.5 = (f32[8,1024]{1,0:T(8,128)S(1)}, f32[8,1024]{1,0:T(8,128)S(1)}, u32[]{:S(2)}, u32[]{:S(2)}) collective-permute-start(f32[8,1024]{1,0:T(8,128)S(1)} %get-tuple-element.35.after), channel_id=1, source_target_pairs={{1,0},{2,1},{3,2},{4,3},{5,4},{6,5},{7,6},{8,7},{9,8},{10,9},{11,1... | collective-permute-start | bytes 98312 | tf_op jit(solution)/shard_map/ppermute | solution.py:300
  70.6 1.1 %high_votes.1.tally.high = f32[9,9,8,1024]{3,2,1,0:T(8,128)S(1)} custom-call(f32[8,8,128]{2,1,0:T(8,128)S(1)} %get-tuple-element.31.caps.caps_of, f32[16,8,8,128]{3,2,1,0:T(8,128)S(1)} %all-to-all-done.1.batches, f32[8,1024]{1,0:T(8,128)S(1)} %get-tuple-element.35.after), custom_call_target="tpu_custom_call" | custom-call | flops 12000000000 | bytes 36000000 | tf_op jit(solution)/shard_map/high_votes/pallas_call | solution.py:344
  71.8 0.3 high_update.1
  72.0 2.3 %collective-permute-done.6.values = f32[16,1024]{1,0:T(8,128)S(1)} collective-permute-done((f32[16,1024]{1,0:T(8,128)S(1)}, f32[16,1024]{1,0:T(8,128)S(1)}, u32[]{:S(2)}, u32[]{:S(2)}) %collective-permute-start.6) | collective-permute-done | bytes 65568 | tf_op jit(solution)/shard_map/ppermute | solution.py:300
  74.3 0.1 past_update.1.past
  74.4 0.0 collective-permute-done.5.ahead
  74.4 0.1 top_dual.1.after
  74.6 8.7 %collective-permute-start.7 = (f32[16,1024]{1,0:T(8,128)S(1)}, f32[16,1024]{1,0:T(8,128)S(1)}, u32[]{:S(2)}, u32[]{:S(2)}) collective-permute-start(f32[16,1024]{1,0:T(8,128)S(1)} %top_dual.1.after), channel_id=1, source_target_pairs={{0,16},{16,32},{32,48},{48,64},{64,80},{80,96},{96,112},{112,128},... | collective-permute-start | bytes 196616 | tf_op jit(solution)/shard_map/ppermute | solution.py:300
  83.2 1.7 %second_duals.1 = (f32[3,8,16,1024]{3,2,1,0:T(8,128)}, f32[8,1024]{1,0:T(8,128)S(1)}) custom-call(f32[8,8,1024]{2,1,0:T(8,128)S(1)} %get-tuple-element.37.low, f32[8,8,1024]{2,1,0:T(8,128)S(1)} %get-tuple-element.38.high, f32[3,8,16,1024]{3,2,1,0:T(8,128)S(1)} %get-tuple-element.28.dual, f32[8,1024]{1,0:T(8,128)S(1)} %collective-permute-done.5.ahead, ...), custom_call_target="tpu_custom_call" | custom-call | flops 1000000000 | bytes 3000000 | tf_op jit(solution)/shard_map/second_duals/pallas_call | solution.py:350
  85.0 0.0 copy-start
  85.0 2.0 %collective-permute-start.8 = (f32[8,1024]{1,0:T(8,128)S(1)}, f32[8,1024]{1,0:T(8,128)S(1)}, u32[]{:S(2)}, u32[]{:S(2)}) collective-permute-start(f32[8,1024]{1,0:T(8,128)S(1)} %get-tuple-element.41.after), channel_id=1, source_target_pairs={{0,1},{1,2},{2,3},{3,4},{4,5},{5,6},{6,7},{7,8},{8,9},{9,10},{10,1... | collective-permute-start | bytes 98312 | tf_op jit(solution)/shard_map/ppermute | solution.py:300
  87.0 2.2 %second_votes.1.tally = f32[9,8,16,1024]{3,2,1,0:T(8,128)S(1)} custom-call(f32[8,8,128]{2,1,0:T(8,128)S(1)} %get-tuple-element.31.caps.caps_of, f32[16,8,8,128]{3,2,1,0:T(8,128)S(1)} %all-to-all-done.1.batches, f32[9,9,8,1024]{3,2,1,0:T(8,128)S(1)} %low_votes.1.tally.low, f32[9,9,8,1024]{3,2,1,0:T(8,128)S(1)} %high_votes.1.tally.high, ...), custom_call_target="tpu_custom_call" | custom-call | flops 3000000000 | bytes 9000000 | tf_op jit(solution)/shard_map/second_votes/pallas_call | solution.py:354
  89.2 1.1 %collective-permute-done.8.before = f32[8,1024]{1,0:T(8,128)S(1)} collective-permute-done((f32[8,1024]{1,0:T(8,128)S(1)}, f32[8,1024]{1,0:T(8,128)S(1)}, u32[]{:S(2)}, u32[]{:S(2)}) %collective-permute-start.8) | collective-permute-done | bytes 32800 | tf_op jit(solution)/shard_map/ppermute | solution.py:300
  90.3 0.0 copy-done
  90.3 1.4 %last_layers.1.updated_in = f32[8,16,1024]{2,1,0:T(8,128)} custom-call(f32[8,8,1024]{2,1,0:T(8,128)S(1)} %get-tuple-element.34.low, f32[8,8,1024]{2,1,0:T(8,128)S(1)} %get-tuple-element.36.high, f32[3,8,16,1024]{3,2,1,0:T(8,128)S(1)} %copy-done, f32[8,1024]{1,0:T(8,128)S(1)} %collective-permute-done.8.before, f32[9,8,16,1024]{3,2,1,0:T(8,128)S(1)} %second_votes.1.tally), custom_call_target="tpu_custom_call" | custom-call | flops 1000000000 | bytes 3000000 | tf_op jit(solution)/shard_map/last_layers/pallas_call | solution.py:357
  91.8 3.3 %collective-permute-done.7.above = f32[16,1024]{1,0:T(8,128)S(1)} collective-permute-done((f32[16,1024]{1,0:T(8,128)S(1)}, f32[16,1024]{1,0:T(8,128)S(1)}, u32[]{:S(2)}, u32[]{:S(2)}) %collective-permute-start.7) | collective-permute-done | bytes 65568 | tf_op jit(solution)/shard_map/ppermute | solution.py:300
  95.0 0.8 last_layer.1
  (1 shorter events, 0.0 us)
Async XLA Ops:
  0.6 26.6 %all-to-all-start = ((f32[16,8,8,128]{3,2,1,0:T(8,128)}), f32[16,8,8,128]{3,2,1,0:T(8,128)S(1)}, u32[]{:S(2)}, u32[]{:S(2)}) async-start(f32[16,8,8,128]{3,2,1,0:T(8,128)} %bitcast.6), calls=%async_computation | async-start | bytes 1048576 | tf_op jit(solution)/shard_map/all_to_all | solution.py:307
  10.0 25.2 %collective-permute-start.1 = (f32[16,1024]{1,0:T(8,128)S(1)}, f32[16,1024]{1,0:T(8,128)S(1)}, u32[]{:S(2)}, u32[]{:S(2)}) collective-permute-start(f32[16,1024]{1,0:T(8,128)S(1)} %get-tuple-element.26), channel_id=1, source_target_pairs={{16,0},{32,16},{48,32},{64,48},{80,64},{96,80},{112,96},{128,112},... | collective-permute-start | bytes 196616 | tf_op jit(solution)/shard_map/ppermute | solution.py:300
  27.9 22.6 %collective-permute-start.4 = (f32[8,8,128]{2,1,0:T(8,128)S(1)}, f32[8,8,128]{2,1,0:T(8,128)S(1)}, u32[]{:S(2)}, u32[]{:S(2)}) collective-permute-start(f32[8,8,128]{2,1,0:T(8,128)S(1)} %pick.1.kept), channel_id=1, source_target_pairs={{0,16},{16,0},{32,48},{48,32},{64,80},{80,64},{96,112},{112,96},{1... | collective-permute-start | bytes 98312 | tf_op jit(solution)/shard_map/ppermute | solution.py:326
  33.0 3.7 %copy-start.1 = (f32[3,8,16,1024]{3,2,1,0:T(8,128)S(1)}, f32[3,8,16,1024]{3,2,1,0:T(8,128)}, u32[]{:S(2)}) copy-start(f32[3,8,16,1024]{3,2,1,0:T(8,128)} %dual.1) | copy-start | bytes 4718596
  33.1 3.6 %collective-permute-start = (f32[8,1024]{1,0:T(8,128)S(1)}, f32[8,1024]{1,0:T(8,128)S(1)}, u32[]{:S(2)}, u32[]{:S(2)}) collective-permute-start(f32[8,1024]{1,0:T(8,128)S(1)} %get-tuple-element.25), channel_id=1, source_target_pairs={{1,0},{2,1},{3,2},{4,3},{5,4},{6,5},{7,6},{8,7},{9,8},{10,9},{11,1... | collective-permute-start | bytes 98312 | tf_op jit(solution)/shard_map/ppermute | solution.py:300
  37.3 20.0 %collective-permute-start.3 = (f32[8,1024]{1,0:T(8,128)S(1)}, f32[8,1024]{1,0:T(8,128)S(1)}, u32[]{:S(2)}, u32[]{:S(2)}) collective-permute-start(f32[8,1024]{1,0:T(8,128)S(1)} %get-tuple-element.30), channel_id=1, source_target_pairs={{0,1},{1,2},{2,3},{3,4},{4,5},{5,6},{6,7},{7,8},{8,9},{9,10},{10,1... | collective-permute-start | bytes 98312 | tf_op jit(solution)/shard_map/ppermute | solution.py:300
  41.0 25.5 %collective-permute-start.2 = (f32[16,1024]{1,0:T(8,128)S(1)}, f32[16,1024]{1,0:T(8,128)S(1)}, u32[]{:S(2)}, u32[]{:S(2)}) collective-permute-start(f32[16,1024]{1,0:T(8,128)S(1)} %get-tuple-element.29), channel_id=1, source_target_pairs={{0,16},{16,32},{32,48},{48,64},{64,80},{80,96},{96,112},{112,128},... | collective-permute-start | bytes 196616 | tf_op jit(solution)/shard_map/ppermute | solution.py:300
  51.4 15.3 %all-to-all-start.1 = ((f32[16,8,8,128]{3,2,1,0:T(8,128)}), f32[16,8,8,128]{3,2,1,0:T(8,128)S(1)}, u32[]{:S(2)}, u32[]{:S(2)}) async-start(f32[16,8,8,128]{3,2,1,0:T(8,128)} %copies_of.1), calls=%async_computation.1 | async-start | bytes 1048576 | tf_op jit(solution)/shard_map/all_to_all | solution.py:307
  57.4 16.9 %collective-permute-start.6 = (f32[16,1024]{1,0:T(8,128)S(1)}, f32[16,1024]{1,0:T(8,128)S(1)}, u32[]{:S(2)}, u32[]{:S(2)}) collective-permute-start(f32[16,1024]{1,0:T(8,128)S(1)} %first_values.1), channel_id=1, source_target_pairs={{16,0},{32,16},{48,32},{64,48},{80,64},{96,80},{112,96},{128,112},... | collective-permute-start | bytes 196616 | tf_op jit(solution)/shard_map/ppermute | solution.py:300
  68.2 6.3 %collective-permute-start.5 = (f32[8,1024]{1,0:T(8,128)S(1)}, f32[8,1024]{1,0:T(8,128)S(1)}, u32[]{:S(2)}, u32[]{:S(2)}) collective-permute-start(f32[8,1024]{1,0:T(8,128)S(1)} %get-tuple-element.35.after), channel_id=1, source_target_pairs={{1,0},{2,1},{3,2},{4,3},{5,4},{6,5},{7,6},{8,7},{9,8},{10,9},{11,1... | collective-permute-start | bytes 98312 | tf_op jit(solution)/shard_map/ppermute | solution.py:300
  74.6 20.5 %collective-permute-start.7 = (f32[16,1024]{1,0:T(8,128)S(1)}, f32[16,1024]{1,0:T(8,128)S(1)}, u32[]{:S(2)}, u32[]{:S(2)}) collective-permute-start(f32[16,1024]{1,0:T(8,128)S(1)} %top_dual.1.after), channel_id=1, source_target_pairs={{0,16},{16,32},{32,48},{48,64},{64,80},{80,96},{96,112},{112,128},... | collective-permute-start | bytes 196616 | tf_op jit(solution)/shard_map/ppermute | solution.py:300
  85.0 5.4 %copy-start = (f32[3,8,16,1024]{3,2,1,0:T(8,128)S(1)}, f32[3,8,16,1024]{3,2,1,0:T(8,128)}, u32[]{:S(2)}) copy-start(f32[3,8,16,1024]{3,2,1,0:T(8,128)} %get-tuple-element.22.dual) | copy-start | bytes 4718596
  85.0 5.4 %collective-permute-start.8 = (f32[8,1024]{1,0:T(8,128)S(1)}, f32[8,1024]{1,0:T(8,128)S(1)}, u32[]{:S(2)}, u32[]{:S(2)}) collective-permute-start(f32[8,1024]{1,0:T(8,128)S(1)} %get-tuple-element.41.after), channel_id=1, source_target_pairs={{0,1},{1,2},{2,3},{3,4},{4,5},{5,6},{6,7},{7,8},{8,9},{9,10},{10,1... | collective-permute-start | bytes 98312 | tf_op jit(solution)/shard_map/ppermute | solution.py:300

commit v12 on v11

--- a/solution.py
+++ b/solution.py
@@ -84,14 +84,22 @@
         copies[place] = piece
 
 
-def staged(owner, visible, field, first_layer, first_rows, field_here, caps, mine, sems):
+def staged(owner_far, visible_far, field, first_layer, first_rows, field_here, caps, mine, owner, visible, sems):
     moves = [
         pltpu.make_async_copy(field.at[:, 0], first_rows, sems.at[0]),
         pltpu.make_async_copy(field.at[0], first_layer, sems.at[1]),
         pltpu.make_async_copy(field, field_here, sems.at[2]),
     ]
+    scalars = [
+        pltpu.make_async_copy(owner_far, owner, sems.at[3]),
+        pltpu.make_async_copy(visible_far, visible, sems.at[4]),
+    ]
+    for scalar in scalars:
+        scalar.start()
     for move in moves:
         move.start()
+    for scalar in scalars:
+        scalar.wait()
     for view in range(ITERS * VIEWS):
         cap = STEP * visible[view // VIEWS, 0, view % VIEWS].astype(jnp.float32)
         caps[view] = jnp.full((8, 128), cap, jnp.float32)
@@ -316,8 +324,10 @@
     spread = exchange(pieces)
 
     first_layer, first_rows, field, caps, mine = call(
-        staged, [(ROWS, LANES), (LAYERS, LANES), block, (ITERS * VIEWS, 8, 128), (8, 128)], 1, [SMEM, SMEM, HBM],
-        scratch_shapes=[pltpu.SemaphoreType.DMA((3,))],
+        staged, [(ROWS, LANES), (LAYERS, LANES), block, (ITERS * VIEWS, 8, 128), (8, 128)], 1, [HBM] * 3,
+        scratch_shapes=[
+            pltpu.SMEM((ITERS,), jnp.int32), pltpu.SMEM((ITERS, 1, VIEWS), jnp.int32), pltpu.SemaphoreType.DMA((5,))
+        ],
     )(owner, visible, pltpu.with_memory_space_constraint(field, pltpu.HBM))
     below = passed_along(first_layer, "slab", -1)
     (kept,) = call(pick, [(8, 8, 128)], 1, [SMEM, VMEM])(owner, spread)

time: 96.4 us -> 96 us (level)
  transfers between devices with their start and end apart: 11 -> 11, of which waited for: 4 -> 4; matrix products, arithmetic and copies ran while one was open for 0% -> 0% of each run, Pallas kernels for 13% -> 12%
where the time goes in v12:
time: 96 us; the launch traced here: 95.4 us
  starting transfers between devices  74.1 us (77%)
  Pallas kernels  12.8 us (13%)
  waiting for transfers between devices  7.63 us (8%)
    ppermute x8, starting transfers between devices, passed_along(): lax.ppermute(value, axis, [(source, source + steps) for source in range(f...  55 us
    all_to_all x2, starting transfers between devices, exchange(): return lax.all_to_all(pieces, 'slab', 0, 0, axis_index_groups=GROUPS)  13.3 us
    ppermute x8, waiting for transfers between devices, passed_along(): lax.ppermute(value, axis, [(source, source + steps) for source in range(f...  7.62 us
    ppermute x1, starting transfers between devices, per_device(): lax.ppermute(kept, 'slab', [(index, index ^ 1) for index in range(32)])  5.82 us
    pallas_call x1, Pallas kernels, per_device(): call(second_votes, [(BINS + 1,) + block], 3, [VMEM] * 4 + [ANY])  2.2 us
  transfers between devices with their start and end apart: 11, of which 4 were waited for; matrix products, arithmetic and copies ran while one was open for 0% of the time, Pallas kernels for 12%

profile of v12, /device:TPU:38, one launch (start us, length us, event | category | flops | bytes accessed | tf_op | source)
XLA Modules:
  0.0 95.4 jit_solution(16161222089503560221)
XLA Ops:
  0.6 7.4 %all-to-all-start = ((f32[16,8,8,128]{3,2,1,0:T(8,128)}), f32[16,8,8,128]{3,2,1,0:T(8,128)S(1)}, u32[]{:S(2)}, u32[]{:S(2)}) async-start(f32[16,8,8,128]{3,2,1,0:T(8,128)} %bitcast.6), calls=%async_computation | async-start | bytes 1048576 | tf_op jit(solution)/shard_map/all_to_all | solution.py:315
  8.1 1.2 %staged.1 = (f32[16,1024]{1,0:T(8,128)S(1)}, f32[8,1024]{1,0:T(8,128)S(1)}, f32[8,16,1024]{2,1,0:T(8,128)S(1)}, f32[8,8,128]{2,1,0:T(8,128)S(1)}, f32[8,128]{1,0:T(8,128)S(1)}) custom-call(s32[2]{0:T(128)} %owner.1, s32[2,1,4]{2,1,0:T(1,128)} %bitcast.7, f32[8,16,1024]{2,1,0:T(8,128)} %field.1), custom_call_target="tpu_custom_call" | custom-call | flops 1000000000 | bytes 3000000 | tf_op jit(solution)/shard_map/staged/pallas_call | solution.py:326
  9.3 17.2 %collective-permute-start.1 = (f32[16,1024]{1,0:T(8,128)S(1)}, f32[16,1024]{1,0:T(8,128)S(1)}, u32[]{:S(2)}, u32[]{:S(2)}) collective-permute-start(f32[16,1024]{1,0:T(8,128)S(1)} %get-tuple-element.26), channel_id=1, source_target_pairs={{16,0},{32,16},{48,32},{64,48},{80,64},{96,80},{112,96},{128,112},... | collective-permute-start | bytes 196616 | tf_op jit(solution)/shard_map/ppermute | solution.py:308
  26.5 0.0 all-to-all-done.spread
  26.5 0.7 pick.1.kept
  27.2 5.8 %collective-permute-start.4 = (f32[8,8,128]{2,1,0:T(8,128)S(1)}, f32[8,8,128]{2,1,0:T(8,128)S(1)}, u32[]{:S(2)}, u32[]{:S(2)}) collective-permute-start(f32[8,8,128]{2,1,0:T(8,128)S(1)} %pick.1.kept), channel_id=1, source_target_pairs={{0,16},{16,0},{32,48},{48,32},{64,80},{80,64},{96,112},{112,96},{1... | collective-permute-start | bytes 98312 | tf_op jit(solution)/shard_map/ppermute | solution.py:336
  33.0 0.0 copy-start.1
  33.1 2.1 %collective-permute-start = (f32[8,1024]{1,0:T(8,128)S(1)}, f32[8,1024]{1,0:T(8,128)S(1)}, u32[]{:S(2)}, u32[]{:S(2)}) collective-permute-start(f32[8,1024]{1,0:T(8,128)S(1)} %get-tuple-element.25), channel_id=1, source_target_pairs={{1,0},{2,1},{3,2},{4,3},{5,4},{6,5},{7,6},{8,7},{9,8},{10,9},{11,1... | collective-permute-start | bytes 98312 | tf_op jit(solution)/shard_map/ppermute | solution.py:308
  35.1 0.0 collective-permute-done.1.given
  35.1 1.6 %collective-permute-done.ahead = f32[8,1024]{1,0:T(8,128)S(1)} collective-permute-done((f32[8,1024]{1,0:T(8,128)S(1)}, f32[8,1024]{1,0:T(8,128)S(1)}, u32[]{:S(2)}, u32[]{:S(2)}) %collective-permute-start) | collective-permute-done | bytes 32800 | tf_op jit(solution)/shard_map/ppermute | solution.py:308
  36.7 0.0 copy-done.1
  36.7 0.6 all_duals.1
  37.3 3.7 %collective-permute-start.3 = (f32[8,1024]{1,0:T(8,128)S(1)}, f32[8,1024]{1,0:T(8,128)S(1)}, u32[]{:S(2)}, u32[]{:S(2)}) collective-permute-start(f32[8,1024]{1,0:T(8,128)S(1)} %get-tuple-element.30), channel_id=1, source_target_pairs={{0,1},{1,2},{2,3},{3,4},{4,5},{5,6},{6,7},{7,8},{8,9},{9,10},{10,1... | collective-permute-start | bytes 98312 | tf_op jit(solution)/shard_map/ppermute | solution.py:308
  41.0 8.4 %collective-permute-start.2 = (f32[16,1024]{1,0:T(8,128)S(1)}, f32[16,1024]{1,0:T(8,128)S(1)}, u32[]{:S(2)}, u32[]{:S(2)}) collective-permute-start(f32[16,1024]{1,0:T(8,128)S(1)} %get-tuple-element.29), channel_id=1, source_target_pairs={{0,16},{16,32},{32,48},{48,64},{64,80},{80,96},{96,112},{112,128},... | collective-permute-start | bytes 196616 | tf_op jit(solution)/shard_map/ppermute | solution.py:308
  49.4 0.0 collective-permute-done.4.across
  49.4 0.8 copies_of.1
  50.2 5.8 %all-to-all-start.1 = ((f32[16,8,8,128]{3,2,1,0:T(8,128)}), f32[16,8,8,128]{3,2,1,0:T(8,128)S(1)}, u32[]{:S(2)}, u32[]{:S(2)}) async-start(f32[16,8,8,128]{3,2,1,0:T(8,128)} %copies_of.1), calls=%async_computation.1 | async-start | bytes 1048576 | tf_op jit(solution)/shard_map/all_to_all | solution.py:315
  56.1 0.0 collective-permute-done.3.before
  56.1 0.1 first_values.1
  56.2 10.3 %collective-permute-start.6 = (f32[16,1024]{1,0:T(8,128)S(1)}, f32[16,1024]{1,0:T(8,128)S(1)}, u32[]{:S(2)}, u32[]{:S(2)}) collective-permute-start(f32[16,1024]{1,0:T(8,128)S(1)} %first_values.1), channel_id=1, source_target_pairs={{16,0},{32,16},{48,32},{64,48},{80,64},{96,80},{112,96},{128,112},... | collective-permute-start | bytes 196616 | tf_op jit(solution)/shard_map/ppermute | solution.py:308
  66.4 0.0 collective-permute-done.2.above
  66.5 0.3 all_values.1.values
  66.7 0.0 all-to-all-done.1.batches
  66.7 1.1 %low_votes.1.tally.low = f32[9,9,8,1024]{3,2,1,0:T(8,128)S(1)} custom-call(f32[8,8,128]{2,1,0:T(8,128)S(1)} %get-tuple-element.31.caps.caps_of, f32[16,8,8,128]{3,2,1,0:T(8,128)S(1)} %all-to-all-done.1.batches), custom_call_target="tpu_custom_call" | custom-call | flops 12000000000 | bytes 36000000 | tf_op jit(solution)/shard_map/low_votes/pallas_call | solution.py:351
  67.9 0.3 low_update.1
  68.2 1.9 %collective-permute-start.5 = (f32[8,1024]{1,0:T(8,128)S(1)}, f32[8,1024]{1,0:T(8,128)S(1)}, u32[]{:S(2)}, u32[]{:S(2)}) collective-permute-start(f32[8,1024]{1,0:T(8,128)S(1)} %get-tuple-element.35.after), channel_id=1, source_target_pairs={{1,0},{2,1},{3,2},{4,3},{5,4},{6,5},{7,6},{8,7},{9,8},{10,9},{11,1... | collective-permute-start | bytes 98312 | tf_op jit(solution)/shard_map/ppermute | solution.py:308
  70.1 1.1 %high_votes.1.tally.high = f32[9,9,8,1024]{3,2,1,0:T(8,128)S(1)} custom-call(f32[8,8,128]{2,1,0:T(8,128)S(1)} %get-tuple-element.31.caps.caps_of, f32[16,8,8,128]{3,2,1,0:T(8,128)S(1)} %all-to-all-done.1.batches, f32[8,1024]{1,0:T(8,128)S(1)} %get-tuple-element.35.after), custom_call_target="tpu_custom_call" | custom-call | flops 12000000000 | bytes 36000000 | tf_op jit(solution)/shard_map/high_votes/pallas_call | solution.py:354
  71.2 0.3 high_update.1
  71.5 2.1 %collective-permute-done.6.values = f32[16,1024]{1,0:T(8,128)S(1)} collective-permute-done((f32[16,1024]{1,0:T(8,128)S(1)}, f32[16,1024]{1,0:T(8,128)S(1)}, u32[]{:S(2)}, u32[]{:S(2)}) %collective-permute-start.6) | collective-permute-done | bytes 65568 | tf_op jit(solution)/shard_map/ppermute | solution.py:308
  73.6 0.1 past_update.1.past
  73.6 0.0 collective-permute-done.5.ahead
  73.7 0.1 top_dual.1.after
  73.8 9.5 %collective-permute-start.7 = (f32[16,1024]{1,0:T(8,128)S(1)}, f32[16,1024]{1,0:T(8,128)S(1)}, u32[]{:S(2)}, u32[]{:S(2)}) collective-permute-start(f32[16,1024]{1,0:T(8,128)S(1)} %top_dual.1.after), channel_id=1, source_target_pairs={{0,16},{16,32},{32,48},{48,64},{64,80},{80,96},{96,112},{112,128},... | collective-permute-start | bytes 196616 | tf_op jit(solution)/shard_map/ppermute | solution.py:308
  83.2 1.7 %second_duals.1 = (f32[3,8,16,1024]{3,2,1,0:T(8,128)}, f32[8,1024]{1,0:T(8,128)S(1)}) custom-call(f32[8,8,1024]{2,1,0:T(8,128)S(1)} %get-tuple-element.37.low, f32[8,8,1024]{2,1,0:T(8,128)S(1)} %get-tuple-element.38.high, f32[3,8,16,1024]{3,2,1,0:T(8,128)S(1)} %get-tuple-element.28.dual, f32[8,1024]{1,0:T(8,128)S(1)} %collective-permute-done.5.ahead, ...), custom_call_target="tpu_custom_call" | custom-call | flops 1000000000 | bytes 3000000 | tf_op jit(solution)/shard_map/second_duals/pallas_call | solution.py:360
  85.0 0.0 copy-start
  85.0 2.0 %collective-permute-start.8 = (f32[8,1024]{1,0:T(8,128)S(1)}, f32[8,1024]{1,0:T(8,128)S(1)}, u32[]{:S(2)}, u32[]{:S(2)}) collective-permute-start(f32[8,1024]{1,0:T(8,128)S(1)} %get-tuple-element.41.after), channel_id=1, source_target_pairs={{0,1},{1,2},{2,3},{3,4},{4,5},{5,6},{6,7},{7,8},{8,9},{9,10},{10,1... | collective-permute-start | bytes 98312 | tf_op jit(solution)/shard_map/ppermute | solution.py:308
  87.0 2.2 %second_votes.1.tally = f32[9,8,16,1024]{3,2,1,0:T(8,128)S(1)} custom-call(f32[8,8,128]{2,1,0:T(8,128)S(1)} %get-tuple-element.31.caps.caps_of, f32[16,8,8,128]{3,2,1,0:T(8,128)S(1)} %all-to-all-done.1.batches, f32[9,9,8,1024]{3,2,1,0:T(8,128)S(1)} %low_votes.1.tally.low, f32[9,9,8,1024]{3,2,1,0:T(8,128)S(1)} %high_votes.1.tally.high, ...), custom_call_target="tpu_custom_call" | custom-call | flops 3000000000 | bytes 9000000 | tf_op jit(solution)/shard_map/second_votes/pallas_call | solution.py:364
  89.2 1.1 %collective-permute-done.8.before = f32[8,1024]{1,0:T(8,128)S(1)} collective-permute-done((f32[8,1024]{1,0:T(8,128)S(1)}, f32[8,1024]{1,0:T(8,128)S(1)}, u32[]{:S(2)}, u32[]{:S(2)}) %collective-permute-start.8) | collective-permute-done | bytes 32800 | tf_op jit(solution)/shard_map/ppermute | solution.py:308
  90.3 0.0 copy-done
  90.3 1.4 %last_layers.1.updated_in = f32[8,16,1024]{2,1,0:T(8,128)} custom-call(f32[8,8,1024]{2,1,0:T(8,128)S(1)} %get-tuple-element.34.low, f32[8,8,1024]{2,1,0:T(8,128)S(1)} %get-tuple-element.36.high, f32[3,8,16,1024]{3,2,1,0:T(8,128)S(1)} %copy-done, f32[8,1024]{1,0:T(8,128)S(1)} %collective-permute-done.8.before, f32[9,8,16,1024]{3,2,1,0:T(8,128)S(1)} %second_votes.1.tally), custom_call_target="tpu_custom_call" | custom-call | flops 1000000000 | bytes 3000000 | tf_op jit(solution)/shard_map/last_layers/pallas_call | solution.py:367
  91.8 2.9 %collective-permute-done.7.above = f32[16,1024]{1,0:T(8,128)S(1)} collective-permute-done((f32[16,1024]{1,0:T(8,128)S(1)}, f32[16,1024]{1,0:T(8,128)S(1)}, u32[]{:S(2)}, u32[]{:S(2)}) %collective-permute-start.7) | collective-permute-done | bytes 65568 | tf_op jit(solution)/shard_map/ppermute | solution.py:308
  94.7 0.8 last_layer.1
  (1 shorter events, 0.0 us)
Async XLA Ops:
  0.6 25.9 %all-to-all-start = ((f32[16,8,8,128]{3,2,1,0:T(8,128)}), f32[16,8,8,128]{3,2,1,0:T(8,128)S(1)}, u32[]{:S(2)}, u32[]{:S(2)}) async-start(f32[16,8,8,128]{3,2,1,0:T(8,128)} %bitcast.6), calls=%async_computation | async-start | bytes 1048576 | tf_op jit(solution)/shard_map/all_to_all | solution.py:315
  9.3 25.8 %collective-permute-start.1 = (f32[16,1024]{1,0:T(8,128)S(1)}, f32[16,1024]{1,0:T(8,128)S(1)}, u32[]{:S(2)}, u32[]{:S(2)}) collective-permute-start(f32[16,1024]{1,0:T(8,128)S(1)} %get-tuple-element.26), channel_id=1, source_target_pairs={{16,0},{32,16},{48,32},{64,48},{80,64},{96,80},{112,96},{128,112},... | collective-permute-start | bytes 196616 | tf_op jit(solution)/shard_map/ppermute | solution.py:308
  27.2 22.2 %collective-permute-start.4 = (f32[8,8,128]{2,1,0:T(8,128)S(1)}, f32[8,8,128]{2,1,0:T(8,128)S(1)}, u32[]{:S(2)}, u32[]{:S(2)}) collective-permute-start(f32[8,8,128]{2,1,0:T(8,128)S(1)} %pick.1.kept), channel_id=1, source_target_pairs={{0,16},{16,0},{32,48},{48,32},{64,80},{80,64},{96,112},{112,96},{1... | collective-permute-start | bytes 98312 | tf_op jit(solution)/shard_map/ppermute | solution.py:336
  33.0 3.7 %copy-start.1 = (f32[3,8,16,1024]{3,2,1,0:T(8,128)S(1)}, f32[3,8,16,1024]{3,2,1,0:T(8,128)}, u32[]{:S(2)}) copy-start(f32[3,8,16,1024]{3,2,1,0:T(8,128)} %dual.1) | copy-start | bytes 4718596
  33.1 3.6 %collective-permute-start = (f32[8,1024]{1,0:T(8,128)S(1)}, f32[8,1024]{1,0:T(8,128)S(1)}, u32[]{:S(2)}, u32[]{:S(2)}) collective-permute-start(f32[8,1024]{1,0:T(8,128)S(1)} %get-tuple-element.25), channel_id=1, source_target_pairs={{1,0},{2,1},{3,2},{4,3},{5,4},{6,5},{7,6},{8,7},{9,8},{10,9},{11,1... | collective-permute-start | bytes 98312 | tf_op jit(solution)/shard_map/ppermute | solution.py:308
  37.3 18.8 %collective-permute-start.3 = (f32[8,1024]{1,0:T(8,128)S(1)}, f32[8,1024]{1,0:T(8,128)S(1)}, u32[]{:S(2)}, u32[]{:S(2)}) collective-permute-start(f32[8,1024]{1,0:T(8,128)S(1)} %get-tuple-element.30), channel_id=1, source_target_pairs={{0,1},{1,2},{2,3},{3,4},{4,5},{5,6},{6,7},{7,8},{8,9},{9,10},{10,1... | collective-permute-start | bytes 98312 | tf_op jit(solution)/shard_map/ppermute | solution.py:308
  41.0 25.5 %collective-permute-start.2 = (f32[16,1024]{1,0:T(8,128)S(1)}, f32[16,1024]{1,0:T(8,128)S(1)}, u32[]{:S(2)}, u32[]{:S(2)}) collective-permute-start(f32[16,1024]{1,0:T(8,128)S(1)} %get-tuple-element.29), channel_id=1, source_target_pairs={{0,16},{16,32},{32,48},{48,64},{64,80},{80,96},{96,112},{112,128},... | collective-permute-start | bytes 196616 | tf_op jit(solution)/shard_map/ppermute | solution.py:308
  50.2 16.5 %all-to-all-start.1 = ((f32[16,8,8,128]{3,2,1,0:T(8,128)}), f32[16,8,8,128]{3,2,1,0:T(8,128)S(1)}, u32[]{:S(2)}, u32[]{:S(2)}) async-start(f32[16,8,8,128]{3,2,1,0:T(8,128)} %copies_of.1), calls=%async_computation.1 | async-start | bytes 1048576 | tf_op jit(solution)/shard_map/all_to_all | solution.py:315
  56.2 17.4 %collective-permute-start.6 = (f32[16,1024]{1,0:T(8,128)S(1)}, f32[16,1024]{1,0:T(8,128)S(1)}, u32[]{:S(2)}, u32[]{:S(2)}) collective-permute-start(f32[16,1024]{1,0:T(8,128)S(1)} %first_values.1), channel_id=1, source_target_pairs={{16,0},{32,16},{48,32},{64,48},{80,64},{96,80},{112,96},{128,112},... | collective-permute-start | bytes 196616 | tf_op jit(solution)/shard_map/ppermute | solution.py:308
  68.2 5.5 %collective-permute-start.5 = (f32[8,1024]{1,0:T(8,128)S(1)}, f32[8,1024]{1,0:T(8,128)S(1)}, u32[]{:S(2)}, u32[]{:S(2)}) collective-permute-start(f32[8,1024]{1,0:T(8,128)S(1)} %get-tuple-element.35.after), channel_id=1, source_target_pairs={{1,0},{2,1},{3,2},{4,3},{5,4},{6,5},{7,6},{8,7},{9,8},{10,9},{11,1... | collective-permute-start | bytes 98312 | tf_op jit(solution)/shard_map/ppermute | solution.py:308
  73.8 20.9 %collective-permute-start.7 = (f32[16,1024]{1,0:T(8,128)S(1)}, f32[16,1024]{1,0:T(8,128)S(1)}, u32[]{:S(2)}, u32[]{:S(2)}) collective-permute-start(f32[16,1024]{1,0:T(8,128)S(1)} %top_dual.1.after), channel_id=1, source_target_pairs={{0,16},{16,32},{32,48},{48,64},{64,80},{80,96},{96,112},{112,128},... | collective-permute-start | bytes 196616 | tf_op jit(solution)/shard_map/ppermute | solution.py:308
  85.0 5.4 %copy-start = (f32[3,8,16,1024]{3,2,1,0:T(8,128)S(1)}, f32[3,8,16,1024]{3,2,1,0:T(8,128)}, u32[]{:S(2)}) copy-start(f32[3,8,16,1024]{3,2,1,0:T(8,128)} %get-tuple-element.22.dual) | copy-start | bytes 4718596
  85.0 5.4 %collective-permute-start.8 = (f32[8,1024]{1,0:T(8,128)S(1)}, f32[8,1024]{1,0:T(8,128)S(1)}, u32[]{:S(2)}, u32[]{:S(2)}) collective-permute-start(f32[8,1024]{1,0:T(8,128)S(1)} %get-tuple-element.41.after), channel_id=1, source_target_pairs={{0,1},{1,2},{2,3},{3,4},{4,5},{5,6},{6,7},{7,8},{8,9},{9,10},{10,1... | collective-permute-start | bytes 98312 | tf_op jit(solution)/shard_map/ppermute | solution.py:308

commit v13 on v12

--- a/solution.py
+++ b/solution.py
@@ -290,13 +290,14 @@
     top[...] = dual_layer(here, past[...], row, dual[0, last], dual[1, last], dual[2, last], slab_end)[0]
 
 
-def last_layers(low, high, dual, before, tally, updated):
+def last_layers(low, high, dual, before, tally, updated, part):
+    part[...] = joined(low, high, 0) + 0.25 * (dual[0, 0] + flux_of(dual, before, 0))
     for layer in range(1, LAYERS):
         updated[layer] = counted(stepped(joined(low, high, layer), dual, None, before, layer), tally, layer)
 
 
-def last_layer(low, high, dual, above, before, tally, updated_in, updated, layer, sem):
-    layer[...] = counted(stepped(joined(low, high, 0), dual, above, before, 0), tally, 0)
+def last_layer(part, above, tally, updated_in, updated, layer, sem):
+    layer[...] = counted(part[...] - 0.25 * above[...], tally, 0)
     move = pltpu.make_async_copy(layer, updated.at[0], sem)
     move.start()
     move.wait()
@@ -364,12 +365,12 @@
     (tally,) = call(second_votes, [(BINS + 1,) + block], 3, [VMEM] * 4 + [ANY])(
         caps, batches, low_tally, high_tally, side
     )
-    (rest,) = call(last_layers, [block], 1, [VMEM] * 5)(low, high, dual, before, tally)
+    rest, part = call(last_layers, [block, layer], 1, [VMEM] * 5)(low, high, dual, before, tally)
     above, rest = lax.optimization_barrier((above, rest))
     (current,) = call(
-        last_layer, [block], 1, [VMEM] * 6 + [ANY], out_specs=(ANY,), input_output_aliases={6: 0},
+        last_layer, [block], 1, [VMEM] * 3 + [ANY], out_specs=(ANY,), input_output_aliases={3: 0},
         scratch_shapes=[pltpu.VMEM((ROWS, LANES), jnp.float32), pltpu.SemaphoreType.DMA],
-    )(low, high, dual, above, before, tally, rest)
+    )(part, above, tally, rest)
     return (current, dual)
 
 

time: 96 us -> 95.9 us (level)
  transfers between devices with their start and end apart: 11 -> 11, of which waited for: 4 -> 4; matrix products, arithmetic and copies ran while one was open for 0% -> 0% of each run, Pallas kernels for 12% -> 13%
where the time goes in v13:
time: 95.9 us; the launch traced here: 95.4 us
  starting transfers between devices  74.1 us (77%)
  Pallas kernels  12.8 us (13%)
  waiting for transfers between devices  7.6 us (8%)
    ppermute x8, starting transfers between devices, passed_along(): lax.ppermute(value, axis, [(source, source + steps) for source in range(f...  55 us
    all_to_all x2, starting transfers between devices, exchange(): return lax.all_to_all(pieces, 'slab', 0, 0, axis_index_groups=GROUPS)  13.3 us
    ppermute x8, waiting for transfers between devices, passed_along(): lax.ppermute(value, axis, [(source, source + steps) for source in range(f...  7.59 us
    ppermute x1, starting transfers between devices, per_device(): lax.ppermute(kept, 'slab', [(index, index ^ 1) for index in range(32)])  5.82 us
    pallas_call x1, Pallas kernels, per_device(): call(second_votes, [(BINS + 1,) + block], 3, [VMEM] * 4 + [ANY])  2.2 us
  transfers between devices with their start and end apart: 11, of which 4 were waited for; matrix products, arithmetic and copies ran while one was open for 0% of the time, Pallas kernels for 13%

profile of v13, /device:TPU:38, one launch (start us, length us, event | category | flops | bytes accessed | tf_op | source)
XLA Modules:
  0.0 95.4 jit_solution(10633599003110850207)
XLA Ops:
  0.6 7.4 %all-to-all-start = ((f32[16,8,8,128]{3,2,1,0:T(8,128)}), f32[16,8,8,128]{3,2,1,0:T(8,128)S(1)}, u32[]{:S(2)}, u32[]{:S(2)}) async-start(f32[16,8,8,128]{3,2,1,0:T(8,128)} %bitcast.6), calls=%async_computation | async-start | bytes 1048576 | tf_op jit(solution)/shard_map/all_to_all | solution.py:316
  8.1 1.2 %staged.1 = (f32[16,1024]{1,0:T(8,128)S(1)}, f32[8,1024]{1,0:T(8,128)S(1)}, f32[8,16,1024]{2,1,0:T(8,128)S(1)}, f32[8,8,128]{2,1,0:T(8,128)S(1)}, f32[8,128]{1,0:T(8,128)S(1)}) custom-call(s32[2]{0:T(128)} %owner.1, s32[2,1,4]{2,1,0:T(1,128)} %bitcast.7, f32[8,16,1024]{2,1,0:T(8,128)} %field.1), custom_call_target="tpu_custom_call" | custom-call | flops 1000000000 | bytes 3000000 | tf_op jit(solution)/shard_map/staged/pallas_call | solution.py:327
  9.3 17.2 %collective-permute-start.1 = (f32[16,1024]{1,0:T(8,128)S(1)}, f32[16,1024]{1,0:T(8,128)S(1)}, u32[]{:S(2)}, u32[]{:S(2)}) collective-permute-start(f32[16,1024]{1,0:T(8,128)S(1)} %get-tuple-element.28), channel_id=1, source_target_pairs={{16,0},{32,16},{48,32},{64,48},{80,64},{96,80},{112,96},{128,112},... | collective-permute-start | bytes 196616 | tf_op jit(solution)/shard_map/ppermute | solution.py:309
  26.5 0.0 all-to-all-done.spread
  26.5 0.7 pick.1.kept
  27.2 5.8 %collective-permute-start.4 = (f32[8,8,128]{2,1,0:T(8,128)S(1)}, f32[8,8,128]{2,1,0:T(8,128)S(1)}, u32[]{:S(2)}, u32[]{:S(2)}) collective-permute-start(f32[8,8,128]{2,1,0:T(8,128)S(1)} %pick.1.kept), channel_id=1, source_target_pairs={{0,16},{16,0},{32,48},{48,32},{64,80},{80,64},{96,112},{112,96},{1... | collective-permute-start | bytes 98312 | tf_op jit(solution)/shard_map/ppermute | solution.py:337
  33.0 0.0 copy-start.1
  33.1 2.1 %collective-permute-start = (f32[8,1024]{1,0:T(8,128)S(1)}, f32[8,1024]{1,0:T(8,128)S(1)}, u32[]{:S(2)}, u32[]{:S(2)}) collective-permute-start(f32[8,1024]{1,0:T(8,128)S(1)} %get-tuple-element.27), channel_id=1, source_target_pairs={{1,0},{2,1},{3,2},{4,3},{5,4},{6,5},{7,6},{8,7},{9,8},{10,9},{11,1... | collective-permute-start | bytes 98312 | tf_op jit(solution)/shard_map/ppermute | solution.py:309
  35.1 0.0 collective-permute-done.1.given
  35.1 1.6 %collective-permute-done.ahead = f32[8,1024]{1,0:T(8,128)S(1)} collective-permute-done((f32[8,1024]{1,0:T(8,128)S(1)}, f32[8,1024]{1,0:T(8,128)S(1)}, u32[]{:S(2)}, u32[]{:S(2)}) %collective-permute-start) | collective-permute-done | bytes 32800 | tf_op jit(solution)/shard_map/ppermute | solution.py:309
  36.7 0.0 copy-done.1
  36.7 0.6 all_duals.1
  37.3 3.7 %collective-permute-start.3 = (f32[8,1024]{1,0:T(8,128)S(1)}, f32[8,1024]{1,0:T(8,128)S(1)}, u32[]{:S(2)}, u32[]{:S(2)}) collective-permute-start(f32[8,1024]{1,0:T(8,128)S(1)} %get-tuple-element.32), channel_id=1, source_target_pairs={{0,1},{1,2},{2,3},{3,4},{4,5},{5,6},{6,7},{7,8},{8,9},{9,10},{10,1... | collective-permute-start | bytes 98312 | tf_op jit(solution)/shard_map/ppermute | solution.py:309
  41.0 8.4 %collective-permute-start.2 = (f32[16,1024]{1,0:T(8,128)S(1)}, f32[16,1024]{1,0:T(8,128)S(1)}, u32[]{:S(2)}, u32[]{:S(2)}) collective-permute-start(f32[16,1024]{1,0:T(8,128)S(1)} %get-tuple-element.31), channel_id=1, source_target_pairs={{0,16},{16,32},{32,48},{48,64},{64,80},{80,96},{96,112},{112,128},... | collective-permute-start | bytes 196616 | tf_op jit(solution)/shard_map/ppermute | solution.py:309
  49.4 0.0 collective-permute-done.4.across
  49.4 0.8 copies_of.1
  50.2 5.8 %all-to-all-start.1 = ((f32[16,8,8,128]{3,2,1,0:T(8,128)}), f32[16,8,8,128]{3,2,1,0:T(8,128)S(1)}, u32[]{:S(2)}, u32[]{:S(2)}) async-start(f32[16,8,8,128]{3,2,1,0:T(8,128)} %copies_of.1), calls=%async_computation.1 | async-start | bytes 1048576 | tf_op jit(solution)/shard_map/all_to_all | solution.py:316
  56.1 0.0 collective-permute-done.3.before
  56.1 0.1 first_values.1
  56.2 10.3 %collective-permute-start.6 = (f32[16,1024]{1,0:T(8,128)S(1)}, f32[16,1024]{1,0:T(8,128)S(1)}, u32[]{:S(2)}, u32[]{:S(2)}) collective-permute-start(f32[16,1024]{1,0:T(8,128)S(1)} %first_values.1), channel_id=1, source_target_pairs={{16,0},{32,16},{48,32},{64,48},{80,64},{96,80},{112,96},{128,112},... | collective-permute-start | bytes 196616 | tf_op jit(solution)/shard_map/ppermute | solution.py:309
  66.4 0.0 collective-permute-done.2.above
  66.5 0.3 all_values.1.values
  66.7 0.0 all-to-all-done.1.batches
  66.7 1.1 %low_votes.1.tally.low = f32[9,9,8,1024]{3,2,1,0:T(8,128)S(1)} custom-call(f32[8,8,128]{2,1,0:T(8,128)S(1)} %get-tuple-element.33.caps.caps_of, f32[16,8,8,128]{3,2,1,0:T(8,128)S(1)} %all-to-all-done.1.batches), custom_call_target="tpu_custom_call" | custom-call | flops 12000000000 | bytes 36000000 | tf_op jit(solution)/shard_map/low_votes/pallas_call | solution.py:352
  67.9 0.3 low_update.1
  68.2 1.9 %collective-permute-start.5 = (f32[8,1024]{1,0:T(8,128)S(1)}, f32[8,1024]{1,0:T(8,128)S(1)}, u32[]{:S(2)}, u32[]{:S(2)}) collective-permute-start(f32[8,1024]{1,0:T(8,128)S(1)} %get-tuple-element.37.after), channel_id=1, source_target_pairs={{1,0},{2,1},{3,2},{4,3},{5,4},{6,5},{7,6},{8,7},{9,8},{10,9},{11,1... | collective-permute-start | bytes 98312 | tf_op jit(solution)/shard_map/ppermute | solution.py:309
  70.1 1.1 %high_votes.1.tally.high = f32[9,9,8,1024]{3,2,1,0:T(8,128)S(1)} custom-call(f32[8,8,128]{2,1,0:T(8,128)S(1)} %get-tuple-element.33.caps.caps_of, f32[16,8,8,128]{3,2,1,0:T(8,128)S(1)} %all-to-all-done.1.batches, f32[8,1024]{1,0:T(8,128)S(1)} %get-tuple-element.37.after), custom_call_target="tpu_custom_call" | custom-call | flops 12000000000 | bytes 36000000 | tf_op jit(solution)/shard_map/high_votes/pallas_call | solution.py:355
  71.2 0.3 high_update.1
  71.5 2.1 %collective-permute-done.6.values = f32[16,1024]{1,0:T(8,128)S(1)} collective-permute-done((f32[16,1024]{1,0:T(8,128)S(1)}, f32[16,1024]{1,0:T(8,128)S(1)}, u32[]{:S(2)}, u32[]{:S(2)}) %collective-permute-start.6) | collective-permute-done | bytes 65568 | tf_op jit(solution)/shard_map/ppermute | solution.py:309
  73.6 0.1 past_update.1.past
  73.6 0.0 collective-permute-done.5.ahead
  73.7 0.1 top_dual.1.after
  73.8 9.5 %collective-permute-start.8 = (f32[16,1024]{1,0:T(8,128)S(1)}, f32[16,1024]{1,0:T(8,128)S(1)}, u32[]{:S(2)}, u32[]{:S(2)}) collective-permute-start(f32[16,1024]{1,0:T(8,128)S(1)} %top_dual.1.after), channel_id=1, source_target_pairs={{0,16},{16,32},{32,48},{48,64},{64,80},{80,96},{96,112},{112,128},... | collective-permute-start | bytes 196616 | tf_op jit(solution)/shard_map/ppermute | solution.py:309
  83.2 1.7 %second_duals.1 = (f32[3,8,16,1024]{3,2,1,0:T(8,128)}, f32[8,1024]{1,0:T(8,128)S(1)}) custom-call(f32[8,8,1024]{2,1,0:T(8,128)S(1)} %get-tuple-element.39.low, f32[8,8,1024]{2,1,0:T(8,128)S(1)} %get-tuple-element.40.high, f32[3,8,16,1024]{3,2,1,0:T(8,128)S(1)} %get-tuple-element.30.dual, f32[8,1024]{1,0:T(8,128)S(1)} %collective-permute-done.5.ahead, ...), custom_call_target="tpu_custom_call" | custom-call | flops 1000000000 | bytes 3000000 | tf_op jit(solution)/shard_map/second_duals/pallas_call | solution.py:361
  85.0 0.0 copy-start
  85.0 2.0 %collective-permute-start.7 = (f32[8,1024]{1,0:T(8,128)S(1)}, f32[8,1024]{1,0:T(8,128)S(1)}, u32[]{:S(2)}, u32[]{:S(2)}) collective-permute-start(f32[8,1024]{1,0:T(8,128)S(1)} %get-tuple-element.43.after), channel_id=1, source_target_pairs={{0,1},{1,2},{2,3},{3,4},{4,5},{5,6},{6,7},{7,8},{8,9},{9,10},{10,1... | collective-permute-start | bytes 98312 | tf_op jit(solution)/shard_map/ppermute | solution.py:309
  87.0 2.2 %second_votes.1.tally = f32[9,8,16,1024]{3,2,1,0:T(8,128)S(1)} custom-call(f32[8,8,128]{2,1,0:T(8,128)S(1)} %get-tuple-element.33.caps.caps_of, f32[16,8,8,128]{3,2,1,0:T(8,128)S(1)} %all-to-all-done.1.batches, f32[9,9,8,1024]{3,2,1,0:T(8,128)S(1)} %low_votes.1.tally.low, f32[9,9,8,1024]{3,2,1,0:T(8,128)S(1)} %high_votes.1.tally.high, ...), custom_call_target="tpu_custom_call" | custom-call | flops 3000000000 | bytes 9000000 | tf_op jit(solution)/shard_map/second_votes/pallas_call | solution.py:365
  89.2 1.1 %collective-permute-done.7.before = f32[8,1024]{1,0:T(8,128)S(1)} collective-permute-done((f32[8,1024]{1,0:T(8,128)S(1)}, f32[8,1024]{1,0:T(8,128)S(1)}, u32[]{:S(2)}, u32[]{:S(2)}) %collective-permute-start.7) | collective-permute-done | bytes 32800 | tf_op jit(solution)/shard_map/ppermute | solution.py:309
  90.3 0.0 copy-done
  90.3 1.5 %last_layers.1 = (f32[8,16,1024]{2,1,0:T(8,128)}, f32[16,1024]{1,0:T(8,128)S(1)}) custom-call(f32[8,8,1024]{2,1,0:T(8,128)S(1)} %get-tuple-element.36.low, f32[8,8,1024]{2,1,0:T(8,128)S(1)} %get-tuple-element.38.high, f32[3,8,16,1024]{3,2,1,0:T(8,128)S(1)} %copy-done, f32[8,1024]{1,0:T(8,128)S(1)} %collective-permute-done.7.before, ...), custom_call_target="tpu_custom_call" | custom-call | flops 1000000000 | bytes 3000000 | tf_op jit(solution)/shard_map/last_layers/pallas_call | solution.py:368
  91.8 2.9 %collective-permute-done.8.above = f32[16,1024]{1,0:T(8,128)S(1)} collective-permute-done((f32[16,1024]{1,0:T(8,128)S(1)}, f32[16,1024]{1,0:T(8,128)S(1)}, u32[]{:S(2)}, u32[]{:S(2)}) %collective-permute-start.8) | collective-permute-done | bytes 65568 | tf_op jit(solution)/shard_map/ppermute | solution.py:309
  94.7 0.7 last_layer.1
  (1 shorter events, 0.0 us)
Async XLA Ops:
  0.6 25.9 %all-to-all-start = ((f32[16,8,8,128]{3,2,1,0:T(8,128)}), f32[16,8,8,128]{3,2,1,0:T(8,128)S(1)}, u32[]{:S(2)}, u32[]{:S(2)}) async-start(f32[16,8,8,128]{3,2,1,0:T(8,128)} %bitcast.6), calls=%async_computation | async-start | bytes 1048576 | tf_op jit(solution)/shard_map/all_to_all | solution.py:316
  9.3 25.8 %collective-permute-start.1 = (f32[16,1024]{1,0:T(8,128)S(1)}, f32[16,1024]{1,0:T(8,128)S(1)}, u32[]{:S(2)}, u32[]{:S(2)}) collective-permute-start(f32[16,1024]{1,0:T(8,128)S(1)} %get-tuple-element.28), channel_id=1, source_target_pairs={{16,0},{32,16},{48,32},{64,48},{80,64},{96,80},{112,96},{128,112},... | collective-permute-start | bytes 196616 | tf_op jit(solution)/shard_map/ppermute | solution.py:309
  27.2 22.2 %collective-permute-start.4 = (f32[8,8,128]{2,1,0:T(8,128)S(1)}, f32[8,8,128]{2,1,0:T(8,128)S(1)}, u32[]{:S(2)}, u32[]{:S(2)}) collective-permute-start(f32[8,8,128]{2,1,0:T(8,128)S(1)} %pick.1.kept), channel_id=1, source_target_pairs={{0,16},{16,0},{32,48},{48,32},{64,80},{80,64},{96,112},{112,96},{1... | collective-permute-start | bytes 98312 | tf_op jit(solution)/shard_map/ppermute | solution.py:337
  33.0 3.7 %copy-start.1 = (f32[3,8,16,1024]{3,2,1,0:T(8,128)S(1)}, f32[3,8,16,1024]{3,2,1,0:T(8,128)}, u32[]{:S(2)}) copy-start(f32[3,8,16,1024]{3,2,1,0:T(8,128)} %dual.1) | copy-start | bytes 4718596
  33.1 3.6 %collective-permute-start = (f32[8,1024]{1,0:T(8,128)S(1)}, f32[8,1024]{1,0:T(8,128)S(1)}, u32[]{:S(2)}, u32[]{:S(2)}) collective-permute-start(f32[8,1024]{1,0:T(8,128)S(1)} %get-tuple-element.27), channel_id=1, source_target_pairs={{1,0},{2,1},{3,2},{4,3},{5,4},{6,5},{7,6},{8,7},{9,8},{10,9},{11,1... | collective-permute-start | bytes 98312 | tf_op jit(solution)/shard_map/ppermute | solution.py:309
  37.3 18.8 %collective-permute-start.3 = (f32[8,1024]{1,0:T(8,128)S(1)}, f32[8,1024]{1,0:T(8,128)S(1)}, u32[]{:S(2)}, u32[]{:S(2)}) collective-permute-start(f32[8,1024]{1,0:T(8,128)S(1)} %get-tuple-element.32), channel_id=1, source_target_pairs={{0,1},{1,2},{2,3},{3,4},{4,5},{5,6},{6,7},{7,8},{8,9},{9,10},{10,1... | collective-permute-start | bytes 98312 | tf_op jit(solution)/shard_map/ppermute | solution.py:309
  41.0 25.5 %collective-permute-start.2 = (f32[16,1024]{1,0:T(8,128)S(1)}, f32[16,1024]{1,0:T(8,128)S(1)}, u32[]{:S(2)}, u32[]{:S(2)}) collective-permute-start(f32[16,1024]{1,0:T(8,128)S(1)} %get-tuple-element.31), channel_id=1, source_target_pairs={{0,16},{16,32},{32,48},{48,64},{64,80},{80,96},{96,112},{112,128},... | collective-permute-start | bytes 196616 | tf_op jit(solution)/shard_map/ppermute | solution.py:309
  50.2 16.5 %all-to-all-start.1 = ((f32[16,8,8,128]{3,2,1,0:T(8,128)}), f32[16,8,8,128]{3,2,1,0:T(8,128)S(1)}, u32[]{:S(2)}, u32[]{:S(2)}) async-start(f32[16,8,8,128]{3,2,1,0:T(8,128)} %copies_of.1), calls=%async_computation.1 | async-start | bytes 1048576 | tf_op jit(solution)/shard_map/all_to_all | solution.py:316
  56.2 17.4 %collective-permute-start.6 = (f32[16,1024]{1,0:T(8,128)S(1)}, f32[16,1024]{1,0:T(8,128)S(1)}, u32[]{:S(2)}, u32[]{:S(2)}) collective-permute-start(f32[16,1024]{1,0:T(8,128)S(1)} %first_values.1), channel_id=1, source_target_pairs={{16,0},{32,16},{48,32},{64,48},{80,64},{96,80},{112,96},{128,112},... | collective-permute-start | bytes 196616 | tf_op jit(solution)/shard_map/ppermute | solution.py:309
  68.2 5.5 %collective-permute-start.5 = (f32[8,1024]{1,0:T(8,128)S(1)}, f32[8,1024]{1,0:T(8,128)S(1)}, u32[]{:S(2)}, u32[]{:S(2)}) collective-permute-start(f32[8,1024]{1,0:T(8,128)S(1)} %get-tuple-element.37.after), channel_id=1, source_target_pairs={{1,0},{2,1},{3,2},{4,3},{5,4},{6,5},{7,6},{8,7},{9,8},{10,9},{11,1... | collective-permute-start | bytes 98312 | tf_op jit(solution)/shard_map/ppermute | solution.py:309
  73.8 20.9 %collective-permute-start.8 = (f32[16,1024]{1,0:T(8,128)S(1)}, f32[16,1024]{1,0:T(8,128)S(1)}, u32[]{:S(2)}, u32[]{:S(2)}) collective-permute-start(f32[16,1024]{1,0:T(8,128)S(1)} %top_dual.1.after), channel_id=1, source_target_pairs={{0,16},{16,32},{32,48},{48,64},{64,80},{80,96},{96,112},{112,128},... | collective-permute-start | bytes 196616 | tf_op jit(solution)/shard_map/ppermute | solution.py:309
  85.0 5.4 %copy-start = (f32[3,8,16,1024]{3,2,1,0:T(8,128)S(1)}, f32[3,8,16,1024]{3,2,1,0:T(8,128)}, u32[]{:S(2)}) copy-start(f32[3,8,16,1024]{3,2,1,0:T(8,128)} %get-tuple-element.24.dual) | copy-start | bytes 4718596
  85.0 5.4 %collective-permute-start.7 = (f32[8,1024]{1,0:T(8,128)S(1)}, f32[8,1024]{1,0:T(8,128)S(1)}, u32[]{:S(2)}, u32[]{:S(2)}) collective-permute-start(f32[8,1024]{1,0:T(8,128)S(1)} %get-tuple-element.43.after), channel_id=1, source_target_pairs={{0,1},{1,2},{2,3},{3,4},{4,5},{5,6},{6,7},{7,8},{8,9},{9,10},{10,1... | collective-permute-start | bytes 98312 | tf_op jit(solution)/shard_map/ppermute | solution.py:309
